TPU v7x, 32 devices: a whole 2x2x4 slice. The times are simulated.
32 devices in a mesh: dp: 16 (over z, y, x), seq: 2 (over core).
Axes of the slice: x: 2, y: 2, z: 4, core: 2. Of those that a mesh axis runs over, the one named last changes fastest.
Arguments:
- hidden_in: bfloat16 [16384, 768], P(('dp', 'seq')), may hold values from -6 to 6
- prefix: int32 [16], P('dp'), may hold values from 102 to 512
- w_qkv: bfloat16 [768, 2304], P(('dp', 'seq')), may hold values from -0.21875 to 0.21875
- q_bias: bfloat16 [768], P(('dp', 'seq')), may hold values from -3 to 3
- v_bias: bfloat16 [768], P(('dp', 'seq')), may hold values from -3 to 3
- rel_table: bfloat16 [512, 768], P(('dp', 'seq')), may hold values from -6 to 6
- w_posk: bfloat16 [768, 768], P(('dp', 'seq')), may hold values from -0.21875 to 0.21875
- w_posq: bfloat16 [768, 768], P(('dp', 'seq')), may hold values from -0.21875 to 0.21875
- posq_bias: bfloat16 [768], P(('dp', 'seq')), may hold values from -3 to 3
- w_out: bfloat16 [768, 768], P(('dp', 'seq')), may hold values from -0.875 to 0.875
- out_bias: bfloat16 [768], P(('dp', 'seq')), may hold values from -3 to 3
- norm1_gain: bfloat16 [768], P(('dp', 'seq')), may hold values from 0.5 to 1.5
- norm1_bias: bfloat16 [768], P(('dp', 'seq')), may hold values from -3 to 3
- w_up: bfloat16 [768, 3072], P(('dp', 'seq')), may hold values from -0.21875 to 0.21875
- up_bias: bfloat16 [3072], P(('dp', 'seq')), may hold values from -3 to 3
- w_down: bfloat16 [3072, 768], P(('dp', 'seq')), may hold values from -0.109375 to 0.109375
- down_bias: bfloat16 [768], P(('dp', 'seq')), may hold values from -3 to 3
- norm2_gain: bfloat16 [768], P(('dp', 'seq')), may hold values from 0.5 to 1.5
- norm2_bias: bfloat16 [768], P(('dp', 'seq')), may hold values from -3 to 3
- out_grad: bfloat16 [16384, 768], P(('dp', 'seq')), may hold values from -6 to 6
Outputs:
- hidden_out: bfloat16 [16384, 768], P(('dp', 'seq'))
- in_grad: float32 [16384, 768], P(('dp', 'seq'))
- w_qkv_grad: float32 [768, 2304], P(('dp', 'seq'))
- q_bias_grad: float32 [768], P(('dp', 'seq'))
- v_bias_grad: float32 [768], P(('dp', 'seq'))
- rel_table_grad: float32 [512, 768], P(('dp', 'seq'))
- w_posk_grad: float32 [768, 768], P(('dp', 'seq'))
- w_posq_grad: float32 [768, 768], P(('dp', 'seq'))
- posq_bias_grad: float32 [768], P(('dp', 'seq'))
- w_out_grad: float32 [768, 768], P(('dp', 'seq'))
- out_bias_grad: float32 [768], P(('dp', 'seq'))
- norm1_gain_grad: float32 [768], P(('dp', 'seq'))
- norm1_bias_grad: float32 [768], P(('dp', 'seq'))
- w_up_grad: float32 [768, 3072], P(('dp', 'seq'))
- up_bias_grad: float32 [3072], P(('dp', 'seq'))
- w_down_grad: float32 [3072, 768], P(('dp', 'seq'))
- down_bias_grad: float32 [768], P(('dp', 'seq'))
- norm2_gain_grad: float32 [768], P(('dp', 'seq'))
- norm2_bias_grad: float32 [768], P(('dp', 'seq'))
All inputs are finite; a program needn't handle non-finite values.
Results may differ from a plain program's by a relative error of at most 0.023.
Values may be sent and summed in bfloat16 or wider, within the bound.
No kernel may reach another device: no remote copies, remote signals or barrier semaphores. Data moves between devices by JAX's collectives and lax.ppermute only.
A program may use at most 192 MiB of HBM per device.

v0:
```python
import functools
import math

import jax
import jax.numpy as jnp
from jax import lax
from jax.experimental import pallas as pl
from jax.experimental.pallas import tpu as pltpu
from jax.sharding import PartitionSpec as P

D = 768
HEADS = 12
HEAD_DIM = 64
SPAN = 256
TILE = 128
BLOCK = 256
BAND = 768
PAIR = 2 * HEAD_DIM


eps_norm = 1e-07


def normalize(value, gain, shift):
    average = jnp.mean(value, axis=-1, keepdims=True)
    centred = value - average
    variance = jnp.mean(centred * centred, axis=-1, keepdims=True)
    return centred * lax.rsqrt(variance + eps_norm) * gain + shift


def gelu_exact(value):
    return jax.nn.gelu(value, approximate=False)


def product(left, right):
    return jnp.dot(left, right, preferred_element_type=jnp.float32)


def inner_first(left, right):
    return lax.dot_general(
        left, right, (((0,), (0,)), ((), ())), preferred_element_type=jnp.float32
    )


def inner_last(left, right):
    return lax.dot_general(
        left, right, (((1,), (1,)), ((), ())), preferred_element_type=jnp.float32
    )


def split_heads(matrix):
    return matrix.reshape(matrix.shape[0], HEADS, HEAD_DIM).transpose(1, 0, 2)


def join_heads(stacked):
    return stacked.transpose(1, 0, 2).reshape(stacked.shape[1], D)


def column_sums(matrix):
    return jnp.sum(matrix.astype(jnp.float32), axis=0)


def nn(left, right):
    return lax.dot_general(
        left, right, (((1,), (0,)), ((), ())), preferred_element_type=jnp.float32
    )


def nt(left, right):
    return lax.dot_general(
        left, right, (((1,), (1,)), ((), ())), preferred_element_type=jnp.float32
    )


def unit_matrix(size, reverse=False):
    rows = lax.broadcasted_iota(jnp.int32, (size, size), 0)
    cols = lax.broadcasted_iota(jnp.int32, (size, size), 1)
    if reverse:
        cols = size - 1 - cols
    return jnp.where(rows == cols, 1.0, 0.0).astype(jnp.bfloat16)


def turn_matrix():
    rows = lax.broadcasted_iota(jnp.int32, (BLOCK, BLOCK), 0)
    cols = lax.broadcasted_iota(jnp.int32, (BLOCK, BLOCK), 1)
    mirrored = rows // TILE * (2 * TILE) + TILE - 1 - rows
    return jnp.where(mirrored == cols, 1.0, 0.0).astype(jnp.bfloat16)


def head_lanes(head):
    lanes = lax.broadcasted_iota(jnp.int32, (1, PAIR), 1)
    return lanes // HEAD_DIM == head


def head_rows(head):
    rows = lax.broadcasted_iota(jnp.int32, (HEAD_DIM, PAIR), 0)
    cols = lax.broadcasted_iota(jnp.int32, (HEAD_DIM, PAIR), 1)
    return jnp.where(cols == rows + head * HEAD_DIM, 1.0, 0.0).astype(jnp.bfloat16)


def key_tiles(block, length):
    return max(length // 2, (block + 1) * BLOCK) // TILE


def tile_seen(query_tile, key_tile, length):
    return key_tile < key_tiles(query_tile * TILE // BLOCK, length)


def skewed(window):
    return pltpu.roll(window, 0, 1, stride=1, stride_axis=0)


def forward_body(head, prefix_ref, q_ref, k_ref, v_ref, pk_ref, pq_ref, *refs):
    ctx_ref, p_ref, wb_ref, far_ref, s_ref = refs[-5:]
    length = q_ref.shape[0]
    mine = head_lanes(head)
    prefix = prefix_ref[0]
    eye = unit_matrix(TILE)
    eye_block = unit_matrix(BLOCK)
    zero = jnp.zeros((), jnp.bfloat16)
    scale = math.log2(math.e) / math.sqrt(3 * HEAD_DIM)
    for tile in range(length // TILE):
        rows = slice(tile * TILE, (tile + 1) * TILE)
        table = nt(jnp.where(mine, k_ref[rows, :], zero), pq_ref[...])
        wb_ref[rows, :] = skewed(table)
        wb_ref[rows, 0:TILE] = table[:, BAND - TILE :]
        far_ref[rows, :] = table[:, 0:TILE]
    v_cols = nt(jnp.where(lax.broadcasted_iota(jnp.int32, (PAIR, PAIR), 0) // HEAD_DIM == head, unit_matrix(PAIR), zero), v_ref[...]).astype(jnp.bfloat16)
    for block in range(length // BLOCK):
        cols = slice(block * BLOCK, (block + 1) * BLOCK)
        q_own = jnp.where(mine, q_ref[cols, :], zero)
        skews, highs, lows = [], [], []
        for sub in range(2):
            table = nt(q_own[sub * TILE : (sub + 1) * TILE], pk_ref[...])
            skews.append(skewed(table).astype(jnp.bfloat16))
            highs.append(table[:, 0:TILE].astype(jnp.bfloat16))
            lows.append(table[:, BAND - TILE :].astype(jnp.bfloat16))
        count = key_tiles(block, length)
        highest = None
        for tile in range(count):
            rows = slice(tile * TILE, (tile + 1) * TILE)
            parts_a, parts_b = [], []
            for sub in range(2):
                step = 2 * block + sub - tile
                if step >= 3:
                    parts_a.append(highs[sub])
                    parts_b.append(wb_ref[rows, 0:TILE])
                elif step <= -3:
                    parts_a.append(lows[sub])
                    parts_b.append(far_ref[rows, :])
                else:
                    at = 384 - TILE * step
                    parts_a.append(skews[sub][:, at : at + TILE])
                    at = 384 + TILE * step
                    parts_b.append(wb_ref[rows, at : at + TILE])
            right = jnp.concatenate([jnp.concatenate(parts_a, axis=0), q_own], axis=1)
            left = jnp.concatenate([eye, k_ref[rows, :]], axis=1)
            raw = nt(left, right) + jnp.concatenate(parts_b, axis=1)
            if (tile + 1) * TILE > block * BLOCK + 1:
                keys = tile * TILE + lax.broadcasted_iota(jnp.int32, (TILE, BLOCK), 0)
                queries = block * BLOCK + lax.broadcasted_iota(jnp.int32, (TILE, BLOCK), 1)
                raw = jnp.where((keys < prefix) | (keys <= queries), raw, -jnp.inf)
            s_ref[rows, :] = raw
            top = jnp.max(raw, axis=0, keepdims=True)
            highest = top if highest is None else jnp.maximum(highest, top)
        total = jnp.zeros((1, BLOCK), jnp.float32)
        for tile in range(count):
            rows = slice(tile * TILE, (tile + 1) * TILE)
            expo = jnp.exp2((s_ref[rows, :] - highest) * scale)
            s_ref[rows, :] = expo
            total = total + jnp.sum(expo, axis=0, keepdims=True)
        inverse = 1.0 / total
        for tile in range(count):
            rows = slice(tile * TILE, (tile + 1) * TILE)
            p_ref[rows, cols] = (s_ref[rows, :] * inverse).astype(jnp.bfloat16)
        seen = count * TILE
        ctx_cols = nn(v_cols[:, :seen], p_ref[0:seen, cols]).astype(jnp.bfloat16)
        ctx = nt(eye_block, ctx_cols).astype(jnp.bfloat16)

        ctx_ref[cols, :] = ctx if head == 0 else refs[0][cols, :] + ctx


def attention_forward(prefix, merged, pos_band, pair, head, found=()):
    length, width = merged.shape[0], merged.shape[1] // 3
    pairs = width // PAIR
    tall = [pl.BlockSpec((length, PAIR), lambda p, at=at: (0, at)) for at in (pair, pairs + pair, 2 * pairs + pair)]
    band = [pl.BlockSpec((BAND, PAIR), lambda p, at=at: (0, at)) for at in (pair, pairs + pair)]
    own = pl.BlockSpec((length, PAIR), lambda p: (0, 0))
    return pl.pallas_call(
        functools.partial(forward_body, head),
        grid=(1,),
        in_specs=[pl.BlockSpec(memory_space=pltpu.SMEM)] + tall + band + [own] * len(found),
        out_specs=[own, pl.BlockSpec((length, length), lambda p: (0, 0))],
        out_shape=[
            jax.ShapeDtypeStruct((length, PAIR), jnp.bfloat16),
            jax.ShapeDtypeStruct((length, length), jnp.bfloat16),
        ],
        scratch_shapes=[
            pltpu.VMEM((length, BAND), jnp.float32),
            pltpu.VMEM((length, TILE), jnp.float32),
            pltpu.VMEM((length, BLOCK), jnp.float32),
        ],
        compiler_params=pltpu.CompilerParams(dimension_semantics=("arbitrary",), vmem_limit_bytes=24 << 20),
        cost_estimate=pl.CostEstimate(flops=10**9, transcendentals=length * length, bytes_accessed=3 << 20),
        name="attention_forward",
    )(prefix, merged, merged, merged, pos_band, pos_band, *found)


def backward_body(head, q_ref, k_ref, v_ref, dctx_ref, p_ref, pk_ref, pq_ref, *refs):
    dq_ref, dk_ref, dv_ref, dpk_ref, dpq_ref, dr_ref, dk_acc, dv_acc = refs[-8:]
    outs = (dq_ref, dk_ref, dv_ref)
    length = q_ref.shape[0]
    mine = head_lanes(head)
    flip = turn_matrix()
    pick = head_rows(head)
    bf = jnp.bfloat16
    zero = jnp.zeros((), bf)
    scale = 1.0 / math.sqrt(3 * HEAD_DIM)
    back = BAND - (TILE - 1)
    blank = jnp.zeros((TILE, TILE), bf)
    dk_acc[...] = jnp.zeros_like(dk_acc)
    dv_acc[...] = jnp.zeros_like(dv_acc)
    dpk = jnp.zeros((HEAD_DIM, BAND), jnp.float32)
    dpq = jnp.zeros((HEAD_DIM, BAND), jnp.float32)
    tiles = length // TILE

    def put(index, rows, value):
        earlier = jnp.zeros((), bf) if head == 0 else refs[index][rows, :]
        outs[index][rows, :] = jnp.where(mine, value.astype(bf), earlier)

    def unskew(parts):
        return pltpu.roll(jnp.concatenate(parts, axis=1), back, 1, stride=1, stride_axis=0)

    for block in range(length // BLOCK):
        cols = slice(block * BLOCK, (block + 1) * BLOCK)
        count = key_tiles(block, length)
        seen = count * TILE
        dctx = dctx_ref[cols, :]
        v_own = jnp.where(mine, v_ref[0:seen, :], zero)
        probs_low = p_ref[0:seen, cols]
        probs = probs_low.astype(jnp.float32)
        d_probs = nt(v_own, dctx)
        row_dot = jnp.sum(probs * d_probs, axis=0, keepdims=True)
        dr_ref[0:seen, cols] = (probs * ((d_probs - row_dot) * scale)).astype(bf)
        d_raw = dr_ref[0:seen, cols]
        dv_acc[0:seen, :] += nn(probs_low, dctx)
        dk_acc[0:seen, :] += nn(d_raw, q_ref[cols, :])
        turned = nt(flip, d_raw).astype(bf)
        spreads = []
        for sub in range(2):
            tile = 2 * block + sub
            own = turned[sub * TILE : (sub + 1) * TILE]

            def piece(key_tile):
                return own[:, key_tile * TILE : (key_tile + 1) * TILE]

            near = [t for t in range(count) if tile - t >= 3]
            far = [t for t in range(count) if tile - t <= -3]
            band = [blank]
            for step in (2, 1, 0, -1, -2):
                key_tile = tile - step
                band.append(piece(key_tile) if 0 <= key_tile < count else blank)
            spreads.append(
                add_edges(unskew(band), [piece(t).astype(jnp.float32) for t in near], [piece(t).astype(jnp.float32) for t in far])
            )
        spread = jnp.concatenate(spreads, axis=0)
        dq = nn(turned, k_ref[0:seen, :]) + nn(spread, pk_ref[...])
        put(0, cols, nn(flip, dq.astype(bf)))
        q_cols = nt(pick, nn(flip, q_ref[cols, :]).astype(bf)).astype(bf)
        dpk = dpk + nn(q_cols, spread)
    dpk_ref[...] = dpk
    for block in range(length // BLOCK):
        rows = slice(block * BLOCK, (block + 1) * BLOCK)
        groups, edges = [], []
        for sub in range(2):
            key_tile = 2 * block + sub
            own = slice(key_tile * TILE, (key_tile + 1) * TILE)
            seen_by = [t for t in range(tiles) if tile_seen(t, key_tile, length)]

            def held(query_tile):
                return dr_ref[own, query_tile * TILE : (query_tile + 1) * TILE]

            band = [blank]
            for step in (-2, -1, 0, 1, 2):
                query_tile = key_tile + step
                band.append(held(query_tile) if query_tile in seen_by else blank)
            ends = []
            for chosen in ([t for t in seen_by if t - key_tile <= -3], [t for t in seen_by if t - key_tile >= 3]):
                total = blank
                if chosen:
                    total = sum((held(t).astype(jnp.float32) for t in chosen[1:]), held(chosen[0]).astype(jnp.float32)).astype(bf)
                ends.append(total)
            groups.append(jnp.concatenate(band[1:] + ends, axis=1))
        turned = nn(flip, jnp.concatenate(groups, axis=0))
        width = BAND - TILE
        spreads = []
        for sub in range(2):
            own = turned[sub * TILE : (sub + 1) * TILE]
            spreads.append(
                add_edges(unskew([blank, own[:, :width].astype(bf)]), [own[:, width : width + TILE]], [own[:, width + TILE :]])
            )
        spread = jnp.concatenate(spreads, axis=0)
        d_key = nn(flip, nn(spread, pq_ref[...]).astype(bf))
        put(1, rows, dk_acc[rows, :] + d_key)
        k_cols = nt(pick, nn(flip, k_ref[rows, :]).astype(bf)).astype(bf)
        dpq = dpq + nn(k_cols, spread)
        put(2, rows, dv_acc[rows, :])
    dpq_ref[...] = dpq


def add_edges(spread, first, last):
    parts = [spread[:, 0:TILE], spread[:, TILE : BAND - TILE], spread[:, BAND - TILE :]]
    for place, tiles in ((0, first), (2, last)):
        if tiles:
            total = parts[place].astype(jnp.float32)
            for tile in tiles:
                total = total + tile
            parts[place] = total.astype(jnp.bfloat16)
    return jnp.concatenate(parts, axis=1)


def attention_backward(merged, dctx, probs, pos_band, pair, head, found=()):
    length, width = merged.shape[0], merged.shape[1] // 3
    pairs = width // PAIR
    tall = [pl.BlockSpec((length, PAIR), lambda p, at=at: (0, at)) for at in (pair, pairs + pair, 2 * pairs + pair, pair)]
    band = [pl.BlockSpec((BAND, PAIR), lambda p, at=at: (0, at)) for at in (pair, pairs + pair)]
    own = pl.BlockSpec((length, PAIR), lambda p: (0, 0))
    table = pl.BlockSpec((HEAD_DIM, BAND), lambda p: (0, 0))
    flat = jax.ShapeDtypeStruct((length, PAIR), jnp.bfloat16)
    wide = jax.ShapeDtypeStruct((HEAD_DIM, BAND), jnp.float32)
    return pl.pallas_call(
        functools.partial(backward_body, head),
        grid=(1,),
        in_specs=tall + [pl.BlockSpec((length, length), lambda p: (0, 0))] + band + [own] * len(found),
        out_specs=[own, own, own, table, table],
        out_shape=[flat, flat, flat, wide, wide],
        scratch_shapes=[
            pltpu.VMEM((length, length), jnp.bfloat16),
            pltpu.VMEM((length, PAIR), jnp.float32),
            pltpu.VMEM((length, PAIR), jnp.float32),
        ],
        compiler_params=pltpu.CompilerParams(dimension_semantics=("arbitrary",), vmem_limit_bytes=24 << 20),
        cost_estimate=pl.CostEstimate(flops=2 * 10**9, transcendentals=0, bytes_accessed=4 << 20),
        name="attention_backward",
    )(merged, merged, merged, dctx, probs, pos_band, pos_band, *found)


CORES = [(0, 1), (1, 0)]


def swap(value):
    return lax.ppermute(value, "seq", CORES)


def ordered(core, own, other, axis=0):
    return jnp.concatenate(
        [jnp.where(core == 0, own, other), jnp.where(core == 0, other, own)], axis=axis
    )


def half_of(core, matrix, axis):
    size = matrix.shape[axis] // 2
    return lax.dynamic_slice_in_dim(matrix, core * size, size, axis)


def chip_bits():
    chip = lax.axis_index("dp")
    return chip // 4, (chip // 2) % 2, chip % 2


def exchange(value, mask):
    return lax.ppermute(value, "dp", [(i, i ^ mask) for i in range(16)])


def tie(chains, others=()):
    states, others = lax.optimization_barrier(([chain.state for chain in chains], others))
    for chain, state in zip(chains, states):
        chain.state = state
    return others


class Gather:
    def __init__(self, *values):
        self.state = values

    def line(self, step):
        up = [(i, i + 4) for i in range(12) if i // 4 >= step - 1]
        down = [(i + 4, i) for i in range(12) if i // 4 <= 3 - step]
        if step == 1:
            self.state = [([value], [value]) for value in self.state]
        self.state = [
            (below + [lax.ppermute(below[-1], "dp", up)], above + [lax.ppermute(above[-1], "dp", down)])
            for below, above in self.state
        ]
        if step == 3:
            z = chip_bits()[0]
            lines = []
            for below, above in self.state:
                blocks = []
                for block in range(4):
                    options = [below[k - block] if k >= block else above[block - k] for k in range(4)]
                    blocks.append(lax.select_n(z, *options))
                lines.append(tuple(jnp.stack([b[side] for b in blocks]) for side in range(2)))
            self.state = lines

    def double(self, step):
        z = chip_bits()[0]
        bit = z % 2 if step == 1 else z // 2
        result = []
        for value in self.state:
            other = exchange(value, 4 * step)
            result.append(jnp.stack([jnp.where(bit == 0, value, other), jnp.where(bit == 0, other, value)]))
        self.state = result
        if step == 2:
            self.state = [
                tuple(value[:, :, side].reshape((4,) + value.shape[3:]) for side in range(2)) for value in result
            ]

    def pair(self, step):
        _, y, x = chip_bits()
        order = ((x, 1), (y, 2)) if step == 1 else ((y, 2), (x, 1))
        lines = []
        for halves in self.state:
            result = []
            for value, (bit, mask) in zip(halves, order):
                other = exchange(value, mask)
                result.append(jnp.stack([jnp.where(bit == 0, value, other), jnp.where(bit == 0, other, value)]))
            lines.append(tuple(result))
        self.state = lines

    def rows(self, index, low, high):
        first, second = [half[..., low:high] for half in self.state[index]]
        first = jnp.moveaxis(first, (0, 1, 2), (1, 2, 0))
        second = jnp.moveaxis(second, (0, 1, 2), (2, 1, 0))
        whole = jnp.stack([first, second], axis=3)
        return whole.reshape(-1, whole.shape[-1])


class Scatter:
    def __init__(self, *values):
        self.state = []
        for value in values:
            grid = value.reshape((4, 2, 2) + value.shape[1:])
            self.state.append((jnp.moveaxis(grid[:, :, :, 0], 2, 0), jnp.moveaxis(grid[:, :, :, 1], 1, 0)))

    def pair(self, step):
        _, y, x = chip_bits()
        order = ((x, 1), (y, 2)) if step == 1 else ((y, 2), (x, 1))
        sums = []
        for halves in self.state:
            result = []
            for value, (bit, mask) in zip(halves, order):
                keep = jnp.where(bit == 0, value[0], value[1])
                give = jnp.where(bit == 0, value[1], value[0])
                total = (keep.astype(jnp.float32) + exchange(give, mask).astype(jnp.float32)).astype(value.dtype)
                result.append(jnp.moveaxis(total, 1, 0) if step == 1 else total)
            sums.append(tuple(result) if step == 1 else (jnp.stack(result, axis=1), None, None))
        self.state = sums

    def line(self, step):
        z = chip_bits()[0]
        offset = 4 - step
        ups = [(i, i + 4) for i in range(12) if i // 4 + offset <= 3]
        downs = [(i + 4, i) for i in range(12) if i // 4 + 1 - offset >= 0]
        sums, self.totals = [], []
        for value, up, down in self.state:

            def block(at):
                options = [value[min(max(k + at, 0), 3)] for k in range(4)]
                return lax.select_n(z, *options).astype(jnp.float32)

            to_above, to_below = block(offset), block(-offset)
            if up is not None:
                to_above = to_above + up.astype(jnp.float32)
                to_below = to_below + down.astype(jnp.float32)
            up = lax.ppermute(to_above.astype(value.dtype), "dp", ups)
            down = lax.ppermute(to_below.astype(value.dtype), "dp", downs)
            sums.append((value, up, down))
            if step == 3:
                self.totals.append(block(0) + up.astype(jnp.float32) + down.astype(jnp.float32))
        self.state = sums


def norm_parts(value):
    average = jnp.mean(value, axis=-1, keepdims=True)
    centred = value - average
    variance = jnp.mean(centred * centred, axis=-1, keepdims=True)
    inverse = lax.rsqrt(variance + eps_norm)
    return centred * inverse, inverse


def norm_back(unit, inverse, gain, grad):
    scaled = grad * gain
    mean_grad = jnp.mean(scaled, axis=-1, keepdims=True)
    mean_along = jnp.mean(scaled * unit, axis=-1, keepdims=True)
    return inverse * (scaled - mean_grad - unit * mean_along)


def head_split(
    hidden_in, prefix, w_qkv, q_bias, v_bias, rel_table, w_posk, w_posq, posq_bias, w_out, out_bias,
    norm1_gain, norm1_bias, w_up, up_bias, w_down, down_bias, norm2_gain, norm2_bias, out_grad,
):
    bf = jnp.bfloat16
    f32 = jnp.float32
    core = lax.axis_index("seq")
    rows = w_qkv.shape[0]
    units = w_down.shape[0]
    table_rows = rel_table.shape[0]
    chips = 16
    half = D // 2
    ff_half = chips * units
    buckets = 2 * SPAN

    last_rows = rows - table_rows
    vectors = (q_bias, v_bias, posq_bias, out_bias, norm1_gain, norm1_bias, down_bias, norm2_gain)
    left = jnp.stack(vectors)
    right = jnp.concatenate(
        [jnp.pad(norm2_bias, (0, units - rows))[None], up_bias[None], jnp.zeros((last_rows - 2, units), bf)], axis=0
    )
    small = jnp.concatenate([jnp.pad(left, ((0, 0), (0, 128 - rows))), jnp.pad(right, ((0, 0), (0, half - 128 - units)))], axis=1)

    def columns(side):
        qkv = w_qkv.reshape(rows, 3, 2, half)[:, :, side].reshape(rows, 3 * half)
        corner = jnp.concatenate([rel_table[:, side * half : (side + 1) * half], small], axis=0)
        cut = slice(side * half, (side + 1) * half)
        up = w_up.reshape(rows, chips, 2, units)[:, :, side].reshape(rows, ff_half)
        return (
            jnp.concatenate([qkv, w_posk[:, cut], w_posq[:, cut], corner], axis=1),
            jnp.concatenate([w_out[:, cut], up], axis=1),
        )

    early0, late0 = columns(0)
    early1, late1 = columns(1)
    early_got = swap(jnp.where(core == 0, early1, early0))
    late_got = swap(jnp.where(core == 0, late1, late0))
    hidden_got = swap(hidden_in)

    def by_core(first, second, got):
        own = jnp.where(core == 0, first, second)
        return jnp.stack([jnp.where(core == 0, own, got), jnp.where(core == 0, got, own)])

    early_chain = Gather(by_core(early0, early1, early_got))
    downs = jnp.concatenate([w_down.reshape(2, 2, rows, D)[:, 0], w_down.reshape(2, 2, rows, D)[:, 1]], axis=-1)
    late_chain = Gather(jnp.concatenate([by_core(late0, late1, late_got), downs], axis=-1))
    for step in (1, 2, 3):
        early_chain.line(step)
    tie((early_chain, late_chain))
    early_chain.pair(1)
    late_chain.double(1)
    tie((early_chain, late_chain))
    early_chain.pair(2)
    late_chain.double(2)
    hidden_all = ordered(core, hidden_in, hidden_got)
    w_qkv_own = early_chain.rows(0, 0, 3 * half)
    w_pos_own = early_chain.rows(0, 3 * half, 5 * half)
    corner = early_chain.rows(0, 5 * half, 6 * half).reshape(2 * chips, rows, half)
    table_half = corner[:, :table_rows].reshape(buckets, half)
    small = corner[:, table_rows:]
    table = ordered(core, table_half, swap(table_half), axis=1)

    owner = (lax.broadcasted_iota(jnp.int32, (2 * chips, D), 1) // rows == lax.broadcasted_iota(jnp.int32, (2 * chips, D), 0)).astype(bf)
    inside = lax.broadcasted_iota(jnp.int32, (rows, D), 1) % rows == lax.broadcasted_iota(jnp.int32, (rows, D), 0)
    unit_owner = (
        2 * (lax.broadcasted_iota(jnp.int32, (2 * chips, ff_half), 1) // units) + core
        == lax.broadcasted_iota(jnp.int32, (2 * chips, ff_half), 0)
    ).astype(bf)
    unit_inside = lax.broadcasted_iota(jnp.int32, (units, ff_half), 1) % units == lax.broadcasted_iota(jnp.int32, (units, ff_half), 0)
    spots = jnp.concatenate([small[:, :, :rows], small[:, :, 128 : 128 + rows]], axis=1)
    wide = lax.dot_general(spots, owner, (((0,), (0,)), ((), ())), preferred_element_type=f32)
    lists = jnp.sum(jnp.where(inside, wide, 0.0), axis=1)
    qb, vb, pqb, ob, gain1, shift1, db, gain2, shift2 = [lists[i] for i in range(9)]
    wide = inner_first(small[:, 1, 128 : 128 + units], unit_owner)
    ub = jnp.sum(jnp.where(unit_inside, wide, 0.0), axis=0)

    band = lax.broadcasted_iota(jnp.int32, (BAND, buckets), 0)
    bucket = lax.broadcasted_iota(jnp.int32, (BAND, buckets), 1)
    chosen = (jnp.clip(SPAN + 384 - band, 0, buckets - 1) == bucket).astype(bf)
    pos_shift = jnp.concatenate([jnp.zeros((half,), f32), half_of(core, pqb, 0)])
    pos = (product(table, w_pos_own) + pos_shift).astype(bf)
    pos_band = product(chosen, pos).astype(bf)

    qkv_shift = jnp.concatenate([half_of(core, qb, 0), jnp.zeros((half,), f32), half_of(core, vb, 0)])
    merged = (product(hidden_all, w_qkv_own) + qkv_shift).astype(bf)
    merged, pos_band = tie((late_chain,), (merged, pos_band))
    late_chain.pair(1)
    context_parts, prob_parts = [], []
    for pair in range(half // PAIR):
        part, kept = attention_forward(prefix, merged, pos_band, pair, 0)
        prob_parts.append(kept)
        part, kept = attention_forward(prefix, merged, pos_band, pair, 1, (part,))
        prob_parts.append(kept)
        if pair == 0:
            part, merged = tie((late_chain,), (part, merged))
            late_chain.pair(2)
        context_parts.append(part)
    context = jnp.concatenate(context_parts, axis=1)
    out_columns = late_chain.rows(0, 0, half)
    w_out_own = ordered(
        core, half_of(core, out_columns, 0), swap(half_of(1 - core, out_columns, 0)), axis=1
    )
    w_up_own = late_chain.rows(0, half, half + ff_half)
    down_at = half + ff_half
    down_parts = [late_chain.rows(0, at, at + D).reshape(2 * chips, rows, D) for at in (down_at, down_at + D)]
    w_down_own = jnp.stack(down_parts, axis=1).reshape(ff_half, D)

    def summed_rows(left, multiply):
        given = swap(multiply(half_of(1 - core, left, 0)).astype(bf))
        return multiply(half_of(core, left, 0)) + given.astype(f32)

    hidden_f = hidden_in.astype(f32)
    residual1 = hidden_f + summed_rows(context, lambda part: product(part, w_out_own)) + ob
    unit1, inverse1 = norm_parts(residual1)
    normed = unit1 * gain1 + shift1
    normed_low = normed.astype(bf)
    normed_all = ordered(core, normed_low, swap(normed_low))
    expanded = product(normed_all, w_up_own) + ub
    normal_cdf = 0.5 + 0.5 * lax.erf(expanded * math.sqrt(0.5))
    activated = (expanded * normal_cdf).astype(bf)
    slope = (
        normal_cdf + expanded * jnp.exp(-0.5 * expanded * expanded) * (1.0 / math.sqrt(2.0 * math.pi))
    ).astype(bf)
    residual2 = normed + summed_rows(activated, lambda part: product(part, w_down_own)) + db
    unit2, inverse2 = norm_parts(residual2)
    hidden_out = (unit2 * gain2 + shift2).astype(bf)

    grad = out_grad.astype(f32)
    d_res2 = norm_back(unit2, inverse2, gain2, grad)
    d_gain2 = jnp.sum(grad * unit2, axis=0, keepdims=True)
    d_shift2 = jnp.sum(grad, axis=0, keepdims=True)
    d_reduced = d_res2.astype(bf)
    d_down_bias = column_sums(d_reduced)[None]
    reduced_all = ordered(core, d_reduced, swap(d_reduced))
    d_expanded = (inner_last(reduced_all, w_down_own) * slope.astype(f32)).astype(bf)
    d_normed = summed_rows(d_expanded, lambda part: inner_last(part, w_up_own)) + d_res2
    d_wdown = inner_first(activated, reduced_all).astype(bf)
    d_wup = inner_first(normed_all, d_expanded).astype(bf)
    d_up_bias = column_sums(d_expanded)
    d_res1 = norm_back(unit1, inverse1, gain1, d_normed)
    d_gain1 = jnp.sum(d_normed * unit1, axis=0, keepdims=True)
    d_shift1 = jnp.sum(d_normed, axis=0, keepdims=True)
    d_attended = d_res1.astype(bf)
    d_out_bias = column_sums(d_attended)[None]
    attended_all = ordered(core, d_attended, swap(d_attended))
    d_context = inner_last(attended_all, w_out_own).astype(bf)
    d_wout_rows = inner_first(context, attended_all).astype(bf)
    d_wout = ordered(
        core, half_of(core, d_wout_rows, 1), swap(half_of(1 - core, d_wout_rows, 1)), axis=0
    )

    def rejoin(first, second):
        own = jnp.where(core == 0, first, second)
        got = swap(jnp.where(core == 0, second, first))
        return jnp.where(core == 0, own, got), jnp.where(core == 0, got, own)

    late_cols = jnp.concatenate([d_wout, d_wup], axis=1).reshape(chips, 2, rows, half + ff_half)
    down_cols = d_wdown.reshape(chips, 2, 2, rows, D)
    late_sums = Scatter(jnp.concatenate([late_cols, down_cols[:, :, 0], down_cols[:, :, 1]], axis=-1))
    grads = []
    late_steps = {0: lambda: late_sums.pair(1), 3: lambda: late_sums.pair(2), 5: lambda: late_sums.line(1)}
    found = ()
    for index in range(half // HEAD_DIM):
        if index in late_steps:
            found, d_context = tie((late_sums,), (found, d_context))
            late_steps[index]()
        if index % 2 == 0:
            found = ()
        found = attention_backward(merged, d_context, prob_parts[index], pos_band, index // 2, index % 2, tuple(found[:3]))
        grads.append(found)
    grads[-1] = tie((late_sums,), found)
    late_sums.line(2)
    d_merged = jnp.concatenate([g[i] for i in range(3) for g in grads[1::2]], axis=1)
    d_q, d_v = d_merged[:, :half], d_merged[:, 2 * half :]
    d_wqkv = inner_first(hidden_all, d_merged).astype(bf)
    d_q_bias = column_sums(d_q)[None]
    d_v_bias = column_sums(d_v)[None]
    d_band = jnp.concatenate([g[i] for i in (3, 4) for g in grads], axis=0).astype(bf)
    d_pos = lax.dot_general(
        chosen, d_band, (((0,), (1,)), ((), ())), preferred_element_type=f32
    )
    d_posq_bias = jnp.sum(d_pos[:, half:], axis=0, keepdims=True)
    d_pos_low = d_pos.astype(bf)
    d_wpos = inner_first(table, d_pos_low).astype(bf)
    d_table_all = inner_last(d_pos_low, w_pos_own).astype(bf)
    d_table = (
        half_of(core, d_table_all, 1).astype(f32)
        + swap(half_of(1 - core, d_table_all, 1)).astype(f32)
    ).astype(bf)

    def whole(part):
        blank = jnp.zeros_like(part)
        return ordered(core, part, blank, axis=1)

    lists_grad = jnp.concatenate(
        [whole(jnp.concatenate([d_q_bias, d_v_bias, d_posq_bias], axis=0)), d_out_bias, d_gain1, d_shift1, d_down_bias, d_gain2, d_shift2],
        axis=0,
    ).astype(bf)
    lists_grad = jnp.pad(lists_grad, ((0, 7), (0, 0)))
    pieces = jnp.where(inside, lists_grad[:, None, :], jnp.zeros((), bf)).reshape(16 * rows, D)
    unit_at = lax.broadcasted_iota(jnp.int32, (half, ff_half), 1) % units + 256 == lax.broadcasted_iota(jnp.int32, (half, ff_half), 0)
    unit_pieces = jnp.where(unit_at, d_up_bias.astype(bf), jnp.zeros((), bf))
    vector = (inner_last(owner, pieces) + inner_last(unit_owner, unit_pieces)).astype(bf)
    corner_grad = jnp.concatenate(
        [
            d_table.reshape(2 * chips, table_rows, half),
            jnp.pad(vector[:, None, :], ((0, 0), (0, last_rows - 1), (0, 0))),
        ],
        axis=1,
    ).reshape(chips * 2 * rows, half)
    early_sums = Scatter(
        jnp.concatenate([d_wqkv, d_wpos, corner_grad], axis=1).reshape(chips, 2, rows, 6 * half)
    )
    d_merged = tie((early_sums,), d_merged)
    early_sums.pair(1)
    in_grad = d_res1 + summed_rows(d_merged, lambda part: inner_last(part, w_qkv_own))
    in_grad = tie((late_sums,), in_grad)
    late_sums.line(3)
    late_grads = late_sums.totals[0]
    down_grads = late_grads[:, :, half + ff_half :]
    late_grads = late_grads[:, :, : half + ff_half]
    late_left, late_right = rejoin(late_grads[0], late_grads[1])
    place = lax.broadcasted_iota(jnp.int32, (D, D), 0)
    place = (place % half) // units * (2 * units) + place // half * units + place % units
    unit_order = (place == lax.broadcasted_iota(jnp.int32, (D, D), 1)).astype(bf)
    early_sums.pair(2)
    g_wdown = jnp.stack([down_grads[:, :, :D], down_grads[:, :, D:]], axis=1).reshape(units, D)
    g_wout = jnp.concatenate([late_left[:, :half], late_right[:, :half]], axis=1)
    joined = []
    for group in range(ff_half // half):
        cut = slice(half + group * half, half + (group + 1) * half)
        joined.append(jnp.concatenate([late_left[:, cut], late_right[:, cut]], axis=1))
    joined = product(jnp.concatenate(joined, axis=0).astype(bf), unit_order)
    g_wup = jnp.concatenate([joined[g * rows : (g + 1) * rows] for g in range(ff_half // half)], axis=1)
    g_wdown, g_wout, g_wup, in_grad = tie((early_sums,), (g_wdown, g_wout, g_wup, in_grad))
    for step in (1, 2, 3):
        early_sums.line(step)
    early_grads = early_sums.totals[0]
    early_left, early_right = rejoin(early_grads[0], early_grads[1])
    vector_sum = early_left[table_rows, 5 * half :] + early_right[table_rows, 5 * half :]

    def side_by_side(left, right, at, count):
        pieces = []
        for index in range(count):
            cut = slice((at + index) * half, (at + index + 1) * half)
            pieces += [left[:, cut], right[:, cut]]
        return jnp.concatenate(pieces, axis=1)

    g_wqkv = side_by_side(early_left, early_right, 0, 3)
    g_wposk = side_by_side(early_left, early_right, 3, 1)
    g_wposq = side_by_side(early_left, early_right, 4, 1)
    g_table = side_by_side(early_left, early_right, 5, 1)[:table_rows]
    g = [vector_sum[i * rows : (i + 1) * rows] for i in range(9)]
    g_up_bias = vector_sum[256 : 256 + units]
    return (
        hidden_out, in_grad, g_wqkv, g[0], g[1], g_table, g_wposk, g_wposq, g[2], g_wout, g[3], g[4], g[5],
        g_wup, g_up_bias, g_wdown, g[6], g[7], g[8],
    )


def row_split(
    hidden_in,
    prefix,
    w_qkv,
    q_bias,
    v_bias,
    rel_table,
    w_posk,
    w_posq,
    posq_bias,
    w_out,
    out_bias,
    norm1_gain,
    norm1_bias,
    w_up,
    up_bias,
    w_down,
    down_bias,
    norm2_gain,
    norm2_bias,
    out_grad,
):
    gathered = (
        lax.all_gather(w_qkv, ("dp", "seq"), axis=0, tiled=True),
        lax.all_gather(q_bias, ("dp", "seq"), axis=0, tiled=True),
        lax.all_gather(v_bias, ("dp", "seq"), axis=0, tiled=True),
        lax.all_gather(rel_table, ("dp", "seq"), axis=0, tiled=True),
        lax.all_gather(w_posk, ("dp", "seq"), axis=0, tiled=True),
        lax.all_gather(w_posq, ("dp", "seq"), axis=0, tiled=True),
        lax.all_gather(posq_bias, ("dp", "seq"), axis=0, tiled=True),
        lax.all_gather(w_out, ("dp", "seq"), axis=0, tiled=True),
        lax.all_gather(out_bias, ("dp", "seq"), axis=0, tiled=True),
        lax.all_gather(norm1_gain, ("dp", "seq"), axis=0, tiled=True),
        lax.all_gather(norm1_bias, ("dp", "seq"), axis=0, tiled=True),
        lax.all_gather(w_up, ("dp", "seq"), axis=0, tiled=True),
        lax.all_gather(up_bias, ("dp", "seq"), axis=0, tiled=True),
        lax.all_gather(w_down, ("dp", "seq"), axis=0, tiled=True),
        lax.all_gather(down_bias, ("dp", "seq"), axis=0, tiled=True),
        lax.all_gather(norm2_gain, ("dp", "seq"), axis=0, tiled=True),
        lax.all_gather(norm2_bias, ("dp", "seq"), axis=0, tiled=True),
    )
    (
        full_qkv,
        full_qb,
        full_vb,
        full_table,
        full_posk,
        full_posq,
        full_pqb,
        full_out,
        full_ob,
        full_g1,
        full_b1,
        full_up,
        full_ub,
        full_down,
        full_db,
        full_g2,
        full_b2,
    ) = gathered
    row_count = hidden_in.shape[0]
    groups = lax.axis_size("seq")
    seq_length = row_count * groups
    seq_rank = lax.axis_index("seq")
    prefix_len = prefix[0]
    score_scale = 1.0 / math.sqrt(3 * HEAD_DIM)
    buckets = 2 * SPAN
    window = row_count + buckets
    first_row = seq_rank * row_count
    query_pos = first_row + jnp.arange(row_count, dtype=jnp.int32)
    key_pos = jnp.arange(seq_length, dtype=jnp.int32)
    visible = (key_pos[None, :] < prefix_len) | (key_pos[None, :] <= query_pos[:, None])
    padded_cols = jnp.arange(seq_length + buckets, dtype=jnp.int32)
    below_window = padded_cols[None, :] < first_row

    def skew_table(table, row_total, offset, col_total):
        shifted = jnp.pad(
            jnp.flip(table, axis=1), ((0, 0), (row_count, row_count - 1)), mode="edge"
        )
        stride = shifted.shape[1] - 1
        flattened = shifted.reshape(-1)
        picked = lax.slice_in_dim(flattened, offset, offset + row_total * stride)
        return picked.reshape(row_total, stride)[:, :col_total]

    def pos_terms(table_a, table_w, edge_terms):
        band_terms = (
            skew_table(table_a, row_count, row_count - 1, window)
            + skew_table(table_w, window, window - 1, row_count).T
        )
        low_side = table_a[:, buckets - 1 : buckets] + jnp.pad(edge_terms[0], (SPAN, SPAN))[None, :]
        high_side = table_a[:, 0:1] + jnp.pad(edge_terms[1], (SPAN, SPAN))[None, :]
        backdrop = jnp.where(below_window, low_side, high_side)
        placed = lax.dynamic_update_slice(
            backdrop, band_terms, (jnp.zeros((), jnp.int32), first_row)
        )
        return placed[:, SPAN : SPAN + seq_length]

    pos_keys = product(full_table, full_posk).astype(jnp.bfloat16)
    pos_queries = (product(full_table, full_posq) + full_pqb.astype(jnp.float32)).astype(
        jnp.bfloat16
    )
    merged = product(hidden_in, full_qkv)
    queries = (merged[:, :D] + full_qb.astype(jnp.float32)).astype(jnp.bfloat16)
    keys_local = merged[:, D : 2 * D].astype(jnp.bfloat16)
    values_local = (merged[:, 2 * D :] + full_vb.astype(jnp.float32)).astype(jnp.bfloat16)
    keys_all, values_all = (
        lax.all_gather(keys_local, "seq", axis=0, tiled=True),
        lax.all_gather(values_local, "seq", axis=0, tiled=True),
    )
    query_heads = split_heads(queries)
    key_heads = split_heads(keys_all)
    value_heads = split_heads(values_all)
    posk_heads = split_heads(pos_keys)
    posq_heads = split_heads(pos_queries)

    def head_scores(query_h, key_h, posk_h, posq_h):
        content = inner_last(query_h, key_h)
        table_a = inner_last(query_h, posk_h)
        key_padded = jnp.pad(key_h, ((SPAN, SPAN), (0, 0)))
        key_window = lax.dynamic_slice_in_dim(key_padded, first_row, window, 0)
        table_w = inner_last(key_window, posq_h)
        end_rows = jnp.stack([posq_h[0], posq_h[buckets - 1]])
        edge_terms = inner_last(end_rows, key_h)
        raw = content + pos_terms(table_a, table_w, edge_terms)
        masked = jnp.where(visible, raw * score_scale, -jnp.inf)
        return (masked, table_a, table_w, edge_terms, key_window, end_rows)

    def head_forward(operands):
        query_h, key_h, value_h, posk_h, posq_h = operands
        scores = head_scores(query_h, key_h, posk_h, posq_h)[0]
        highest = jnp.max(scores, axis=1, keepdims=True)
        expo = jnp.exp(scores - highest)
        totals = jnp.sum(expo, axis=1, keepdims=True)
        probs_low = (expo / totals).astype(jnp.bfloat16)
        return (product(probs_low, value_h), (highest + jnp.log(totals))[:, 0])

    contexts, log_totals = lax.map(
        head_forward, (query_heads, key_heads, value_heads, posk_heads, posq_heads)
    )
    context = join_heads(contexts).astype(jnp.bfloat16)
    hidden_f = hidden_in.astype(jnp.float32)
    residual1 = hidden_f + product(context, full_out) + full_ob.astype(jnp.float32)
    gain1 = full_g1.astype(jnp.float32)
    shift1 = full_b1.astype(jnp.float32)
    normed = normalize(residual1, gain1, shift1)
    normed_low = normed.astype(jnp.bfloat16)
    expanded = product(normed_low, full_up) + full_ub.astype(jnp.float32)
    activated = gelu_exact(expanded).astype(jnp.bfloat16)
    residual2 = normed + product(activated, full_down) + full_db.astype(jnp.float32)
    gain2 = full_g2.astype(jnp.float32)
    shift2 = full_b2.astype(jnp.float32)
    hidden_out = normalize(residual2, gain2, shift2).astype(jnp.bfloat16)
    regathered = (
        lax.all_gather(w_qkv, ("dp", "seq"), axis=0, tiled=True),
        lax.all_gather(q_bias, ("dp", "seq"), axis=0, tiled=True),
        lax.all_gather(v_bias, ("dp", "seq"), axis=0, tiled=True),
        lax.all_gather(rel_table, ("dp", "seq"), axis=0, tiled=True),
        lax.all_gather(w_posk, ("dp", "seq"), axis=0, tiled=True),
        lax.all_gather(w_posq, ("dp", "seq"), axis=0, tiled=True),
        lax.all_gather(posq_bias, ("dp", "seq"), axis=0, tiled=True),
        lax.all_gather(w_out, ("dp", "seq"), axis=0, tiled=True),
        lax.all_gather(out_bias, ("dp", "seq"), axis=0, tiled=True),
        lax.all_gather(norm1_gain, ("dp", "seq"), axis=0, tiled=True),
        lax.all_gather(norm1_bias, ("dp", "seq"), axis=0, tiled=True),
        lax.all_gather(w_up, ("dp", "seq"), axis=0, tiled=True),
        lax.all_gather(up_bias, ("dp", "seq"), axis=0, tiled=True),
        lax.all_gather(w_down, ("dp", "seq"), axis=0, tiled=True),
        lax.all_gather(down_bias, ("dp", "seq"), axis=0, tiled=True),
        lax.all_gather(norm2_gain, ("dp", "seq"), axis=0, tiled=True),
        lax.all_gather(norm2_bias, ("dp", "seq"), axis=0, tiled=True),
    )
    (
        back_qkv,
        back_qb,
        back_vb,
        back_table,
        back_posk,
        back_posq,
        back_pqb,
        back_out,
        back_ob,
        back_g1,
        back_b1,
        back_up,
        back_ub,
        back_down,
        back_db,
        back_g2,
        back_b2,
    ) = regathered
    _, pull_second = jax.vjp(normalize, residual2, gain2, shift2)
    d_res2, d_gain2, d_shift2 = pull_second(out_grad.astype(jnp.float32))
    d_reduced = d_res2.astype(jnp.bfloat16)
    d_wdown = inner_first(activated, d_reduced)
    d_down_bias = column_sums(d_reduced)
    d_activated = inner_last(d_reduced, back_down)
    _, pull_gelu = jax.vjp(gelu_exact, expanded)
    d_expanded = pull_gelu(d_activated)[0].astype(jnp.bfloat16)
    d_wup = inner_first(normed_low, d_expanded)
    d_up_bias = column_sums(d_expanded)
    d_normed = inner_last(d_expanded, back_up) + d_res2
    _, pull_first = jax.vjp(normalize, residual1, gain1, shift1)
    d_res1, d_gain1, d_shift1 = pull_first(d_normed)
    d_attended = d_res1.astype(jnp.bfloat16)
    d_wout = inner_first(context, d_attended)
    d_out_bias = column_sums(d_attended)
    d_context = inner_last(d_attended, back_out).astype(jnp.bfloat16)
    dctx_heads = split_heads(d_context)

    def head_backward(operands):
        query_h, key_h, value_h, posk_h, posq_h, log_total, dctx_h = operands
        scores, table_a, table_w, edge_terms, key_window, end_rows = head_scores(
            query_h, key_h, posk_h, posq_h
        )
        probs = jnp.exp(scores - log_total[:, None])
        probs_low = probs.astype(jnp.bfloat16)
        d_probs = inner_last(dctx_h, value_h)
        d_value = inner_first(probs_low, dctx_h)
        row_dot = jnp.sum(probs * d_probs, axis=1, keepdims=True)
        d_raw = (probs * (d_probs - row_dot) * score_scale).astype(jnp.bfloat16)
        _, pull_terms = jax.vjp(pos_terms, table_a, table_w, edge_terms)
        d_table_a, d_table_w, d_edges = pull_terms(d_raw.astype(jnp.float32))
        d_table_a = d_table_a.astype(jnp.bfloat16)
        d_table_w = d_table_w.astype(jnp.bfloat16)
        d_edges = d_edges.astype(jnp.bfloat16)
        d_query = product(d_raw, key_h) + product(d_table_a, posk_h)
        window_grad = product(d_table_w, posq_h)
        key_canvas = jnp.zeros((seq_length + buckets, HEAD_DIM), jnp.float32)
        placed_grad = lax.dynamic_update_slice(
            key_canvas, window_grad, (first_row, jnp.zeros((), jnp.int32))
        )
        d_key = (
            inner_first(d_raw, query_h)
            + placed_grad[SPAN : SPAN + seq_length]
            + inner_first(d_edges, end_rows)
        )
        d_posk = inner_first(d_table_a, query_h)
        end_grads = product(d_edges, key_h)
        d_posq = inner_first(d_table_w, key_window)
        d_posq = d_posq.at[0].add(end_grads[0]).at[buckets - 1].add(end_grads[1])
        return (d_query, d_key, d_value, d_posk, d_posq)

    d_q_heads, d_k_heads, d_v_heads, d_posk_heads, d_posq_heads = lax.map(
        head_backward,
        (query_heads, key_heads, value_heads, posk_heads, posq_heads, log_totals, dctx_heads),
    )
    d_queries = join_heads(d_q_heads).astype(jnp.bfloat16)
    d_keys_part, d_values_part = (
        lax.psum_scatter(
            join_heads(d_k_heads).astype(jnp.bfloat16), "seq", scatter_dimension=0, tiled=True
        ).astype(jnp.float32),
        lax.psum_scatter(
            join_heads(d_v_heads).astype(jnp.bfloat16), "seq", scatter_dimension=0, tiled=True
        ).astype(jnp.float32),
    )
    d_keys = d_keys_part.astype(jnp.bfloat16)
    d_values = d_values_part.astype(jnp.bfloat16)
    d_merged = jnp.concatenate([d_queries, d_keys, d_values], axis=1)
    d_wqkv = inner_first(hidden_in, d_merged)
    d_q_bias = column_sums(d_queries)
    d_v_bias = column_sums(d_values)
    in_grad = d_res1 + inner_last(d_merged, back_qkv)
    d_posk_rows, d_posq_rows = (
        lax.psum_scatter(join_heads(d_posk_heads), ("dp", "seq"), scatter_dimension=0, tiled=True),
        lax.psum_scatter(join_heads(d_posq_heads), ("dp", "seq"), scatter_dimension=0, tiled=True),
    )
    d_posk_low = d_posk_rows.astype(jnp.bfloat16)
    d_posq_low = d_posq_rows.astype(jnp.bfloat16)
    rel_table_grad = inner_last(d_posk_low, back_posk) + inner_last(d_posq_low, back_posq)
    d_wposk = inner_first(rel_table, d_posk_low)
    d_wposq = inner_first(rel_table, d_posq_low)
    d_posq_bias = column_sums(d_posq_low)
    summed = (
        lax.psum_scatter(d_wqkv, ("dp", "seq"), scatter_dimension=0, tiled=True),
        lax.psum_scatter(d_q_bias, ("dp", "seq"), scatter_dimension=0, tiled=True),
        lax.psum_scatter(d_v_bias, ("dp", "seq"), scatter_dimension=0, tiled=True),
        lax.psum_scatter(d_wposk, ("dp", "seq"), scatter_dimension=0, tiled=True),
        lax.psum_scatter(d_wposq, ("dp", "seq"), scatter_dimension=0, tiled=True),
        lax.psum_scatter(d_posq_bias, ("dp", "seq"), scatter_dimension=0, tiled=True),
        lax.psum_scatter(d_wout, ("dp", "seq"), scatter_dimension=0, tiled=True),
        lax.psum_scatter(d_out_bias, ("dp", "seq"), scatter_dimension=0, tiled=True),
        lax.psum_scatter(d_gain1, ("dp", "seq"), scatter_dimension=0, tiled=True),
        lax.psum_scatter(d_shift1, ("dp", "seq"), scatter_dimension=0, tiled=True),
        lax.psum_scatter(d_wup, ("dp", "seq"), scatter_dimension=0, tiled=True),
        lax.psum_scatter(d_up_bias, ("dp", "seq"), scatter_dimension=0, tiled=True),
        lax.psum_scatter(d_wdown, ("dp", "seq"), scatter_dimension=0, tiled=True),
        lax.psum_scatter(d_down_bias, ("dp", "seq"), scatter_dimension=0, tiled=True),
        lax.psum_scatter(d_gain2, ("dp", "seq"), scatter_dimension=0, tiled=True),
        lax.psum_scatter(d_shift2, ("dp", "seq"), scatter_dimension=0, tiled=True),
    )
    return (
        hidden_out,
        in_grad,
        summed[0],
        summed[1],
        summed[2],
        rel_table_grad,
        summed[3],
        summed[4],
        summed[5],
        summed[6],
        summed[7],
        summed[8],
        summed[9],
        summed[10],
        summed[11],
        summed[12],
        summed[13],
        summed[14],
        summed[15],
    )


def solution(mesh):
    placed = (
        P(("dp", "seq"), None),
        P("dp"),
        P(("dp", "seq"), None),
        P(("dp", "seq")),
        P(("dp", "seq")),
        P(("dp", "seq"), None),
        P(("dp", "seq"), None),
        P(("dp", "seq"), None),
        P(("dp", "seq")),
        P(("dp", "seq"), None),
        P(("dp", "seq")),
        P(("dp", "seq")),
        P(("dp", "seq")),
        P(("dp", "seq"), None),
        P(("dp", "seq")),
        P(("dp", "seq"), None),
        P(("dp", "seq")),
        P(("dp", "seq")),
        P(("dp", "seq")),
        P(("dp", "seq"), None),
    )
    return jax.shard_map(
        head_split if dict(mesh.shape) == {"dp": 16, "seq": 2} else row_split,
        mesh=mesh,
        in_specs=placed,
        out_specs=(
            P(("dp", "seq"), None),
            P(("dp", "seq"), None),
            P(("dp", "seq"), None),
            P(("dp", "seq")),
            P(("dp", "seq")),
            P(("dp", "seq"), None),
            P(("dp", "seq"), None),
            P(("dp", "seq"), None),
            P(("dp", "seq")),
            P(("dp", "seq"), None),
            P(("dp", "seq")),
            P(("dp", "seq")),
            P(("dp", "seq")),
            P(("dp", "seq"), None),
            P(("dp", "seq")),
            P(("dp", "seq"), None),
            P(("dp", "seq")),
            P(("dp", "seq")),
            P(("dp", "seq")),
        ),
        check_vma=False,
    )
```

profile of v0, /device:TPU:0, one launch (start us, length us, event | category | flops | bytes accessed | tf_op | source)
XLA Modules:
  0.0 372.7 jit_solution(2438687535953890849)
XLA Ops:
  8.5 5.0 %collective-permute-start.1 = (bf16[2,24,2304]{2,1,0:T(8,128)(2,1)S(1)}, bf16[2,24,2304]{2,1,0:T(8,128)(2,1)S(1)}, u32[]{:S(2)}, u32[]{:S(2)}) collective-permute-start(bf16[2,24,2304]{2,1,0:T(8,128)(2,1)S(1)} %pad_maximum_fusion.44), channel_id=1, source_target_pairs={{0,8},{2,10},{4,12},{6,14},{8,16},{10,18},{12,20},{14,22},{16,24},... | collective-permute-start | bytes 663560 | tf_op jit(solution)/shard_map/ppermute | solution.py:392
  24.5 6.2 %collective-permute-done.5 = bf16[2,24,2304]{2,1,0:T(8,128)(2,1)S(1)} collective-permute-done((bf16[2,24,2304]{2,1,0:T(8,128)(2,1)S(1)}, bf16[2,24,2304]{2,1,0:T(8,128)(2,1)S(1)}, u32[]{:S(2)}, u32[]{:S(2)}) %collective-permute-start.5) | collective-permute-done | bytes 221216 | tf_op jit(solution)/shard_map/ppermute | solution.py:392
  32.2 6.3 %collective-permute-done.6 = bf16[2,24,2304]{2,1,0:T(8,128)(2,1)S(1)} collective-permute-done((bf16[2,24,2304]{2,1,0:T(8,128)(2,1)S(1)}, bf16[2,24,2304]{2,1,0:T(8,128)(2,1)S(1)}, u32[]{:S(2)}, u32[]{:S(2)}) %collective-permute-start.6) | collective-permute-done | bytes 221216 | tf_op jit(solution)/shard_map/ppermute | solution.py:392
  46.2 6.8 %collective-permute-done.9 = bf16[4,24,2304]{2,1,0:T(8,128)(2,1)S(1)} collective-permute-done((bf16[4,24,2304]{2,1,0:T(8,128)(2,1)S(1)}, bf16[4,24,2304]{2,1,0:T(8,128)(2,1)S(1)}, u32[]{:S(2)}, u32[]{:S(2)}) %collective-permute-start.9) | collective-permute-done | bytes 442400 | tf_op jit(solution)/shard_map/ppermute | solution.py:372
  59.2 26.6 %collective-permute-done.11 = bf16[2,2,24,3456]{3,2,1,0:T(8,128)(2,1)} collective-permute-done((bf16[2,2,24,3456]{3,2,1,0:T(8,128)(2,1)S(1)}, bf16[2,2,24,3456]{3,2,1,0:T(8,128)(2,1)}, u32[]{:S(2)}, u32[]{:S(2)}) %collective-permute-start.11) | collective-permute-done | bytes 663584 | tf_op jit(solution)/shard_map/ppermute | solution.py:372
  104.0 5.1 %attention_forward.6 = (bf16[1024,128]{1,0:T(8,128)(2,1)S(1)}, bf16[1024,1024]{1,0:T(8,128)(2,1)S(1)}) custom-call(s32[1]{0:T(128)S(6)} %copy.205.prefix_ref, bf16[1024,1152]{1,0:T(8,128)(2,1)S(1)} %add_convert_fusion.q_ref.k_ref.v_ref, bf16[1024,1152]{1,0:T(8,128)(2,1)S(1)} %add_convert_fusion.q_ref.k_ref.v_ref, ...), custom_call_target="tpu_custom_call" | custom-call | flops 1000000000 | bytes 3145728 | tf_op jit(solution)/shard_map/attention_forward/pallas_call | solution.py:189
  110.5 5.3 %attention_forward.7 = (bf16[1024,128]{1,0:T(8,128)(2,1)S(1)}, bf16[1024,1024]{1,0:T(8,128)(2,1)S(1)}) custom-call(s32[1]{0:T(128)S(6)} %copy.205.prefix_ref, bf16[1024,1152]{1,0:T(8,128)(2,1)S(1)} %add_convert_fusion.q_ref.k_ref.v_ref, bf16[1024,1152]{1,0:T(8,128)(2,1)S(1)} %add_convert_fusion.q_ref.k_ref.v_ref, ...), custom_call_target="tpu_custom_call" | custom-call | flops 1000000000 | bytes 3145728 | tf_op jit(solution)/shard_map/attention_forward/pallas_call | solution.py:189
  124.9 5.1 %attention_forward.10 = (bf16[1024,128]{1,0:T(8,128)(2,1)S(1)}, bf16[1024,1024]{1,0:T(8,128)(2,1)S(1)}) custom-call(s32[1]{0:T(128)S(6)} %copy.205.prefix_ref, bf16[1024,1152]{1,0:T(8,128)(2,1)S(1)} %add_convert_fusion.q_ref.k_ref.v_ref, bf16[1024,1152]{1,0:T(8,128)(2,1)S(1)} %add_convert_fusion.q_ref.k_ref.v_ref, ...), custom_call_target="tpu_custom_call" | custom-call | flops 1000000000 | bytes 3145728 | tf_op jit(solution)/shard_map/attention_forward/pallas_call | solution.py:189
  130.0 5.6 %attention_forward.8 = (bf16[1024,128]{1,0:T(8,128)(2,1)S(1)}, bf16[1024,1024]{1,0:T(8,128)(2,1)S(1)}) custom-call(s32[1]{0:T(128)S(6)} %copy.205.prefix_ref, bf16[1024,1152]{1,0:T(8,128)(2,1)S(1)} %add_convert_fusion.q_ref.k_ref.v_ref, bf16[1024,1152]{1,0:T(8,128)(2,1)S(1)} %add_convert_fusion.q_ref.k_ref.v_ref, ...), custom_call_target="tpu_custom_call" | custom-call | flops 1000000000 | bytes 3145728 | tf_op jit(solution)/shard_map/attention_forward/pallas_call | solution.py:189
  135.6 5.1 %attention_forward.11 = (bf16[1024,128]{1,0:T(8,128)(2,1)S(1)}, bf16[1024,1024]{1,0:T(8,128)(2,1)S(1)}) custom-call(s32[1]{0:T(128)S(6)} %copy.205.prefix_ref, bf16[1024,1152]{1,0:T(8,128)(2,1)S(1)} %add_convert_fusion.q_ref.k_ref.v_ref, bf16[1024,1152]{1,0:T(8,128)(2,1)S(1)} %add_convert_fusion.q_ref.k_ref.v_ref, ...), custom_call_target="tpu_custom_call" | custom-call | flops 1000000000 | bytes 3145728 | tf_op jit(solution)/shard_map/attention_forward/pallas_call | solution.py:189
  140.8 11.5 %collective-permute-done.18 = bf16[2,4,24,3456]{3,2,0,1:T(8,128)(2,1)} collective-permute-done((bf16[2,4,24,3456]{3,2,0,1:T(8,128)(2,1)}, bf16[2,4,24,3456]{3,2,0,1:T(8,128)(2,1)}, u32[]{:S(2)}, u32[]{:S(2)}) %collective-permute-start.18) | collective-permute-done | bytes 1327136 | tf_op jit(solution)/shard_map/ppermute | solution.py:372
  156.1 5.1 %attention_forward.9 = (bf16[1024,128]{1,0:T(8,128)(2,1)S(1)}, bf16[1024,1024]{1,0:T(8,128)(2,1)S(1)}) custom-call(s32[1]{0:T(128)S(6)} %copy.205.prefix_ref, bf16[1024,1152]{1,0:T(8,128)(2,1)S(1)} %add_convert_fusion.q_ref.k_ref.v_ref, bf16[1024,1152]{1,0:T(8,128)(2,1)S(1)} %add_convert_fusion.q_ref.k_ref.v_ref, ...), custom_call_target="tpu_custom_call" | custom-call | flops 1000000000 | bytes 3145728 | tf_op jit(solution)/shard_map/attention_forward/pallas_call | solution.py:189
  169.4 5.5 %multiply_convert_fusion.1 = (bf16[1024,1536]{1,0:T(8,128)(2,1)S(1)}, f32[1024,1536]{1,0:T(8,128)}) fusion(f32[1536]{0:T(1024)S(1)} %fusion.54, bf16[768,1536]{1,0:T(8,128)(2,1)S(1)} %bitcast.416, bf16[512,768]{1,0:T(8,128)(2,1)S(1)} %get-tuple-element.252, bf16[512,768]{1,0:T(8,128)(2,1)S(1)} %get-tuple-element.251), kind=kOutput, calls=%fused_computation.7 | convolution fusion | flops 2428502016 | bytes 13375488 | tf_op jit(solution)/shard_map/dot_general | solution.py:36
  186.2 6.8 %fusion.252 = (bf16[1536]{0:T(1024)(128)(2,1)S(1)}, bf16[1024,1536]{1,0:T(8,128)(2,1)S(1)}) fusion(f32[1024,1536]{1,0:T(8,128)} %get-tuple-element.359, f32[1536]{0:T(1024)S(1)} %fusion.54, bf16[1536,768]{1,0:T(8,128)(2,1)S(1)} %bitcast.421, bf16[512,768]{1,0:T(8,128)(2,1)S(1)} %get-tuple-element.250, bf16[512,768]{1,0:T(8,128)(2,1)S(1)} %get-tuple-element.249), kind=kOutput, calls=%fused_computation.544 | convolution fusion | flops 2441083392 | bytes 13378560 | tf_op jit(solution)/shard_map/dot_general | solution.py:46
  216.2 9.1 %attention_backward.8 = (bf16[1024,128]{1,0:T(8,128)(2,1)S(1)}, bf16[1024,128]{1,0:T(8,128)(2,1)S(1)}, bf16[1024,128]{1,0:T(8,128)(2,1)S(1)}, f32[64,768]{1,0:T(8,128)S(1)}, f32[64,768]{1,0:T(8,128)S(1)}) custom-call(bf16[1024,1152]{1,0:T(8,128)(2,1)S(1)} %add_convert_fusion.q_ref.k_ref.v_ref, bf16[1024,1152]{1,0:T(8,128)(2,1)S(1)} %add_convert_fusion.q_ref.k_ref.v_ref, ...), custom_call_target="tpu_custom_call" | custom-call | flops 2000000000 | bytes 4194304 | tf_op jit(solution)/shard_map/attention_backward/pallas_call | solution.py:331
  225.4 9.3 %attention_backward.6 = (bf16[1024,128]{1,0:T(8,128)(2,1)S(1)}, bf16[1024,128]{1,0:T(8,128)(2,1)S(1)}, bf16[1024,128]{1,0:T(8,128)(2,1)S(1)}, f32[64,768]{1,0:T(8,128)S(1)}, f32[64,768]{1,0:T(8,128)S(1)}) custom-call(bf16[1024,1152]{1,0:T(8,128)(2,1)S(1)} %add_convert_fusion.q_ref.k_ref.v_ref, bf16[1024,1152]{1,0:T(8,128)(2,1)S(1)} %add_convert_fusion.q_ref.k_ref.v_ref, ...), custom_call_target="tpu_custom_call" | custom-call | flops 2000000000 | bytes 4194304 | tf_op jit(solution)/shard_map/attention_backward/pallas_call | solution.py:331
  234.6 9.5 %attention_backward.7 = (bf16[1024,128]{1,0:T(8,128)(2,1)S(1)}, bf16[1024,128]{1,0:T(8,128)(2,1)S(1)}, bf16[1024,128]{1,0:T(8,128)(2,1)S(1)}, f32[64,768]{1,0:T(8,128)S(1)}, f32[64,768]{1,0:T(8,128)S(1)}) custom-call(bf16[1024,1152]{1,0:T(8,128)(2,1)S(1)} %add_convert_fusion.q_ref.k_ref.v_ref, bf16[1024,1152]{1,0:T(8,128)(2,1)S(1)} %add_convert_fusion.q_ref.k_ref.v_ref, ...), custom_call_target="tpu_custom_call" | custom-call | flops 2000000000 | bytes 4194304 | tf_op jit(solution)/shard_map/attention_backward/pallas_call | solution.py:331
  249.3 9.1 %attention_backward.10 = (bf16[1024,128]{1,0:T(8,128)(2,1)S(1)}, bf16[1024,128]{1,0:T(8,128)(2,1)S(1)}, bf16[1024,128]{1,0:T(8,128)(2,1)S(1)}, f32[64,768]{1,0:T(8,128)S(1)}, f32[64,768]{1,0:T(8,128)S(1)}) custom-call(bf16[1024,1152]{1,0:T(8,128)(2,1)S(1)} %add_convert_fusion.q_ref.k_ref.v_ref, bf16[1024,1152]{1,0:T(8,128)(2,1)S(1)} %add_convert_fusion.q_ref.k_ref.v_ref, ...), custom_call_target="tpu_custom_call" | custom-call | flops 2000000000 | bytes 4194304 | tf_op jit(solution)/shard_map/attention_backward/pallas_call | solution.py:331
  258.5 9.3 %attention_backward.9 = (bf16[1024,128]{1,0:T(8,128)(2,1)S(1)}, bf16[1024,128]{1,0:T(8,128)(2,1)S(1)}, bf16[1024,128]{1,0:T(8,128)(2,1)S(1)}, f32[64,768]{1,0:T(8,128)S(1)}, f32[64,768]{1,0:T(8,128)S(1)}) custom-call(bf16[1024,1152]{1,0:T(8,128)(2,1)S(1)} %add_convert_fusion.q_ref.k_ref.v_ref, bf16[1024,1152]{1,0:T(8,128)(2,1)S(1)} %add_convert_fusion.q_ref.k_ref.v_ref, ...), custom_call_target="tpu_custom_call" | custom-call | flops 2000000000 | bytes 4194304 | tf_op jit(solution)/shard_map/attention_backward/pallas_call | solution.py:331
  270.7 9.1 %attention_backward.11 = (bf16[1024,128]{1,0:T(8,128)(2,1)S(1)}, bf16[1024,128]{1,0:T(8,128)(2,1)S(1)}, bf16[1024,128]{1,0:T(8,128)(2,1)S(1)}, f32[64,768]{1,0:T(8,128)S(1)}, f32[64,768]{1,0:T(8,128)S(1)}) custom-call(bf16[1024,1152]{1,0:T(8,128)(2,1)S(1)} %add_convert_fusion.q_ref.k_ref.v_ref, bf16[1024,1152]{1,0:T(8,128)(2,1)S(1)} %add_convert_fusion.q_ref.k_ref.v_ref, ...), custom_call_target="tpu_custom_call" | custom-call | flops 2000000000 | bytes 4194304 | tf_op jit(solution)/shard_map/attention_backward/pallas_call | solution.py:331
  308.8 13.0 %collective-permute-done.35 = bf16[4,2,24,2304]{3,2,0,1:T(8,128)(2,1)S(1)} collective-permute-done((bf16[4,2,24,2304]{3,2,0,1:T(8,128)(2,1)S(1)}, bf16[4,2,24,2304]{3,2,0,1:T(8,128)(2,1)S(1)}, u32[]{:S(2)}, u32[]{:S(2)}) %collective-permute-start.35) | collective-permute-done | bytes 884768 | tf_op jit(solution)/shard_map/ppermute | solution.py:372
  328.9 4.6 %collective-permute-done.36 = bf16[4,24,2304]{2,1,0:T(8,128)(2,1)S(1)} collective-permute-done((bf16[4,24,2304]{2,1,0:T(8,128)(2,1)S(1)}, bf16[4,24,2304]{2,1,0:T(8,128)(2,1)S(1)}, u32[]{:S(2)}, u32[]{:S(2)}) %collective-permute-start.36) | collective-permute-done | bytes 442400 | tf_op jit(solution)/shard_map/ppermute | solution.py:372
  349.8 9.8 %collective-permute-start.47 = (bf16[2,24,2304]{2,1,0:T(8,128)(2,1)S(1)}, bf16[2,24,2304]{2,1,0:T(8,128)(2,1)S(1)}, u32[]{:S(2)}, u32[]{:S(2)}) collective-permute-start(bf16[2,24,2304]{2,1,0:T(8,128)(2,1)S(1)} %get-tuple-element.269), channel_id=1, source_target_pairs={{0,8},{2,10},{4,12},{6,14},{8,16},{10,18},{12,20},{14,22},{16,24},... | collective-permute-start | bytes 663560 | tf_op jit(solution)/shard_map/ppermute | solution.py:476
  363.0 4.4 %collective-permute-done.50 = bf16[2,24,2304]{2,1,0:T(8,128)(2,1)S(1)} collective-permute-done((bf16[2,24,2304]{2,1,0:T(8,128)(2,1)S(1)}, bf16[2,24,2304]{2,1,0:T(8,128)(2,1)S(1)}, u32[]{:S(2)}, u32[]{:S(2)}) %collective-permute-start.50) | collective-permute-done | bytes 221216 | tf_op jit(solution)/shard_map/ppermute | solution.py:477
  (460 shorter events, 175.5 us)
Async XLA Ops:
  8.3 15.4 %collective-permute-start.7 = (bf16[24,1920]{1,0:T(8,128)(2,1)S(1)}, bf16[24,1920]{1,0:T(8,128)(2,1)S(1)}, u32[]{:S(2)}, u32[]{:S(2)}) collective-permute-start(bf16[24,1920]{1,0:T(8,128)(2,1)S(1)} %broadcast_select_fusion.17), channel_id=1, source_target_pairs={{0,1},{1,0},{2,3},{3,2},{4,5},{5,4},{6,7},{7,6},{8,9},{9,8},{10,11... | collective-permute-start | bytes 276488 | tf_op jit(solution)/shard_map/ppermute | solution.py:352
  39.8 15.0 %collective-permute-start.12 = (bf16[512,768]{1,0:T(8,128)(2,1)S(1)}, bf16[512,768]{1,0:T(8,128)(2,1)}, u32[]{:S(2)}, u32[]{:S(2)}) collective-permute-start(bf16[512,768]{1,0:T(8,128)(2,1)S(1)} %copy-done.9), channel_id=1, source_target_pairs={{0,1},{1,0},{2,3},{3,2},{4,5},{5,4},{6,7},{7,6},{8,9},{9,8},{10,11... | collective-permute-start | bytes 2359304 | tf_op jit(solution)/shard_map/ppermute | solution.py:352
  40.4 12.6 %collective-permute-start.9 = (bf16[4,24,2304]{2,1,0:T(8,128)(2,1)S(1)}, bf16[4,24,2304]{2,1,0:T(8,128)(2,1)S(1)}, u32[]{:S(2)}, u32[]{:S(2)}) collective-permute-start(bf16[4,24,2304]{2,1,0:T(8,128)(2,1)S(1)} %pad_maximum_fusion.40), channel_id=1, source_target_pairs={{0,4},{2,6},{4,0},{6,2},{8,12},{10,14},{12,8},{14,10},{16,20},{18,... | collective-permute-start | bytes 1327112 | tf_op jit(solution)/shard_map/ppermute | solution.py:372
  41.9 12.3 %collective-permute-start.8 = (bf16[4,24,2304]{2,1,0:T(8,128)(2,1)S(1)}, bf16[4,24,2304]{2,1,0:T(8,128)(2,1)S(1)}, u32[]{:S(2)}, u32[]{:S(2)}) collective-permute-start(bf16[4,24,2304]{2,1,0:T(8,128)(2,1)S(1)} %pad_maximum_fusion.39), channel_id=1, source_target_pairs={{0,2},{2,0},{4,6},{6,4},{8,10},{10,8},{12,14},{14,12},{16,18},{18,... | collective-permute-start | bytes 1327112 | tf_op jit(solution)/shard_map/ppermute | solution.py:372
  54.4 31.5 %collective-permute-start.11 = (bf16[2,2,24,3456]{3,2,1,0:T(8,128)(2,1)S(1)}, bf16[2,2,24,3456]{3,2,1,0:T(8,128)(2,1)}, u32[]{:S(2)}, u32[]{:S(2)}) collective-permute-start(bf16[2,2,24,3456]{3,2,1,0:T(8,128)(2,1)S(1)} %pad_maximum_fusion.28), channel_id=1, source_target_pairs={{0,16},{2,18},{4,20},{6,22},{8,24},{10,26},{12,28},{14,30},{16,0},... | collective-permute-start | bytes 1990664 | tf_op jit(solution)/shard_map/ppermute | solution.py:372
  57.2 31.1 %collective-permute-start.13 = (bf16[2,4,24,2304]{3,2,1,0:T(8,128)(2,1)S(1)}, bf16[2,4,24,2304]{3,2,1,0:T(8,128)(2,1)S(1)}, u32[]{:S(2)}, u32[]{:S(2)}) collective-permute-start(bf16[2,4,24,2304]{3,2,1,0:T(8,128)(2,1)S(1)} %pad_maximum_fusion.23), channel_id=1, source_target_pairs={{0,4},{2,6},{4,0},{6,2},{8,12},{10,14},{12,8},{14,10},{16,20},{18,... | collective-permute-start | bytes 2654216 | tf_op jit(solution)/shard_map/ppermute | solution.py:372
  57.7 30.8 %collective-permute-start.14 = (bf16[2,4,24,2304]{3,2,1,0:T(8,128)(2,1)S(1)}, bf16[2,4,24,2304]{3,2,1,0:T(8,128)(2,1)S(1)}, u32[]{:S(2)}, u32[]{:S(2)}) collective-permute-start(bf16[2,4,24,2304]{3,2,1,0:T(8,128)(2,1)S(1)} %pad_maximum_fusion.24), channel_id=1, source_target_pairs={{0,2},{2,0},{4,6},{6,4},{8,10},{10,8},{12,14},{14,12},{16,18},{18,... | collective-permute-start | bytes 2654216 | tf_op jit(solution)/shard_map/ppermute | solution.py:372
  101.0 17.6 %collective-permute-start.17 = (bf16[4,24,3456]{2,1,0:T(8,128)(2,1)}, bf16[4,24,3456]{2,1,0:T(8,128)(2,1)S(1)}, u32[]{:S(2)}, u32[]{:S(2)}) collective-permute-start(bf16[4,24,3456]{2,1,0:T(8,128)(2,1)} %bitcast.414), channel_id=1, source_target_pairs={{0,4},{2,6},{4,0},{6,2},{8,12},{10,14},{12,8},{14,10},{16,20},{18,... | collective-permute-start | bytes 1990664 | tf_op jit(solution)/shard_map/ppermute | solution.py:372
  102.5 17.5 %collective-permute-start.16 = (bf16[4,24,3456]{2,1,0:T(8,128)(2,1)}, bf16[4,24,3456]{2,1,0:T(8,128)(2,1)S(1)}, u32[]{:S(2)}, u32[]{:S(2)}) collective-permute-start(bf16[4,24,3456]{2,1,0:T(8,128)(2,1)} %bitcast.412), channel_id=1, source_target_pairs={{0,2},{2,0},{4,6},{6,4},{8,10},{10,8},{12,14},{14,12},{16,18},{18,... | collective-permute-start | bytes 1990664 | tf_op jit(solution)/shard_map/ppermute | solution.py:372
  121.3 31.0 %collective-permute-start.18 = (bf16[2,4,24,3456]{3,2,0,1:T(8,128)(2,1)}, bf16[2,4,24,3456]{3,2,0,1:T(8,128)(2,1)}, u32[]{:S(2)}, u32[]{:S(2)}) collective-permute-start(bf16[2,4,24,3456]{3,2,0,1:T(8,128)(2,1)} %pad_maximum_fusion.9), channel_id=1, source_target_pairs={{0,4},{2,6},{4,0},{6,2},{8,12},{10,14},{12,8},{14,10},{16,20},{18,... | collective-permute-start | bytes 3981320 | tf_op jit(solution)/shard_map/ppermute | solution.py:372
  123.3 31.0 %collective-permute-start.19 = (bf16[2,4,24,3456]{3,2,0,1:T(8,128)(2,1)}, bf16[2,4,24,3456]{3,2,0,1:T(8,128)(2,1)S(1)}, u32[]{:S(2)}, u32[]{:S(2)}) collective-permute-start(bf16[2,4,24,3456]{3,2,0,1:T(8,128)(2,1)} %pad_maximum_fusion.10), channel_id=1, source_target_pairs={{0,2},{2,0},{4,6},{6,4},{8,10},{10,8},{12,14},{14,12},{16,18},{18,... | collective-permute-start | bytes 3981320 | tf_op jit(solution)/shard_map/ppermute | solution.py:372
  213.4 31.5 %collective-permute-start.29 = (bf16[4,2,24,3456]{3,2,0,1:T(8,128)(2,1)S(1)}, bf16[4,2,24,3456]{3,2,0,1:T(8,128)(2,1)S(1)}, u32[]{:S(2)}, u32[]{:S(2)}) collective-permute-start(bf16[4,2,24,3456]{3,2,0,1:T(8,128)(2,1)S(1)} %select_bitcast_fusion), channel_id=1, source_target_pairs={{0,4},{2,6},{4,0},{6,2},{8,12},{10,14},{12,8},{14,10},{16,20},{18,... | collective-permute-start | bytes 3981320 | tf_op jit(solution)/shard_map/ppermute | solution.py:372
  214.7 31.2 %collective-permute-start.28 = (bf16[4,2,24,3456]{3,2,0,1:T(8,128)(2,1)S(1)}, bf16[4,2,24,3456]{3,2,0,1:T(8,128)(2,1)S(1)}, u32[]{:S(2)}, u32[]{:S(2)}) collective-permute-start(bf16[4,2,24,3456]{3,2,0,1:T(8,128)(2,1)S(1)} %fusion.44), channel_id=1, source_target_pairs={{0,2},{2,0},{4,6},{6,4},{8,10},{10,8},{12,14},{14,12},{16,18},{18,... | collective-permute-start | bytes 3981320 | tf_op jit(solution)/shard_map/ppermute | solution.py:372
  246.4 21.4 %collective-permute-start.30 = (bf16[4,24,3456]{2,1,0:T(8,128)(2,1)S(1)}, bf16[4,24,3456]{2,1,0:T(8,128)(2,1)S(1)}, u32[]{:S(2)}, u32[]{:S(2)}) collective-permute-start(bf16[4,24,3456]{2,1,0:T(8,128)(2,1)S(1)} %select_bitcast_fusion.11), channel_id=1, source_target_pairs={{0,4},{2,6},{4,0},{6,2},{8,12},{10,14},{12,8},{14,10},{16,20},{18,... | collective-permute-start | bytes 1990664 | tf_op jit(solution)/shard_map/ppermute | solution.py:372
  247.8 20.3 %collective-permute-start.31 = (bf16[4,24,3456]{2,1,0:T(8,128)(2,1)S(1)}, bf16[4,24,3456]{2,1,0:T(8,128)(2,1)S(1)}, u32[]{:S(2)}, u32[]{:S(2)}) collective-permute-start(bf16[4,24,3456]{2,1,0:T(8,128)(2,1)S(1)} %select_bitcast_fusion.10), channel_id=1, source_target_pairs={{0,2},{2,0},{4,6},{6,4},{8,10},{10,8},{12,14},{14,12},{16,18},{18,... | collective-permute-start | bytes 1990664 | tf_op jit(solution)/shard_map/ppermute | solution.py:372
  268.6 11.3 %collective-permute-start.32 = (bf16[2,24,3456]{2,1,0:T(8,128)(2,1)S(1)}, bf16[2,24,3456]{2,1,0:T(8,128)(2,1)S(1)}, u32[]{:S(2)}, u32[]{:S(2)}) collective-permute-start(bf16[2,24,3456]{2,1,0:T(8,128)(2,1)S(1)} %get-tuple-element.260), channel_id=1, source_target_pairs={{0,8},{2,10},{4,12},{6,14},{1,9},{3,11},{5,13},{7,15}} | collective-permute-start | bytes 995336 | tf_op jit(solution)/shard_map/ppermute | solution.py:476
  289.2 15.1 %collective-permute-start.39 = (bf16[2,24,3456]{2,1,0:T(8,128)(2,1)S(1)}, bf16[2,24,3456]{2,1,0:T(8,128)(2,1)S(1)}, u32[]{:S(2)}, u32[]{:S(2)}) collective-permute-start(bf16[2,24,3456]{2,1,0:T(8,128)(2,1)S(1)} %get-tuple-element.258), channel_id=1, source_target_pairs={{0,8},{2,10},{4,12},{6,14},{8,16},{10,18},{12,20},{14,22},{1,9},{3... | collective-permute-start | bytes 995336 | tf_op jit(solution)/shard_map/ppermute | solution.py:476
  290.7 13.5 %collective-permute-start.40 = (bf16[2,24,3456]{2,1,0:T(8,128)(2,1)S(1)}, bf16[2,24,3456]{2,1,0:T(8,128)(2,1)S(1)}, u32[]{:S(2)}, u32[]{:S(2)}) collective-permute-start(bf16[2,24,3456]{2,1,0:T(8,128)(2,1)S(1)} %get-tuple-element.257), channel_id=1, source_target_pairs={{16,8},{18,10},{20,12},{22,14},{24,16},{26,18},{28,20},{30,22},{17... | collective-permute-start | bytes 995336 | tf_op jit(solution)/shard_map/ppermute | solution.py:477
  300.2 21.6 %collective-permute-start.35 = (bf16[4,2,24,2304]{3,2,0,1:T(8,128)(2,1)S(1)}, bf16[4,2,24,2304]{3,2,0,1:T(8,128)(2,1)S(1)}, u32[]{:S(2)}, u32[]{:S(2)}) collective-permute-start(bf16[4,2,24,2304]{3,2,0,1:T(8,128)(2,1)S(1)} %fusion.84), channel_id=1, source_target_pairs={{0,2},{2,0},{4,6},{6,4},{8,10},{10,8},{12,14},{14,12},{16,18},{18,... | collective-permute-start | bytes 2654216 | tf_op jit(solution)/shard_map/ppermute | solution.py:372
  300.9 22.2 %collective-permute-start.37 = (bf16[4,2,24,2304]{3,2,0,1:T(8,128)(2,1)S(1)}, bf16[4,2,24,2304]{3,2,0,1:T(8,128)(2,1)S(1)}, u32[]{:S(2)}, u32[]{:S(2)}) collective-permute-start(bf16[4,2,24,2304]{3,2,0,1:T(8,128)(2,1)S(1)} %select_bitcast_fusion.5), channel_id=1, source_target_pairs={{0,4},{2,6},{4,0},{6,2},{8,12},{10,14},{12,8},{14,10},{16,20},{18,... | collective-permute-start | bytes 2654216 | tf_op jit(solution)/shard_map/ppermute | solution.py:372
  304.6 19.6 %collective-permute-start.42 = (bf16[2,24,3456]{2,1,0:T(8,128)(2,1)S(1)}, bf16[2,24,3456]{2,1,0:T(8,128)(2,1)S(1)}, u32[]{:S(2)}, u32[]{:S(2)}) collective-permute-start(bf16[2,24,3456]{2,1,0:T(8,128)(2,1)S(1)} %get-tuple-element.255), channel_id=1, source_target_pairs={{0,8},{2,10},{4,12},{6,14},{8,16},{10,18},{12,20},{14,22},{16,24},... | collective-permute-start | bytes 995336 | tf_op jit(solution)/shard_map/ppermute | solution.py:476
  307.5 16.7 %collective-permute-start.43 = (bf16[2,24,3456]{2,1,0:T(8,128)(2,1)S(1)}, bf16[2,24,3456]{2,1,0:T(8,128)(2,1)S(1)}, u32[]{:S(2)}, u32[]{:S(2)}) collective-permute-start(bf16[2,24,3456]{2,1,0:T(8,128)(2,1)S(1)} %get-tuple-element.256), channel_id=1, source_target_pairs={{8,0},{10,2},{12,4},{14,6},{16,8},{18,10},{20,12},{22,14},{24,16},... | collective-permute-start | bytes 995336 | tf_op jit(solution)/shard_map/ppermute | solution.py:477
  322.2 11.3 %collective-permute-start.36 = (bf16[4,24,2304]{2,1,0:T(8,128)(2,1)S(1)}, bf16[4,24,2304]{2,1,0:T(8,128)(2,1)S(1)}, u32[]{:S(2)}, u32[]{:S(2)}) collective-permute-start(bf16[4,24,2304]{2,1,0:T(8,128)(2,1)S(1)} %select_bitcast_fusion.19), channel_id=1, source_target_pairs={{0,4},{2,6},{4,0},{6,2},{8,12},{10,14},{12,8},{14,10},{16,20},{18,... | collective-permute-start | bytes 1327112 | tf_op jit(solution)/shard_map/ppermute | solution.py:372
  349.8 13.3 %collective-permute-start.47 = (bf16[2,24,2304]{2,1,0:T(8,128)(2,1)S(1)}, bf16[2,24,2304]{2,1,0:T(8,128)(2,1)S(1)}, u32[]{:S(2)}, u32[]{:S(2)}) collective-permute-start(bf16[2,24,2304]{2,1,0:T(8,128)(2,1)S(1)} %get-tuple-element.269), channel_id=1, source_target_pairs={{0,8},{2,10},{4,12},{6,14},{8,16},{10,18},{12,20},{14,22},{16,24},... | collective-permute-start | bytes 663560 | tf_op jit(solution)/shard_map/ppermute | solution.py:476
  (86 other events, 425.6 us)
where the time goes:
time: 377 us; the launch traced here: 373 us
  waiting for transfers between devices  110 us (29%)
  Pallas kernels  86.8 us (23%)
  starting transfers between devices  61.3 us (16%)
  matrix products  46.9 us (12%)
  other arithmetic  35.7 us (9%)
  local copies, waits for them, and re-layouts  28.4 us (8%)
  between operations  3.91 us (1%)
    ppermute x18, waiting for transfers between devices, exchange(): return lax.ppermute(value, 'dp', [(i, i ^ mask) for i in range(16)])  71 us
    pallas_call x6, Pallas kernels, attention_backward(): pl.pallas_call(functools.partial(backward_body, head), grid=(1,), in_spec...  55.4 us
    pallas_call x6, Pallas kernels, attention_forward(): pl.pallas_call(functools.partial(forward_body, head), grid=(1,), in_specs...  31.4 us
    ppermute x6, starting transfers between devices, line(): up = lax.ppermute(to_above.astype(value.dtype), 'dp', ups)  23.3 us
    ppermute x18, starting transfers between devices, exchange(): return lax.ppermute(value, 'dp', [(i, i ^ mask) for i in range(16)])  18.7 us
    dot_general x9, matrix products, inner_last(): lax.dot_general(left, right, (((1,), (1,)), ((), ())), preferred_element_...  17.3 us
    dot_general x8, matrix products, product(): return jnp.dot(left, right, preferred_element_type=jnp.float32)  16.3 us
    ppermute x3, waiting for transfers between devices, line(): lax.ppermute(above[-1], 'dp', down)  15.9 us
  transfers between devices with their start and end apart: 52, of which 26 were waited for; matrix products, arithmetic and copies ran while one was open for 14% of the time, Pallas kernels for 23%

commit v1 on v0

--- a/solution.py
+++ b/solution.py
@@ -201,7 +201,7 @@
             pltpu.VMEM((length, BLOCK), jnp.float32),
         ],
         compiler_params=pltpu.CompilerParams(dimension_semantics=("arbitrary",), vmem_limit_bytes=24 << 20),
-        cost_estimate=pl.CostEstimate(flops=10**9, transcendentals=length * length, bytes_accessed=3 << 20),
+        cost_estimate=pl.CostEstimate(flops=2 * 10**9, transcendentals=length * length, bytes_accessed=3 << 20),
         name="attention_forward",
     )(prefix, merged, merged, merged, pos_band, pos_band, *found)
 
@@ -340,7 +340,7 @@
             pltpu.VMEM((length, PAIR), jnp.float32),
         ],
         compiler_params=pltpu.CompilerParams(dimension_semantics=("arbitrary",), vmem_limit_bytes=24 << 20),
-        cost_estimate=pl.CostEstimate(flops=2 * 10**9, transcendentals=0, bytes_accessed=4 << 20),
+        cost_estimate=pl.CostEstimate(flops=4 * 10**9, transcendentals=0, bytes_accessed=4 << 20),
         name="attention_backward",
     )(merged, merged, merged, dctx, probs, pos_band, pos_band, *found)
 
@@ -404,29 +404,35 @@
             self.state = lines
 
     def double(self, step):
+        self.state = [(value, exchange(value, 4 * step)) for value in self.state]
+
+    def finish_double(self, step):
         z = chip_bits()[0]
         bit = z % 2 if step == 1 else z // 2
-        result = []
-        for value in self.state:
-            other = exchange(value, 4 * step)
-            result.append(jnp.stack([jnp.where(bit == 0, value, other), jnp.where(bit == 0, other, value)]))
+        result = [
+            jnp.stack([jnp.where(bit == 0, value, other), jnp.where(bit == 0, other, value)])
+            for value, other in self.state
+        ]
+        if step == 2:
+            result = [tuple(value[:, :, side].reshape((4,) + value.shape[3:]) for side in range(2)) for value in result]
         self.state = result
-        if step == 2:
-            self.state = [
-                tuple(value[:, :, side].reshape((4,) + value.shape[3:]) for side in range(2)) for value in result
-            ]
 
     def pair(self, step):
+        masks = (1, 2) if step == 1 else (2, 1)
+        self.state = [
+            tuple((value, exchange(value, mask)) for value, mask in zip(halves, masks)) for halves in self.state
+        ]
+
+    def finish_pair(self, step):
         _, y, x = chip_bits()
-        order = ((x, 1), (y, 2)) if step == 1 else ((y, 2), (x, 1))
-        lines = []
-        for halves in self.state:
-            result = []
-            for value, (bit, mask) in zip(halves, order):
-                other = exchange(value, mask)
-                result.append(jnp.stack([jnp.where(bit == 0, value, other), jnp.where(bit == 0, other, value)]))
-            lines.append(tuple(result))
-        self.state = lines
+        bits = (x, y) if step == 1 else (y, x)
+        self.state = [
+            tuple(
+                jnp.stack([jnp.where(bit == 0, value, other), jnp.where(bit == 0, other, value)])
+                for (value, other), bit in zip(halves, bits)
+            )
+            for halves in self.state
+        ]
 
     def rows(self, index, low, high):
         first, second = [half[..., low:high] for half in self.state[index]]
@@ -548,8 +554,11 @@
     early_chain.pair(1)
     late_chain.double(1)
     tie((early_chain, late_chain))
+    early_chain.finish_pair(1)
+    late_chain.finish_double(1)
     early_chain.pair(2)
     late_chain.double(2)
+    early_chain.finish_pair(2)
     hidden_all = ordered(core, hidden_in, hidden_got)
     w_qkv_own = early_chain.rows(0, 0, 3 * half)
     w_pos_own = early_chain.rows(0, 3 * half, 5 * half)
@@ -582,6 +591,7 @@
     qkv_shift = jnp.concatenate([half_of(core, qb, 0), jnp.zeros((half,), f32), half_of(core, vb, 0)])
     merged = (product(hidden_all, w_qkv_own) + qkv_shift).astype(bf)
     merged, pos_band = tie((late_chain,), (merged, pos_band))
+    late_chain.finish_double(2)
     late_chain.pair(1)
     context_parts, prob_parts = [], []
     for pair in range(half // PAIR):
@@ -591,8 +601,11 @@
         prob_parts.append(kept)
         if pair == 0:
             part, merged = tie((late_chain,), (part, merged))
+            late_chain.finish_pair(1)
             late_chain.pair(2)
         context_parts.append(part)
+    context_parts = tie((late_chain,), context_parts)
+    late_chain.finish_pair(2)
     context = jnp.concatenate(context_parts, axis=1)
     out_columns = late_chain.rows(0, 0, half)
     w_out_own = ordered(

time: 377 us -> 360 us (0.955)
  waiting for transfers between devices: 110 us -> 92.1 us
    ppermute x18, waiting for transfers between devices: 71 us -> 52.8 us  [exchange(): return lax.ppermute(value, 'dp', [(i, i ^ mask) for i in range(16)])]
    unnamed x136 -> x142, local copies, waits for them, and re-layouts: 12.3 us -> 12 us
  transfers between devices with their start and end apart: 52 -> 52, of which waited for: 26 -> 29; matrix products, arithmetic and copies ran while one was open for 14% -> 15% of each run, Pallas kernels for 23% -> 24%
where the time goes in v1:
time: 360 us; the launch traced here: 356 us
  waiting for transfers between devices  92.1 us (26%)
  Pallas kernels  86.8 us (24%)
  starting transfers between devices  58.4 us (16%)
  matrix products  46.9 us (13%)
  other arithmetic  39.4 us (11%)
  local copies, waits for them, and re-layouts  28.5 us (8%)
  between operations  3.84 us (1%)
    pallas_call x6, Pallas kernels, attention_backward(): pl.pallas_call(functools.partial(backward_body, head), grid=(1,), in_spec...  55.4 us
    ppermute x18, waiting for transfers between devices, exchange(): return lax.ppermute(value, 'dp', [(i, i ^ mask) for i in range(16)])  52.8 us
    pallas_call x6, Pallas kernels, attention_forward(): pl.pallas_call(functools.partial(forward_body, head), grid=(1,), in_specs...  31.4 us
    ppermute x6, starting transfers between devices, line(): up = lax.ppermute(to_above.astype(value.dtype), 'dp', ups)  22.6 us
    dot_general x9, matrix products, inner_last(): lax.dot_general(left, right, (((1,), (1,)), ((), ())), preferred_element_...  17.3 us
    ppermute x3, waiting for transfers between devices, line(): lax.ppermute(above[-1], 'dp', down)  16.4 us
    dot_general x8, matrix products, product(): return jnp.dot(left, right, preferred_element_type=jnp.float32)  16.3 us
    ppermute x18, starting transfers between devices, exchange(): return lax.ppermute(value, 'dp', [(i, i ^ mask) for i in range(16)])  15.7 us
  transfers between devices with their start and end apart: 52, of which 29 were waited for; matrix products, arithmetic and copies ran while one was open for 15% of the time, Pallas kernels for 24%

profile of v1, /device:TPU:0, one launch (start us, length us, event | category | flops | bytes accessed | tf_op | source)
XLA Modules:
  0.0 355.9 jit_solution(9819243049312380990)
XLA Ops:
  9.1 4.6 %collective-permute-start.1 = (bf16[2,24,2304]{2,1,0:T(8,128)(2,1)S(1)}, bf16[2,24,2304]{2,1,0:T(8,128)(2,1)S(1)}, u32[]{:S(2)}, u32[]{:S(2)}) collective-permute-start(bf16[2,24,2304]{2,1,0:T(8,128)(2,1)S(1)} %pad_maximum_fusion.44), channel_id=1, source_target_pairs={{0,8},{2,10},{4,12},{6,14},{8,16},{10,18},{12,20},{14,22},{16,24},... | collective-permute-start | bytes 663560 | tf_op jit(solution)/shard_map/ppermute | solution.py:392
  25.0 6.6 %collective-permute-done.5 = bf16[2,24,2304]{2,1,0:T(8,128)(2,1)S(1)} collective-permute-done((bf16[2,24,2304]{2,1,0:T(8,128)(2,1)S(1)}, bf16[2,24,2304]{2,1,0:T(8,128)(2,1)S(1)}, u32[]{:S(2)}, u32[]{:S(2)}) %collective-permute-start.5) | collective-permute-done | bytes 221216 | tf_op jit(solution)/shard_map/ppermute | solution.py:392
  33.1 6.3 %collective-permute-done.6 = bf16[2,24,2304]{2,1,0:T(8,128)(2,1)S(1)} collective-permute-done((bf16[2,24,2304]{2,1,0:T(8,128)(2,1)S(1)}, bf16[2,24,2304]{2,1,0:T(8,128)(2,1)S(1)}, u32[]{:S(2)}, u32[]{:S(2)}) %collective-permute-start.6) | collective-permute-done | bytes 221216 | tf_op jit(solution)/shard_map/ppermute | solution.py:392
  44.8 5.3 %collective-permute-done.10 = bf16[2,24,3456]{2,1,0:T(8,128)(2,1)} collective-permute-done((bf16[2,24,3456]{2,1,0:T(8,128)(2,1)S(1)}, bf16[2,24,3456]{2,1,0:T(8,128)(2,1)}, u32[]{:S(2)}, u32[]{:S(2)}) %collective-permute-start.10) | collective-permute-done | bytes 331808 | tf_op jit(solution)/shard_map/ppermute | solution.py:372
  56.0 13.7 %collective-permute-done.13 = bf16[2,4,24,2304]{3,2,1,0:T(8,128)(2,1)S(1)} collective-permute-done((bf16[2,4,24,2304]{3,2,1,0:T(8,128)(2,1)S(1)}, bf16[2,4,24,2304]{3,2,1,0:T(8,128)(2,1)S(1)}, u32[]{:S(2)}, u32[]{:S(2)}) %collective-permute-start.13) | collective-permute-done | bytes 884768 | tf_op jit(solution)/shard_map/ppermute | solution.py:372
  90.5 5.1 %attention_forward.6 = (bf16[1024,128]{1,0:T(8,128)(2,1)S(1)}, bf16[1024,1024]{1,0:T(8,128)(2,1)S(1)}) custom-call(s32[1]{0:T(128)S(6)} %copy.205.prefix_ref, bf16[1024,1152]{1,0:T(8,128)(2,1)S(1)} %add_convert_fusion.q_ref.k_ref.v_ref, bf16[1024,1152]{1,0:T(8,128)(2,1)S(1)} %add_convert_fusion.q_ref.k_ref.v_ref, ...), custom_call_target="tpu_custom_call" | custom-call | flops 2000000000 | bytes 3145728 | tf_op jit(solution)/shard_map/attention_forward/pallas_call | solution.py:189
  96.9 5.3 %attention_forward.7 = (bf16[1024,128]{1,0:T(8,128)(2,1)S(1)}, bf16[1024,1024]{1,0:T(8,128)(2,1)S(1)}) custom-call(s32[1]{0:T(128)S(6)} %copy.205.prefix_ref, bf16[1024,1152]{1,0:T(8,128)(2,1)S(1)} %add_convert_fusion.q_ref.k_ref.v_ref, bf16[1024,1152]{1,0:T(8,128)(2,1)S(1)} %add_convert_fusion.q_ref.k_ref.v_ref, ...), custom_call_target="tpu_custom_call" | custom-call | flops 2000000000 | bytes 3145728 | tf_op jit(solution)/shard_map/attention_forward/pallas_call | solution.py:189
  111.9 5.1 %attention_forward.10 = (bf16[1024,128]{1,0:T(8,128)(2,1)S(1)}, bf16[1024,1024]{1,0:T(8,128)(2,1)S(1)}) custom-call(s32[1]{0:T(128)S(6)} %copy.205.prefix_ref, bf16[1024,1152]{1,0:T(8,128)(2,1)S(1)} %add_convert_fusion.q_ref.k_ref.v_ref, bf16[1024,1152]{1,0:T(8,128)(2,1)S(1)} %add_convert_fusion.q_ref.k_ref.v_ref, ...), custom_call_target="tpu_custom_call" | custom-call | flops 2000000000 | bytes 3145728 | tf_op jit(solution)/shard_map/attention_forward/pallas_call | solution.py:189
  117.0 5.1 %attention_forward.8 = (bf16[1024,128]{1,0:T(8,128)(2,1)S(1)}, bf16[1024,1024]{1,0:T(8,128)(2,1)S(1)}) custom-call(s32[1]{0:T(128)S(6)} %copy.205.prefix_ref, bf16[1024,1152]{1,0:T(8,128)(2,1)S(1)} %add_convert_fusion.q_ref.k_ref.v_ref, bf16[1024,1152]{1,0:T(8,128)(2,1)S(1)} %add_convert_fusion.q_ref.k_ref.v_ref, ...), custom_call_target="tpu_custom_call" | custom-call | flops 2000000000 | bytes 3145728 | tf_op jit(solution)/shard_map/attention_forward/pallas_call | solution.py:189
  122.1 5.6 %attention_forward.11 = (bf16[1024,128]{1,0:T(8,128)(2,1)S(1)}, bf16[1024,1024]{1,0:T(8,128)(2,1)S(1)}) custom-call(s32[1]{0:T(128)S(6)} %copy.205.prefix_ref, bf16[1024,1152]{1,0:T(8,128)(2,1)S(1)} %add_convert_fusion.q_ref.k_ref.v_ref, bf16[1024,1152]{1,0:T(8,128)(2,1)S(1)} %add_convert_fusion.q_ref.k_ref.v_ref, ...), custom_call_target="tpu_custom_call" | custom-call | flops 2000000000 | bytes 3145728 | tf_op jit(solution)/shard_map/attention_forward/pallas_call | solution.py:189
  127.7 5.1 %attention_forward.9 = (bf16[1024,128]{1,0:T(8,128)(2,1)S(1)}, bf16[1024,1024]{1,0:T(8,128)(2,1)S(1)}) custom-call(s32[1]{0:T(128)S(6)} %copy.205.prefix_ref, bf16[1024,1152]{1,0:T(8,128)(2,1)S(1)} %add_convert_fusion.q_ref.k_ref.v_ref, bf16[1024,1152]{1,0:T(8,128)(2,1)S(1)} %add_convert_fusion.q_ref.k_ref.v_ref, ...), custom_call_target="tpu_custom_call" | custom-call | flops 2000000000 | bytes 3145728 | tf_op jit(solution)/shard_map/attention_forward/pallas_call | solution.py:189
  132.9 5.5 %collective-permute-done.19 = bf16[2,4,24,3456]{3,2,0,1:T(8,128)(2,1)} collective-permute-done((bf16[2,4,24,3456]{3,2,0,1:T(8,128)(2,1)}, bf16[2,4,24,3456]{3,2,0,1:T(8,128)(2,1)}, u32[]{:S(2)}, u32[]{:S(2)}) %collective-permute-start.19) | collective-permute-done | bytes 1327136 | tf_op jit(solution)/shard_map/ppermute | solution.py:372
  154.2 5.5 %multiply_convert_fusion.1 = (bf16[1024,1536]{1,0:T(8,128)(2,1)S(1)}, f32[1024,1536]{1,0:T(8,128)}) fusion(f32[1536]{0:T(1024)S(1)} %fusion.54, bf16[768,1536]{1,0:T(8,128)(2,1)S(1)} %bitcast.416, bf16[512,768]{1,0:T(8,128)(2,1)S(1)} %get-tuple-element.276, bf16[512,768]{1,0:T(8,128)(2,1)S(1)} %get-tuple-element.275), kind=kOutput, calls=%fused_computation.7 | convolution fusion | flops 2428502016 | bytes 13375488 | tf_op jit(solution)/shard_map/dot_general | solution.py:36
  171.0 6.8 %fusion.252 = (bf16[1536]{0:T(1024)(128)(2,1)S(1)}, bf16[1024,1536]{1,0:T(8,128)(2,1)S(1)}) fusion(f32[1024,1536]{1,0:T(8,128)} %get-tuple-element.383, f32[1536]{0:T(1024)S(1)} %fusion.54, bf16[1536,768]{1,0:T(8,128)(2,1)S(1)} %bitcast.421, bf16[512,768]{1,0:T(8,128)(2,1)S(1)} %get-tuple-element.274, bf16[512,768]{1,0:T(8,128)(2,1)S(1)} %get-tuple-element.273), kind=kOutput, calls=%fused_computation.544 | convolution fusion | flops 2441083392 | bytes 13378560 | tf_op jit(solution)/shard_map/dot_general | solution.py:46
  199.5 9.1 %attention_backward.6 = (bf16[1024,128]{1,0:T(8,128)(2,1)S(1)}, bf16[1024,128]{1,0:T(8,128)(2,1)S(1)}, bf16[1024,128]{1,0:T(8,128)(2,1)S(1)}, f32[64,768]{1,0:T(8,128)S(1)}, f32[64,768]{1,0:T(8,128)S(1)}) custom-call(bf16[1024,1152]{1,0:T(8,128)(2,1)S(1)} %add_convert_fusion.q_ref.k_ref.v_ref, bf16[1024,1152]{1,0:T(8,128)(2,1)S(1)} %add_convert_fusion.q_ref.k_ref.v_ref, ...), custom_call_target="tpu_custom_call" | custom-call | flops 4000000000 | bytes 4194304 | tf_op jit(solution)/shard_map/attention_backward/pallas_call | solution.py:331
  208.7 9.3 %attention_backward.7 = (bf16[1024,128]{1,0:T(8,128)(2,1)S(1)}, bf16[1024,128]{1,0:T(8,128)(2,1)S(1)}, bf16[1024,128]{1,0:T(8,128)(2,1)S(1)}, f32[64,768]{1,0:T(8,128)S(1)}, f32[64,768]{1,0:T(8,128)S(1)}) custom-call(bf16[1024,1152]{1,0:T(8,128)(2,1)S(1)} %add_convert_fusion.q_ref.k_ref.v_ref, bf16[1024,1152]{1,0:T(8,128)(2,1)S(1)} %add_convert_fusion.q_ref.k_ref.v_ref, ...), custom_call_target="tpu_custom_call" | custom-call | flops 4000000000 | bytes 4194304 | tf_op jit(solution)/shard_map/attention_backward/pallas_call | solution.py:331
  218.0 9.5 %attention_backward.8 = (bf16[1024,128]{1,0:T(8,128)(2,1)S(1)}, bf16[1024,128]{1,0:T(8,128)(2,1)S(1)}, bf16[1024,128]{1,0:T(8,128)(2,1)S(1)}, f32[64,768]{1,0:T(8,128)S(1)}, f32[64,768]{1,0:T(8,128)S(1)}) custom-call(bf16[1024,1152]{1,0:T(8,128)(2,1)S(1)} %add_convert_fusion.q_ref.k_ref.v_ref, bf16[1024,1152]{1,0:T(8,128)(2,1)S(1)} %add_convert_fusion.q_ref.k_ref.v_ref, ...), custom_call_target="tpu_custom_call" | custom-call | flops 4000000000 | bytes 4194304 | tf_op jit(solution)/shard_map/attention_backward/pallas_call | solution.py:331
  232.6 9.1 %attention_backward.9 = (bf16[1024,128]{1,0:T(8,128)(2,1)S(1)}, bf16[1024,128]{1,0:T(8,128)(2,1)S(1)}, bf16[1024,128]{1,0:T(8,128)(2,1)S(1)}, f32[64,768]{1,0:T(8,128)S(1)}, f32[64,768]{1,0:T(8,128)S(1)}) custom-call(bf16[1024,1152]{1,0:T(8,128)(2,1)S(1)} %add_convert_fusion.q_ref.k_ref.v_ref, bf16[1024,1152]{1,0:T(8,128)(2,1)S(1)} %add_convert_fusion.q_ref.k_ref.v_ref, ...), custom_call_target="tpu_custom_call" | custom-call | flops 4000000000 | bytes 4194304 | tf_op jit(solution)/shard_map/attention_backward/pallas_call | solution.py:331
  241.8 9.3 %attention_backward.10 = (bf16[1024,128]{1,0:T(8,128)(2,1)S(1)}, bf16[1024,128]{1,0:T(8,128)(2,1)S(1)}, bf16[1024,128]{1,0:T(8,128)(2,1)S(1)}, f32[64,768]{1,0:T(8,128)S(1)}, f32[64,768]{1,0:T(8,128)S(1)}) custom-call(bf16[1024,1152]{1,0:T(8,128)(2,1)S(1)} %add_convert_fusion.q_ref.k_ref.v_ref, bf16[1024,1152]{1,0:T(8,128)(2,1)S(1)} %add_convert_fusion.q_ref.k_ref.v_ref, ...), custom_call_target="tpu_custom_call" | custom-call | flops 4000000000 | bytes 4194304 | tf_op jit(solution)/shard_map/attention_backward/pallas_call | solution.py:331
  254.7 9.1 %attention_backward.11 = (bf16[1024,128]{1,0:T(8,128)(2,1)S(1)}, bf16[1024,128]{1,0:T(8,128)(2,1)S(1)}, bf16[1024,128]{1,0:T(8,128)(2,1)S(1)}, f32[64,768]{1,0:T(8,128)S(1)}, f32[64,768]{1,0:T(8,128)S(1)}) custom-call(bf16[1024,1152]{1,0:T(8,128)(2,1)S(1)} %add_convert_fusion.q_ref.k_ref.v_ref, bf16[1024,1152]{1,0:T(8,128)(2,1)S(1)} %add_convert_fusion.q_ref.k_ref.v_ref, ...), custom_call_target="tpu_custom_call" | custom-call | flops 4000000000 | bytes 4194304 | tf_op jit(solution)/shard_map/attention_backward/pallas_call | solution.py:331
  292.9 12.9 %collective-permute-done.35 = bf16[4,2,24,2304]{3,2,0,1:T(8,128)(2,1)S(1)} collective-permute-done((bf16[4,2,24,2304]{3,2,0,1:T(8,128)(2,1)S(1)}, bf16[4,2,24,2304]{3,2,0,1:T(8,128)(2,1)S(1)}, u32[]{:S(2)}, u32[]{:S(2)}) %collective-permute-start.35) | collective-permute-done | bytes 884768 | tf_op jit(solution)/shard_map/ppermute | solution.py:372
  325.0 4.4 %collective-permute-start.46 = (bf16[2,24,2304]{2,1,0:T(8,128)(2,1)S(1)}, bf16[2,24,2304]{2,1,0:T(8,128)(2,1)S(1)}, u32[]{:S(2)}, u32[]{:S(2)}) collective-permute-start(bf16[2,24,2304]{2,1,0:T(8,128)(2,1)S(1)} %get-tuple-element.295), channel_id=1, source_target_pairs={{0,8},{2,10},{4,12},{6,14},{8,16},{10,18},{12,20},{14,22},{1,9},{3... | collective-permute-start | bytes 663560 | tf_op jit(solution)/shard_map/ppermute | solution.py:482
  333.0 9.9 %collective-permute-start.47 = (bf16[2,24,2304]{2,1,0:T(8,128)(2,1)S(1)}, bf16[2,24,2304]{2,1,0:T(8,128)(2,1)S(1)}, u32[]{:S(2)}, u32[]{:S(2)}) collective-permute-start(bf16[2,24,2304]{2,1,0:T(8,128)(2,1)S(1)} %get-tuple-element.293), channel_id=1, source_target_pairs={{0,8},{2,10},{4,12},{6,14},{8,16},{10,18},{12,20},{14,22},{16,24},... | collective-permute-start | bytes 663560 | tf_op jit(solution)/shard_map/ppermute | solution.py:482
  346.3 4.4 %collective-permute-done.50 = bf16[2,24,2304]{2,1,0:T(8,128)(2,1)S(1)} collective-permute-done((bf16[2,24,2304]{2,1,0:T(8,128)(2,1)S(1)}, bf16[2,24,2304]{2,1,0:T(8,128)(2,1)S(1)}, u32[]{:S(2)}, u32[]{:S(2)}) %collective-permute-start.50) | collective-permute-done | bytes 221216 | tf_op jit(solution)/shard_map/ppermute | solution.py:483
  (466 shorter events, 179.4 us)
Async XLA Ops:
  8.4 15.9 %collective-permute-start.7 = (bf16[24,1920]{1,0:T(8,128)(2,1)S(1)}, bf16[24,1920]{1,0:T(8,128)(2,1)S(1)}, u32[]{:S(2)}, u32[]{:S(2)}) collective-permute-start(bf16[24,1920]{1,0:T(8,128)(2,1)S(1)} %broadcast_select_fusion.17), channel_id=1, source_target_pairs={{0,1},{1,0},{2,3},{3,2},{4,5},{5,4},{6,7},{7,6},{8,9},{9,8},{10,11... | collective-permute-start | bytes 276488 | tf_op jit(solution)/shard_map/ppermute | solution.py:352
  8.4 35.1 %collective-permute-start.12 = (bf16[512,768]{1,0:T(8,128)(2,1)S(1)}, bf16[512,768]{1,0:T(8,128)(2,1)S(1)}, u32[]{:S(2)}, u32[]{:S(2)}) collective-permute-start(bf16[512,768]{1,0:T(8,128)(2,1)S(1)} %copy-done.14), channel_id=1, source_target_pairs={{0,1},{1,0},{2,3},{3,2},{4,5},{5,4},{6,7},{7,6},{8,9},{9,8},{10,11... | collective-permute-start | bytes 2359304 | tf_op jit(solution)/shard_map/ppermute | solution.py:352
  51.7 18.0 %collective-permute-start.13 = (bf16[2,4,24,2304]{3,2,1,0:T(8,128)(2,1)S(1)}, bf16[2,4,24,2304]{3,2,1,0:T(8,128)(2,1)S(1)}, u32[]{:S(2)}, u32[]{:S(2)}) collective-permute-start(bf16[2,4,24,2304]{3,2,1,0:T(8,128)(2,1)S(1)} %pad_maximum_fusion.23), channel_id=1, source_target_pairs={{0,4},{2,6},{4,0},{6,2},{8,12},{10,14},{12,8},{14,10},{16,20},{18,... | collective-permute-start | bytes 2654216 | tf_op jit(solution)/shard_map/ppermute | solution.py:372
  53.5 17.7 %collective-permute-start.14 = (bf16[2,4,24,2304]{3,2,1,0:T(8,128)(2,1)S(1)}, bf16[2,4,24,2304]{3,2,1,0:T(8,128)(2,1)S(1)}, u32[]{:S(2)}, u32[]{:S(2)}) collective-permute-start(bf16[2,4,24,2304]{3,2,1,0:T(8,128)(2,1)S(1)} %pad_maximum_fusion.24), channel_id=1, source_target_pairs={{0,2},{2,0},{4,6},{6,4},{8,10},{10,8},{12,14},{14,12},{16,18},{18,... | collective-permute-start | bytes 2654216 | tf_op jit(solution)/shard_map/ppermute | solution.py:372
  56.0 31.1 %collective-permute-start.11 = (bf16[2,2,24,3456]{3,2,1,0:T(8,128)(2,1)}, bf16[2,2,24,3456]{3,2,1,0:T(8,128)(2,1)}, u32[]{:S(2)}, u32[]{:S(2)}) collective-permute-start(bf16[2,2,24,3456]{3,2,1,0:T(8,128)(2,1)} %pad_maximum_fusion.28), channel_id=1, source_target_pairs={{0,16},{2,18},{4,20},{6,22},{8,24},{10,26},{12,28},{14,30},{16,0},... | collective-permute-start | bytes 1990664 | tf_op jit(solution)/shard_map/ppermute | solution.py:372
  88.7 17.4 %collective-permute-start.16 = (bf16[4,24,3456]{2,1,0:T(8,128)(2,1)S(1)}, bf16[4,24,3456]{2,1,0:T(8,128)(2,1)S(1)}, u32[]{:S(2)}, u32[]{:S(2)}) collective-permute-start(bf16[4,24,3456]{2,1,0:T(8,128)(2,1)S(1)} %bitcast.412), channel_id=1, source_target_pairs={{0,2},{2,0},{4,6},{6,4},{8,10},{10,8},{12,14},{14,12},{16,18},{18,... | collective-permute-start | bytes 1990664 | tf_op jit(solution)/shard_map/ppermute | solution.py:372
  89.3 17.0 %collective-permute-start.17 = (bf16[4,24,3456]{2,1,0:T(8,128)(2,1)S(1)}, bf16[4,24,3456]{2,1,0:T(8,128)(2,1)S(1)}, u32[]{:S(2)}, u32[]{:S(2)}) collective-permute-start(bf16[4,24,3456]{2,1,0:T(8,128)(2,1)S(1)} %bitcast.414), channel_id=1, source_target_pairs={{0,4},{2,6},{4,0},{6,2},{8,12},{10,14},{12,8},{14,10},{16,20},{18,... | collective-permute-start | bytes 1990664 | tf_op jit(solution)/shard_map/ppermute | solution.py:372
  107.7 30.7 %collective-permute-start.19 = (bf16[2,4,24,3456]{3,2,0,1:T(8,128)(2,1)}, bf16[2,4,24,3456]{3,2,0,1:T(8,128)(2,1)}, u32[]{:S(2)}, u32[]{:S(2)}) collective-permute-start(bf16[2,4,24,3456]{3,2,0,1:T(8,128)(2,1)} %pad_maximum_fusion.10), channel_id=1, source_target_pairs={{0,2},{2,0},{4,6},{6,4},{8,10},{10,8},{12,14},{14,12},{16,18},{18,... | collective-permute-start | bytes 3981320 | tf_op jit(solution)/shard_map/ppermute | solution.py:372
  110.5 30.4 %collective-permute-start.18 = (bf16[2,4,24,3456]{3,2,0,1:T(8,128)(2,1)}, bf16[2,4,24,3456]{3,2,0,1:T(8,128)(2,1)}, u32[]{:S(2)}, u32[]{:S(2)}) collective-permute-start(bf16[2,4,24,3456]{3,2,0,1:T(8,128)(2,1)} %pad_maximum_fusion.9), channel_id=1, source_target_pairs={{0,4},{2,6},{4,0},{6,2},{8,12},{10,14},{12,8},{14,10},{16,20},{18,... | collective-permute-start | bytes 3981320 | tf_op jit(solution)/shard_map/ppermute | solution.py:372
  197.9 31.2 %collective-permute-start.29 = (bf16[4,2,24,3456]{3,2,0,1:T(8,128)(2,1)S(1)}, bf16[4,2,24,3456]{3,2,0,1:T(8,128)(2,1)S(1)}, u32[]{:S(2)}, u32[]{:S(2)}) collective-permute-start(bf16[4,2,24,3456]{3,2,0,1:T(8,128)(2,1)S(1)} %select_bitcast_fusion), channel_id=1, source_target_pairs={{0,4},{2,6},{4,0},{6,2},{8,12},{10,14},{12,8},{14,10},{16,20},{18,... | collective-permute-start | bytes 3981320 | tf_op jit(solution)/shard_map/ppermute | solution.py:372
  198.8 30.9 %collective-permute-start.28 = (bf16[4,2,24,3456]{3,2,0,1:T(8,128)(2,1)S(1)}, bf16[4,2,24,3456]{3,2,0,1:T(8,128)(2,1)S(1)}, u32[]{:S(2)}, u32[]{:S(2)}) collective-permute-start(bf16[4,2,24,3456]{3,2,0,1:T(8,128)(2,1)S(1)} %fusion.44), channel_id=1, source_target_pairs={{0,2},{2,0},{4,6},{6,4},{8,10},{10,8},{12,14},{14,12},{16,18},{18,... | collective-permute-start | bytes 3981320 | tf_op jit(solution)/shard_map/ppermute | solution.py:372
  230.3 20.8 %collective-permute-start.30 = (bf16[4,24,3456]{2,1,0:T(8,128)(2,1)S(1)}, bf16[4,24,3456]{2,1,0:T(8,128)(2,1)S(1)}, u32[]{:S(2)}, u32[]{:S(2)}) collective-permute-start(bf16[4,24,3456]{2,1,0:T(8,128)(2,1)S(1)} %select_bitcast_fusion.11), channel_id=1, source_target_pairs={{0,4},{2,6},{4,0},{6,2},{8,12},{10,14},{12,8},{14,10},{16,20},{18,... | collective-permute-start | bytes 1990664 | tf_op jit(solution)/shard_map/ppermute | solution.py:372
  232.0 19.5 %collective-permute-start.31 = (bf16[4,24,3456]{2,1,0:T(8,128)(2,1)S(1)}, bf16[4,24,3456]{2,1,0:T(8,128)(2,1)S(1)}, u32[]{:S(2)}, u32[]{:S(2)}) collective-permute-start(bf16[4,24,3456]{2,1,0:T(8,128)(2,1)S(1)} %select_bitcast_fusion.10), channel_id=1, source_target_pairs={{0,2},{2,0},{4,6},{6,4},{8,10},{10,8},{12,14},{14,12},{16,18},{18,... | collective-permute-start | bytes 1990664 | tf_op jit(solution)/shard_map/ppermute | solution.py:372
  251.9 11.9 %collective-permute-start.32 = (bf16[2,24,3456]{2,1,0:T(8,128)(2,1)S(1)}, bf16[2,24,3456]{2,1,0:T(8,128)(2,1)S(1)}, u32[]{:S(2)}, u32[]{:S(2)}) collective-permute-start(bf16[2,24,3456]{2,1,0:T(8,128)(2,1)S(1)} %get-tuple-element.284), channel_id=1, source_target_pairs={{0,8},{2,10},{4,12},{6,14},{1,9},{3,11},{5,13},{7,15}} | collective-permute-start | bytes 995336 | tf_op jit(solution)/shard_map/ppermute | solution.py:482
  268.6 10.9 %collective-permute-start.34 = (bf16[512,384]{1,0:T(8,128)(2,1)}, bf16[512,384]{1,0:T(8,128)(2,1)S(1)}, u32[]{:S(2)}, u32[]{:S(2)}) collective-permute-start(bf16[512,384]{1,0:T(8,128)(2,1)} %constant_dynamic-slice_fusion), channel_id=1, source_target_pairs={{0,1},{1,0},{2,3},{3,2},{4,5},{5,4},{6,7},{7,6},{8,9},{9,8},{10,11... | collective-permute-start | bytes 1179656 | tf_op jit(solution)/shard_map/ppermute | solution.py:352
  273.2 15.6 %collective-permute-start.39 = (bf16[2,24,3456]{2,1,0:T(8,128)(2,1)S(1)}, bf16[2,24,3456]{2,1,0:T(8,128)(2,1)S(1)}, u32[]{:S(2)}, u32[]{:S(2)}) collective-permute-start(bf16[2,24,3456]{2,1,0:T(8,128)(2,1)S(1)} %get-tuple-element.282), channel_id=1, source_target_pairs={{0,8},{2,10},{4,12},{6,14},{8,16},{10,18},{12,20},{14,22},{1,9},{3... | collective-permute-start | bytes 995336 | tf_op jit(solution)/shard_map/ppermute | solution.py:482
  274.5 14.3 %collective-permute-start.40 = (bf16[2,24,3456]{2,1,0:T(8,128)(2,1)S(1)}, bf16[2,24,3456]{2,1,0:T(8,128)(2,1)S(1)}, u32[]{:S(2)}, u32[]{:S(2)}) collective-permute-start(bf16[2,24,3456]{2,1,0:T(8,128)(2,1)S(1)} %get-tuple-element.281), channel_id=1, source_target_pairs={{16,8},{18,10},{20,12},{22,14},{24,16},{26,18},{28,20},{30,22},{17... | collective-permute-start | bytes 995336 | tf_op jit(solution)/shard_map/ppermute | solution.py:483
  284.2 21.6 %collective-permute-start.35 = (bf16[4,2,24,2304]{3,2,0,1:T(8,128)(2,1)S(1)}, bf16[4,2,24,2304]{3,2,0,1:T(8,128)(2,1)S(1)}, u32[]{:S(2)}, u32[]{:S(2)}) collective-permute-start(bf16[4,2,24,2304]{3,2,0,1:T(8,128)(2,1)S(1)} %fusion.84), channel_id=1, source_target_pairs={{0,2},{2,0},{4,6},{6,4},{8,10},{10,8},{12,14},{14,12},{16,18},{18,... | collective-permute-start | bytes 2654216 | tf_op jit(solution)/shard_map/ppermute | solution.py:372
  285.8 21.4 %collective-permute-start.37 = (bf16[4,2,24,2304]{3,2,0,1:T(8,128)(2,1)S(1)}, bf16[4,2,24,2304]{3,2,0,1:T(8,128)(2,1)S(1)}, u32[]{:S(2)}, u32[]{:S(2)}) collective-permute-start(bf16[4,2,24,2304]{3,2,0,1:T(8,128)(2,1)S(1)} %select_bitcast_fusion.5), channel_id=1, source_target_pairs={{0,4},{2,6},{4,0},{6,2},{8,12},{10,14},{12,8},{14,10},{16,20},{18,... | collective-permute-start | bytes 2654216 | tf_op jit(solution)/shard_map/ppermute | solution.py:372
  289.1 19.6 %collective-permute-start.42 = (bf16[2,24,3456]{2,1,0:T(8,128)(2,1)S(1)}, bf16[2,24,3456]{2,1,0:T(8,128)(2,1)S(1)}, u32[]{:S(2)}, u32[]{:S(2)}) collective-permute-start(bf16[2,24,3456]{2,1,0:T(8,128)(2,1)S(1)} %get-tuple-element.279), channel_id=1, source_target_pairs={{0,8},{2,10},{4,12},{6,14},{8,16},{10,18},{12,20},{14,22},{16,24},... | collective-permute-start | bytes 995336 | tf_op jit(solution)/shard_map/ppermute | solution.py:482
  291.6 17.1 %collective-permute-start.43 = (bf16[2,24,3456]{2,1,0:T(8,128)(2,1)S(1)}, bf16[2,24,3456]{2,1,0:T(8,128)(2,1)S(1)}, u32[]{:S(2)}, u32[]{:S(2)}) collective-permute-start(bf16[2,24,3456]{2,1,0:T(8,128)(2,1)S(1)} %get-tuple-element.280), channel_id=1, source_target_pairs={{8,0},{10,2},{12,4},{14,6},{16,8},{18,10},{20,12},{22,14},{24,16},... | collective-permute-start | bytes 995336 | tf_op jit(solution)/shard_map/ppermute | solution.py:483
  306.2 11.3 %collective-permute-start.36 = (bf16[4,24,2304]{2,1,0:T(8,128)(2,1)S(1)}, bf16[4,24,2304]{2,1,0:T(8,128)(2,1)S(1)}, u32[]{:S(2)}, u32[]{:S(2)}) collective-permute-start(bf16[4,24,2304]{2,1,0:T(8,128)(2,1)S(1)} %select_bitcast_fusion.19), channel_id=1, source_target_pairs={{0,4},{2,6},{4,0},{6,2},{8,12},{10,14},{12,8},{14,10},{16,20},{18,... | collective-permute-start | bytes 1327112 | tf_op jit(solution)/shard_map/ppermute | solution.py:372
  307.5 11.0 %collective-permute-start.38 = (bf16[4,24,2304]{2,1,0:T(8,128)(2,1)S(1)}, bf16[4,24,2304]{2,1,0:T(8,128)(2,1)S(1)}, u32[]{:S(2)}, u32[]{:S(2)}) collective-permute-start(bf16[4,24,2304]{2,1,0:T(8,128)(2,1)S(1)} %select_bitcast_fusion.18), channel_id=1, source_target_pairs={{0,2},{2,0},{4,6},{6,4},{8,10},{10,8},{12,14},{14,12},{16,18},{18,... | collective-permute-start | bytes 1327112 | tf_op jit(solution)/shard_map/ppermute | solution.py:372
  333.0 13.3 %collective-permute-start.47 = (bf16[2,24,2304]{2,1,0:T(8,128)(2,1)S(1)}, bf16[2,24,2304]{2,1,0:T(8,128)(2,1)S(1)}, u32[]{:S(2)}, u32[]{:S(2)}) collective-permute-start(bf16[2,24,2304]{2,1,0:T(8,128)(2,1)S(1)} %get-tuple-element.293), channel_id=1, source_target_pairs={{0,8},{2,10},{4,12},{6,14},{8,16},{10,18},{12,20},{14,22},{16,24},... | collective-permute-start | bytes 663560 | tf_op jit(solution)/shard_map/ppermute | solution.py:482
  (89 other events, 490.5 us)

commit v2 on v1

--- a/solution.py
+++ b/solution.py
@@ -201,7 +201,7 @@
             pltpu.VMEM((length, BLOCK), jnp.float32),
         ],
         compiler_params=pltpu.CompilerParams(dimension_semantics=("arbitrary",), vmem_limit_bytes=24 << 20),
-        cost_estimate=pl.CostEstimate(flops=2 * 10**9, transcendentals=length * length, bytes_accessed=3 << 20),
+        cost_estimate=pl.CostEstimate(flops=3 * 10**8, transcendentals=0, bytes_accessed=3 << 20),
         name="attention_forward",
     )(prefix, merged, merged, merged, pos_band, pos_band, *found)
 
@@ -340,7 +340,7 @@
             pltpu.VMEM((length, PAIR), jnp.float32),
         ],
         compiler_params=pltpu.CompilerParams(dimension_semantics=("arbitrary",), vmem_limit_bytes=24 << 20),
-        cost_estimate=pl.CostEstimate(flops=4 * 10**9, transcendentals=0, bytes_accessed=4 << 20),
+        cost_estimate=pl.CostEstimate(flops=10**9, transcendentals=0, bytes_accessed=4 << 20),
         name="attention_backward",
     )(merged, merged, merged, dctx, probs, pos_band, pos_band, *found)
 
@@ -632,6 +632,7 @@
     slope = (
         normal_cdf + expanded * jnp.exp(-0.5 * expanded * expanded) * (1.0 / math.sqrt(2.0 * math.pi))
     ).astype(bf)
+    activated, slope = lax.optimization_barrier((activated, slope))
     residual2 = normed + summed_rows(activated, lambda part: product(part, w_down_own)) + db
     unit2, inverse2 = norm_parts(residual2)
     hidden_out = (unit2 * gain2 + shift2).astype(bf)
@@ -680,7 +681,6 @@
         found = attention_backward(merged, d_context, prob_parts[index], pos_band, index // 2, index % 2, tuple(found[:3]))
         grads.append(found)
     grads[-1] = tie((late_sums,), found)
-    late_sums.line(2)
     d_merged = jnp.concatenate([g[i] for i in range(3) for g in grads[1::2]], axis=1)
     d_q, d_v = d_merged[:, :half], d_merged[:, 2 * half :]
     d_wqkv = inner_first(hidden_all, d_merged).astype(bf)
@@ -726,6 +726,7 @@
     early_sums.pair(1)
     in_grad = d_res1 + summed_rows(d_merged, lambda part: inner_last(part, w_qkv_own))
     in_grad = tie((late_sums,), in_grad)
+    late_sums.line(2)
     late_sums.line(3)
     late_grads = late_sums.totals[0]
     down_grads = late_grads[:, :, half + ff_half :]
@@ -743,7 +744,6 @@
         joined.append(jnp.concatenate([late_left[:, cut], late_right[:, cut]], axis=1))
     joined = product(jnp.concatenate(joined, axis=0).astype(bf), unit_order)
     g_wup = jnp.concatenate([joined[g * rows : (g + 1) * rows] for g in range(ff_half // half)], axis=1)
-    g_wdown, g_wout, g_wup, in_grad = tie((early_sums,), (g_wdown, g_wout, g_wup, in_grad))
     for step in (1, 2, 3):
         early_sums.line(step)
     early_grads = early_sums.totals[0]

time: 360 us -> 358 us (level)
  waiting for transfers between devices: 92.1 us -> 84.5 us
  local copies, waits for them, and re-layouts: 28.5 us -> 35.9 us
    ppermute x18, waiting for transfers between devices: 52.8 us -> 44.8 us  [exchange(): return lax.ppermute(value, 'dp', [(i, i ^ mask) for i in range(16)])]
    unnamed x142 -> x170, local copies, waits for them, and re-layouts: 12 us -> 19 us
    ppermute x6, starting transfers between devices: 22.6 us -> 18.7 us  [line(): up = lax.ppermute(to_above.astype(value.dtype), 'dp', ups)]
  transfers between devices with their start and end apart: 52 -> 52, of which waited for: 29 -> 27; matrix products, arithmetic and copies ran while one was open for 15% -> 14% of each run, Pallas kernels for 24% -> 25%
where the time goes in v2:
time: 358 us; the launch traced here: 354 us
  Pallas kernels  86.8 us (24%)
  waiting for transfers between devices  84.5 us (24%)
  starting transfers between devices  57.6 us (16%)
  matrix products  46.7 us (13%)
  other arithmetic  38.2 us (11%)
  local copies, waits for them, and re-layouts  35.9 us (10%)
  between operations  3.84 us (1%)
    pallas_call x6, Pallas kernels, attention_backward(): pl.pallas_call(functools.partial(backward_body, head), grid=(1,), in_spec...  55.4 us
    ppermute x18, waiting for transfers between devices, exchange(): return lax.ppermute(value, 'dp', [(i, i ^ mask) for i in range(16)])  44.8 us
    pallas_call x6, Pallas kernels, attention_forward(): pl.pallas_call(functools.partial(forward_body, head), grid=(1,), in_specs...  31.4 us
    ppermute x18, starting transfers between devices, exchange(): return lax.ppermute(value, 'dp', [(i, i ^ mask) for i in range(16)])  19.2 us
    unnamed x170, local copies, waits for them, and re-layouts  19 us
    ppermute x6, starting transfers between devices, line(): up = lax.ppermute(to_above.astype(value.dtype), 'dp', ups)  18.7 us
    dot_general x8, matrix products, product(): return jnp.dot(left, right, preferred_element_type=jnp.float32)  17.3 us
    ppermute x3, waiting for transfers between devices, line(): lax.ppermute(above[-1], 'dp', down)  16.4 us
  transfers between devices with their start and end apart: 52, of which 27 were waited for; matrix products, arithmetic and copies ran while one was open for 14% of the time, Pallas kernels for 25%

profile of v2, /device:TPU:0, one launch (start us, length us, event | category | flops | bytes accessed | tf_op | source)
XLA Modules:
  0.0 353.5 jit_solution(8657482475775599395)
XLA Ops:
  9.1 4.6 %collective-permute-start.1 = (bf16[2,24,2304]{2,1,0:T(8,128)(2,1)S(1)}, bf16[2,24,2304]{2,1,0:T(8,128)(2,1)S(1)}, u32[]{:S(2)}, u32[]{:S(2)}) collective-permute-start(bf16[2,24,2304]{2,1,0:T(8,128)(2,1)S(1)} %pad_maximum_fusion.44), channel_id=1, source_target_pairs={{0,8},{2,10},{4,12},{6,14},{8,16},{10,18},{12,20},{14,22},{16,24},... | collective-permute-start | bytes 663560 | tf_op jit(solution)/shard_map/ppermute | solution.py:392
  25.1 6.6 %collective-permute-done.5 = bf16[2,24,2304]{2,1,0:T(8,128)(2,1)S(1)} collective-permute-done((bf16[2,24,2304]{2,1,0:T(8,128)(2,1)S(1)}, bf16[2,24,2304]{2,1,0:T(8,128)(2,1)S(1)}, u32[]{:S(2)}, u32[]{:S(2)}) %collective-permute-start.5) | collective-permute-done | bytes 221216 | tf_op jit(solution)/shard_map/ppermute | solution.py:392
  33.2 6.3 %collective-permute-done.6 = bf16[2,24,2304]{2,1,0:T(8,128)(2,1)S(1)} collective-permute-done((bf16[2,24,2304]{2,1,0:T(8,128)(2,1)S(1)}, bf16[2,24,2304]{2,1,0:T(8,128)(2,1)S(1)}, u32[]{:S(2)}, u32[]{:S(2)}) %collective-permute-start.6) | collective-permute-done | bytes 221216 | tf_op jit(solution)/shard_map/ppermute | solution.py:392
  44.8 5.4 %collective-permute-done.10 = bf16[2,24,3456]{2,1,0:T(8,128)(2,1)} collective-permute-done((bf16[2,24,3456]{2,1,0:T(8,128)(2,1)S(1)}, bf16[2,24,3456]{2,1,0:T(8,128)(2,1)}, u32[]{:S(2)}, u32[]{:S(2)}) %collective-permute-start.10) | collective-permute-done | bytes 331808 | tf_op jit(solution)/shard_map/ppermute | solution.py:372
  56.2 13.6 %collective-permute-done.14 = bf16[2,4,24,2304]{3,2,1,0:T(8,128)(2,1)S(1)} collective-permute-done((bf16[2,4,24,2304]{3,2,1,0:T(8,128)(2,1)S(1)}, bf16[2,4,24,2304]{3,2,1,0:T(8,128)(2,1)S(1)}, u32[]{:S(2)}, u32[]{:S(2)}) %collective-permute-start.14) | collective-permute-done | bytes 884768 | tf_op jit(solution)/shard_map/ppermute | solution.py:372
  92.6 5.1 %attention_forward.6 = (bf16[1024,128]{1,0:T(8,128)(2,1)S(1)}, bf16[1024,1024]{1,0:T(8,128)(2,1)S(1)}) custom-call(s32[1]{0:T(128)S(6)} %copy.205.prefix_ref, bf16[1024,1152]{1,0:T(8,128)(2,1)S(1)} %add_convert_fusion.q_ref.k_ref.v_ref, bf16[1024,1152]{1,0:T(8,128)(2,1)S(1)} %add_convert_fusion.q_ref.k_ref.v_ref, ...), custom_call_target="tpu_custom_call" | custom-call | flops 300000000 | bytes 3145728 | tf_op jit(solution)/shard_map/attention_forward/pallas_call | solution.py:189
  99.1 5.3 %attention_forward.7 = (bf16[1024,128]{1,0:T(8,128)(2,1)S(1)}, bf16[1024,1024]{1,0:T(8,128)(2,1)S(1)}) custom-call(s32[1]{0:T(128)S(6)} %copy.205.prefix_ref, bf16[1024,1152]{1,0:T(8,128)(2,1)S(1)} %add_convert_fusion.q_ref.k_ref.v_ref, bf16[1024,1152]{1,0:T(8,128)(2,1)S(1)} %add_convert_fusion.q_ref.k_ref.v_ref, ...), custom_call_target="tpu_custom_call" | custom-call | flops 300000000 | bytes 3145728 | tf_op jit(solution)/shard_map/attention_forward/pallas_call | solution.py:189
  112.0 5.1 %attention_forward.8 = (bf16[1024,128]{1,0:T(8,128)(2,1)S(1)}, bf16[1024,1024]{1,0:T(8,128)(2,1)S(1)}) custom-call(s32[1]{0:T(128)S(6)} %copy.205.prefix_ref, bf16[1024,1152]{1,0:T(8,128)(2,1)S(1)} %add_convert_fusion.q_ref.k_ref.v_ref, bf16[1024,1152]{1,0:T(8,128)(2,1)S(1)} %add_convert_fusion.q_ref.k_ref.v_ref, ...), custom_call_target="tpu_custom_call" | custom-call | flops 300000000 | bytes 3145728 | tf_op jit(solution)/shard_map/attention_forward/pallas_call | solution.py:189
  117.2 5.1 %attention_forward.10 = (bf16[1024,128]{1,0:T(8,128)(2,1)S(1)}, bf16[1024,1024]{1,0:T(8,128)(2,1)S(1)}) custom-call(s32[1]{0:T(128)S(6)} %copy.205.prefix_ref, bf16[1024,1152]{1,0:T(8,128)(2,1)S(1)} %add_convert_fusion.q_ref.k_ref.v_ref, bf16[1024,1152]{1,0:T(8,128)(2,1)S(1)} %add_convert_fusion.q_ref.k_ref.v_ref, ...), custom_call_target="tpu_custom_call" | custom-call | flops 300000000 | bytes 3145728 | tf_op jit(solution)/shard_map/attention_forward/pallas_call | solution.py:189
  122.3 5.6 %attention_forward.9 = (bf16[1024,128]{1,0:T(8,128)(2,1)S(1)}, bf16[1024,1024]{1,0:T(8,128)(2,1)S(1)}) custom-call(s32[1]{0:T(128)S(6)} %copy.205.prefix_ref, bf16[1024,1152]{1,0:T(8,128)(2,1)S(1)} %add_convert_fusion.q_ref.k_ref.v_ref, bf16[1024,1152]{1,0:T(8,128)(2,1)S(1)} %add_convert_fusion.q_ref.k_ref.v_ref, ...), custom_call_target="tpu_custom_call" | custom-call | flops 300000000 | bytes 3145728 | tf_op jit(solution)/shard_map/attention_forward/pallas_call | solution.py:189
  127.9 5.1 %attention_forward.11 = (bf16[1024,128]{1,0:T(8,128)(2,1)S(1)}, bf16[1024,1024]{1,0:T(8,128)(2,1)S(1)}) custom-call(s32[1]{0:T(128)S(6)} %copy.205.prefix_ref, bf16[1024,1152]{1,0:T(8,128)(2,1)S(1)} %add_convert_fusion.q_ref.k_ref.v_ref, bf16[1024,1152]{1,0:T(8,128)(2,1)S(1)} %add_convert_fusion.q_ref.k_ref.v_ref, ...), custom_call_target="tpu_custom_call" | custom-call | flops 300000000 | bytes 3145728 | tf_op jit(solution)/shard_map/attention_forward/pallas_call | solution.py:189
  152.1 6.5 %fusion.4 = (bf16[1024,1536]{1,0:T(8,128)(2,1)}, bf16[1024,1536]{1,0:T(8,128)(2,1)S(1)}) fusion(f32[1536]{0:T(1024)S(1)} %fusion.54, bf16[768,1536]{1,0:T(8,128)(2,1)S(1)} %bitcast.382, bf16[512,768]{1,0:T(8,128)(2,1)S(1)} %get-tuple-element.276, bf16[512,768]{1,0:T(8,128)(2,1)S(1)} %get-tuple-element.275), kind=kOutput, calls=%fused_computation.5 | convolution fusion | flops 2437939200 | bytes 10229760 | tf_op jit(solution)/shard_map/dot_general | solution.py:36
  170.0 4.4 %fusion.258 = (bf16[1536]{0:T(1024)(128)(2,1)S(1)}, bf16[1024,1536]{1,0:T(8,128)(2,1)S(1)}) fusion(bf16[1024,1536]{1,0:T(8,128)(2,1)} %get-tuple-element.151, bf16[1536,768]{1,0:T(8,128)(2,1)S(1)} %bitcast.387, bf16[512,768]{1,0:T(8,128)(2,1)S(1)} %get-tuple-element.274, bf16[512,768]{1,0:T(8,128)(2,1)S(1)} %get-tuple-element.273), kind=kOutput, calls=%fused_computation.548 | convolution fusion | flops 2425354752 | bytes 10226688 | tf_op jit(solution)/shard_map/dot_general | solution.py:46
  197.2 9.1 %attention_backward.9 = (bf16[1024,128]{1,0:T(8,128)(2,1)S(1)}, bf16[1024,128]{1,0:T(8,128)(2,1)S(1)}, bf16[1024,128]{1,0:T(8,128)(2,1)S(1)}, f32[64,768]{1,0:T(8,128)S(1)}, f32[64,768]{1,0:T(8,128)S(1)}) custom-call(bf16[1024,1152]{1,0:T(8,128)(2,1)S(1)} %add_convert_fusion.q_ref.k_ref.v_ref, bf16[1024,1152]{1,0:T(8,128)(2,1)S(1)} %add_convert_fusion.q_ref.k_ref.v_ref, ...), custom_call_target="tpu_custom_call" | custom-call | flops 1000000000 | bytes 4194304 | tf_op jit(solution)/shard_map/attention_backward/pallas_call | solution.py:331
  206.3 9.3 %attention_backward.10 = (bf16[1024,128]{1,0:T(8,128)(2,1)S(1)}, bf16[1024,128]{1,0:T(8,128)(2,1)S(1)}, bf16[1024,128]{1,0:T(8,128)(2,1)S(1)}, f32[64,768]{1,0:T(8,128)S(1)}, f32[64,768]{1,0:T(8,128)S(1)}) custom-call(bf16[1024,1152]{1,0:T(8,128)(2,1)S(1)} %add_convert_fusion.q_ref.k_ref.v_ref, bf16[1024,1152]{1,0:T(8,128)(2,1)S(1)} %add_convert_fusion.q_ref.k_ref.v_ref, ...), custom_call_target="tpu_custom_call" | custom-call | flops 1000000000 | bytes 4194304 | tf_op jit(solution)/shard_map/attention_backward/pallas_call | solution.py:331
  216.4 9.5 %attention_backward.6 = (bf16[1024,128]{1,0:T(8,128)(2,1)S(1)}, bf16[1024,128]{1,0:T(8,128)(2,1)S(1)}, bf16[1024,128]{1,0:T(8,128)(2,1)S(1)}, f32[64,768]{1,0:T(8,128)S(1)}, f32[64,768]{1,0:T(8,128)S(1)}) custom-call(bf16[1024,1152]{1,0:T(8,128)(2,1)S(1)} %add_convert_fusion.q_ref.k_ref.v_ref, bf16[1024,1152]{1,0:T(8,128)(2,1)S(1)} %add_convert_fusion.q_ref.k_ref.v_ref, ...), custom_call_target="tpu_custom_call" | custom-call | flops 1000000000 | bytes 4194304 | tf_op jit(solution)/shard_map/attention_backward/pallas_call | solution.py:331
  229.7 9.1 %attention_backward.7 = (bf16[1024,128]{1,0:T(8,128)(2,1)S(1)}, bf16[1024,128]{1,0:T(8,128)(2,1)S(1)}, bf16[1024,128]{1,0:T(8,128)(2,1)S(1)}, f32[64,768]{1,0:T(8,128)S(1)}, f32[64,768]{1,0:T(8,128)S(1)}) custom-call(bf16[1024,1152]{1,0:T(8,128)(2,1)S(1)} %add_convert_fusion.q_ref.k_ref.v_ref, bf16[1024,1152]{1,0:T(8,128)(2,1)S(1)} %add_convert_fusion.q_ref.k_ref.v_ref, ...), custom_call_target="tpu_custom_call" | custom-call | flops 1000000000 | bytes 4194304 | tf_op jit(solution)/shard_map/attention_backward/pallas_call | solution.py:331
  238.8 9.3 %attention_backward.11 = (bf16[1024,128]{1,0:T(8,128)(2,1)S(1)}, bf16[1024,128]{1,0:T(8,128)(2,1)S(1)}, bf16[1024,128]{1,0:T(8,128)(2,1)S(1)}, f32[64,768]{1,0:T(8,128)S(1)}, f32[64,768]{1,0:T(8,128)S(1)}) custom-call(bf16[1024,1152]{1,0:T(8,128)(2,1)S(1)} %add_convert_fusion.q_ref.k_ref.v_ref, bf16[1024,1152]{1,0:T(8,128)(2,1)S(1)} %add_convert_fusion.q_ref.k_ref.v_ref, ...), custom_call_target="tpu_custom_call" | custom-call | flops 1000000000 | bytes 4194304 | tf_op jit(solution)/shard_map/attention_backward/pallas_call | solution.py:331
  252.6 9.1 %attention_backward.8 = (bf16[1024,128]{1,0:T(8,128)(2,1)S(1)}, bf16[1024,128]{1,0:T(8,128)(2,1)S(1)}, bf16[1024,128]{1,0:T(8,128)(2,1)S(1)}, f32[64,768]{1,0:T(8,128)S(1)}, f32[64,768]{1,0:T(8,128)S(1)}) custom-call(bf16[1024,1152]{1,0:T(8,128)(2,1)S(1)} %add_convert_fusion.q_ref.k_ref.v_ref, bf16[1024,1152]{1,0:T(8,128)(2,1)S(1)} %add_convert_fusion.q_ref.k_ref.v_ref, ...), custom_call_target="tpu_custom_call" | custom-call | flops 1000000000 | bytes 4194304 | tf_op jit(solution)/shard_map/attention_backward/pallas_call | solution.py:331
  290.0 14.0 %collective-permute-done.38 = bf16[4,2,24,2304]{3,2,0,1:T(8,128)(2,1)S(1)} collective-permute-done((bf16[4,2,24,2304]{3,2,0,1:T(8,128)(2,1)S(1)}, bf16[4,2,24,2304]{3,2,0,1:T(8,128)(2,1)S(1)}, u32[]{:S(2)}, u32[]{:S(2)}) %collective-permute-start.38) | collective-permute-done | bytes 884768 | tf_op jit(solution)/shard_map/ppermute | solution.py:372
  309.1 4.6 %collective-permute-start.48 = (bf16[2,24,3456]{2,1,0:T(8,128)(2,1)S(1)}, bf16[2,24,3456]{2,1,0:T(8,128)(2,1)S(1)}, u32[]{:S(2)}, u32[]{:S(2)}) collective-permute-start(bf16[2,24,3456]{2,1,0:T(8,128)(2,1)S(1)} %get-tuple-element.279), channel_id=1, source_target_pairs={{0,8},{2,10},{4,12},{6,14},{8,16},{10,18},{12,20},{14,22},{16,24},... | collective-permute-start | bytes 995336 | tf_op jit(solution)/shard_map/ppermute | solution.py:482
  324.0 4.4 %collective-permute-start.41 = (bf16[2,24,2304]{2,1,0:T(8,128)(2,1)S(1)}, bf16[2,24,2304]{2,1,0:T(8,128)(2,1)S(1)}, u32[]{:S(2)}, u32[]{:S(2)}) collective-permute-start(bf16[2,24,2304]{2,1,0:T(8,128)(2,1)S(1)} %get-tuple-element.240), channel_id=1, source_target_pairs={{0,8},{2,10},{4,12},{6,14},{8,16},{10,18},{12,20},{14,22},{1,9},{3... | collective-permute-start | bytes 663560 | tf_op jit(solution)/shard_map/ppermute | solution.py:482
  334.1 5.0 %collective-permute-start.42 = (bf16[2,24,2304]{2,1,0:T(8,128)(2,1)S(1)}, bf16[2,24,2304]{2,1,0:T(8,128)(2,1)S(1)}, u32[]{:S(2)}, u32[]{:S(2)}) collective-permute-start(bf16[2,24,2304]{2,1,0:T(8,128)(2,1)S(1)} %get-tuple-element.238), channel_id=1, source_target_pairs={{0,8},{2,10},{4,12},{6,14},{8,16},{10,18},{12,20},{14,22},{16,24},... | collective-permute-start | bytes 663560 | tf_op jit(solution)/shard_map/ppermute | solution.py:482
  342.5 5.8 %collective-permute-done.45 = bf16[2,24,2304]{2,1,0:T(8,128)(2,1)S(1)} collective-permute-done((bf16[2,24,2304]{2,1,0:T(8,128)(2,1)S(1)}, bf16[2,24,2304]{2,1,0:T(8,128)(2,1)S(1)}, u32[]{:S(2)}, u32[]{:S(2)}) %collective-permute-start.45) | collective-permute-done | bytes 221216 | tf_op jit(solution)/shard_map/ppermute | solution.py:483
  (495 shorter events, 181.9 us)
Async XLA Ops:
  8.4 15.9 %collective-permute-start.7 = (bf16[24,1920]{1,0:T(8,128)(2,1)S(1)}, bf16[24,1920]{1,0:T(8,128)(2,1)S(1)}, u32[]{:S(2)}, u32[]{:S(2)}) collective-permute-start(bf16[24,1920]{1,0:T(8,128)(2,1)S(1)} %broadcast_select_fusion.17), channel_id=1, source_target_pairs={{0,1},{1,0},{2,3},{3,2},{4,5},{5,4},{6,7},{7,6},{8,9},{9,8},{10,11... | collective-permute-start | bytes 276488 | tf_op jit(solution)/shard_map/ppermute | solution.py:352
  8.5 35.0 %collective-permute-start.12 = (bf16[512,768]{1,0:T(8,128)(2,1)S(1)}, bf16[512,768]{1,0:T(8,128)(2,1)S(1)}, u32[]{:S(2)}, u32[]{:S(2)}) collective-permute-start(bf16[512,768]{1,0:T(8,128)(2,1)S(1)} %copy-done.28), channel_id=1, source_target_pairs={{0,1},{1,0},{2,3},{3,2},{4,5},{5,4},{6,7},{7,6},{8,9},{9,8},{10,11... | collective-permute-start | bytes 2359304 | tf_op jit(solution)/shard_map/ppermute | solution.py:352
  51.9 17.9 %collective-permute-start.14 = (bf16[2,4,24,2304]{3,2,1,0:T(8,128)(2,1)S(1)}, bf16[2,4,24,2304]{3,2,1,0:T(8,128)(2,1)S(1)}, u32[]{:S(2)}, u32[]{:S(2)}) collective-permute-start(bf16[2,4,24,2304]{3,2,1,0:T(8,128)(2,1)S(1)} %pad_maximum_fusion.24), channel_id=1, source_target_pairs={{0,2},{2,0},{4,6},{6,4},{8,10},{10,8},{12,14},{14,12},{16,18},{18,... | collective-permute-start | bytes 2654216 | tf_op jit(solution)/shard_map/ppermute | solution.py:372
  52.7 18.2 %collective-permute-start.13 = (bf16[2,4,24,2304]{3,2,1,0:T(8,128)(2,1)S(1)}, bf16[2,4,24,2304]{3,2,1,0:T(8,128)(2,1)S(1)}, u32[]{:S(2)}, u32[]{:S(2)}) collective-permute-start(bf16[2,4,24,2304]{3,2,1,0:T(8,128)(2,1)S(1)} %pad_maximum_fusion.23), channel_id=1, source_target_pairs={{0,4},{2,6},{4,0},{6,2},{8,12},{10,14},{12,8},{14,10},{16,20},{18,... | collective-permute-start | bytes 2654216 | tf_op jit(solution)/shard_map/ppermute | solution.py:372
  56.2 31.7 %collective-permute-start.11 = (bf16[2,2,24,3456]{3,2,1,0:T(8,128)(2,1)}, bf16[2,2,24,3456]{3,2,1,0:T(8,128)(2,1)}, u32[]{:S(2)}, u32[]{:S(2)}) collective-permute-start(bf16[2,2,24,3456]{3,2,1,0:T(8,128)(2,1)} %pad_maximum_fusion.27), channel_id=1, source_target_pairs={{0,16},{2,18},{4,20},{6,22},{8,24},{10,26},{12,28},{14,30},{16,0},... | collective-permute-start | bytes 1990664 | tf_op jit(solution)/shard_map/ppermute | solution.py:372
  89.5 15.7 %collective-permute-start.16 = (bf16[4,24,3456]{2,1,0:T(8,128)(2,1)S(1)}, bf16[4,24,3456]{2,1,0:T(8,128)(2,1)S(1)}, u32[]{:S(2)}, u32[]{:S(2)}) collective-permute-start(bf16[4,24,3456]{2,1,0:T(8,128)(2,1)S(1)} %bitcast.380), channel_id=1, source_target_pairs={{0,2},{2,0},{4,6},{6,4},{8,10},{10,8},{12,14},{14,12},{16,18},{18,... | collective-permute-start | bytes 1990664 | tf_op jit(solution)/shard_map/ppermute | solution.py:372
  90.5 15.4 %collective-permute-start.17 = (bf16[4,24,3456]{2,1,0:T(8,128)(2,1)S(1)}, bf16[4,24,3456]{2,1,0:T(8,128)(2,1)S(1)}, u32[]{:S(2)}, u32[]{:S(2)}) collective-permute-start(bf16[4,24,3456]{2,1,0:T(8,128)(2,1)S(1)} %bitcast.378), channel_id=1, source_target_pairs={{0,4},{2,6},{4,0},{6,2},{8,12},{10,14},{12,8},{14,10},{16,20},{18,... | collective-permute-start | bytes 1990664 | tf_op jit(solution)/shard_map/ppermute | solution.py:372
  107.2 29.0 %collective-permute-start.18 = (bf16[2,4,24,3456]{3,2,0,1:T(8,128)(2,1)}, bf16[2,4,24,3456]{3,2,0,1:T(8,128)(2,1)}, u32[]{:S(2)}, u32[]{:S(2)}) collective-permute-start(bf16[2,4,24,3456]{3,2,0,1:T(8,128)(2,1)} %pad_maximum_fusion.9), channel_id=1, source_target_pairs={{0,4},{2,6},{4,0},{6,2},{8,12},{10,14},{12,8},{14,10},{16,20},{18,... | collective-permute-start | bytes 3981320 | tf_op jit(solution)/shard_map/ppermute | solution.py:372
  110.0 28.8 %collective-permute-start.19 = (bf16[2,4,24,3456]{3,2,0,1:T(8,128)(2,1)}, bf16[2,4,24,3456]{3,2,0,1:T(8,128)(2,1)}, u32[]{:S(2)}, u32[]{:S(2)}) collective-permute-start(bf16[2,4,24,3456]{3,2,0,1:T(8,128)(2,1)} %pad_maximum_fusion.10), channel_id=1, source_target_pairs={{0,2},{2,0},{4,6},{6,4},{8,10},{10,8},{12,14},{14,12},{16,18},{18,... | collective-permute-start | bytes 3981320 | tf_op jit(solution)/shard_map/ppermute | solution.py:372
  195.3 31.2 %collective-permute-start.28 = (bf16[4,2,24,3456]{3,2,0,1:T(8,128)(2,1)S(1)}, bf16[4,2,24,3456]{3,2,0,1:T(8,128)(2,1)S(1)}, u32[]{:S(2)}, u32[]{:S(2)}) collective-permute-start(bf16[4,2,24,3456]{3,2,0,1:T(8,128)(2,1)S(1)} %fusion.44), channel_id=1, source_target_pairs={{0,2},{2,0},{4,6},{6,4},{8,10},{10,8},{12,14},{14,12},{16,18},{18,... | collective-permute-start | bytes 3981320 | tf_op jit(solution)/shard_map/ppermute | solution.py:372
  196.6 31.0 %collective-permute-start.29 = (bf16[4,2,24,3456]{3,2,0,1:T(8,128)(2,1)S(1)}, bf16[4,2,24,3456]{3,2,0,1:T(8,128)(2,1)S(1)}, u32[]{:S(2)}, u32[]{:S(2)}) collective-permute-start(bf16[4,2,24,3456]{3,2,0,1:T(8,128)(2,1)S(1)} %select_bitcast_fusion), channel_id=1, source_target_pairs={{0,4},{2,6},{4,0},{6,2},{8,12},{10,14},{12,8},{14,10},{16,20},{18,... | collective-permute-start | bytes 3981320 | tf_op jit(solution)/shard_map/ppermute | solution.py:372
  228.1 20.1 %collective-permute-start.31 = (bf16[4,24,3456]{2,1,0:T(8,128)(2,1)S(1)}, bf16[4,24,3456]{2,1,0:T(8,128)(2,1)S(1)}, u32[]{:S(2)}, u32[]{:S(2)}) collective-permute-start(bf16[4,24,3456]{2,1,0:T(8,128)(2,1)S(1)} %select_bitcast_fusion.10), channel_id=1, source_target_pairs={{0,2},{2,0},{4,6},{6,4},{8,10},{10,8},{12,14},{14,12},{16,18},{18,... | collective-permute-start | bytes 1990664 | tf_op jit(solution)/shard_map/ppermute | solution.py:372
  229.2 19.3 %collective-permute-start.30 = (bf16[4,24,3456]{2,1,0:T(8,128)(2,1)S(1)}, bf16[4,24,3456]{2,1,0:T(8,128)(2,1)S(1)}, u32[]{:S(2)}, u32[]{:S(2)}) collective-permute-start(bf16[4,24,3456]{2,1,0:T(8,128)(2,1)S(1)} %select_bitcast_fusion.11), channel_id=1, source_target_pairs={{0,4},{2,6},{4,0},{6,2},{8,12},{10,14},{12,8},{14,10},{16,20},{18,... | collective-permute-start | bytes 1990664 | tf_op jit(solution)/shard_map/ppermute | solution.py:372
  249.1 12.7 %collective-permute-start.32 = (bf16[2,24,3456]{2,1,0:T(8,128)(2,1)S(1)}, bf16[2,24,3456]{2,1,0:T(8,128)(2,1)S(1)}, u32[]{:S(2)}, u32[]{:S(2)}) collective-permute-start(bf16[2,24,3456]{2,1,0:T(8,128)(2,1)S(1)} %get-tuple-element.284), channel_id=1, source_target_pairs={{0,8},{2,10},{4,12},{6,14},{1,9},{3,11},{5,13},{7,15}} | collective-permute-start | bytes 995336 | tf_op jit(solution)/shard_map/ppermute | solution.py:482
  251.1 10.6 %collective-permute-start.33 = (bf16[2,24,3456]{2,1,0:T(8,128)(2,1)S(1)}, bf16[2,24,3456]{2,1,0:T(8,128)(2,1)S(1)}, u32[]{:S(2)}, u32[]{:S(2)}) collective-permute-start(bf16[2,24,3456]{2,1,0:T(8,128)(2,1)S(1)} %get-tuple-element.283), channel_id=1, source_target_pairs={{24,16},{26,18},{28,20},{30,22},{25,17},{27,19},{29,21},{31,23}} | collective-permute-start | bytes 995336 | tf_op jit(solution)/shard_map/ppermute | solution.py:483
  282.3 21.7 %collective-permute-start.38 = (bf16[4,2,24,2304]{3,2,0,1:T(8,128)(2,1)S(1)}, bf16[4,2,24,2304]{3,2,0,1:T(8,128)(2,1)S(1)}, u32[]{:S(2)}, u32[]{:S(2)}) collective-permute-start(bf16[4,2,24,2304]{3,2,0,1:T(8,128)(2,1)S(1)} %select_bitcast_fusion.5), channel_id=1, source_target_pairs={{0,4},{2,6},{4,0},{6,2},{8,12},{10,14},{12,8},{14,10},{16,20},{18,... | collective-permute-start | bytes 2654216 | tf_op jit(solution)/shard_map/ppermute | solution.py:372
  284.1 21.4 %collective-permute-start.36 = (bf16[4,2,24,2304]{3,2,0,1:T(8,128)(2,1)S(1)}, bf16[4,2,24,2304]{3,2,0,1:T(8,128)(2,1)S(1)}, u32[]{:S(2)}, u32[]{:S(2)}) collective-permute-start(bf16[4,2,24,2304]{3,2,0,1:T(8,128)(2,1)S(1)} %fusion.84), channel_id=1, source_target_pairs={{0,2},{2,0},{4,6},{6,4},{8,10},{10,8},{12,14},{14,12},{16,18},{18,... | collective-permute-start | bytes 2654216 | tf_op jit(solution)/shard_map/ppermute | solution.py:372
  287.9 19.5 %collective-permute-start.47 = (bf16[2,24,3456]{2,1,0:T(8,128)(2,1)S(1)}, bf16[2,24,3456]{2,1,0:T(8,128)(2,1)S(1)}, u32[]{:S(2)}, u32[]{:S(2)}) collective-permute-start(bf16[2,24,3456]{2,1,0:T(8,128)(2,1)S(1)} %get-tuple-element.281), channel_id=1, source_target_pairs={{0,8},{2,10},{4,12},{6,14},{8,16},{10,18},{12,20},{14,22},{1,9},{3... | collective-permute-start | bytes 995336 | tf_op jit(solution)/shard_map/ppermute | solution.py:482
  289.3 18.2 %collective-permute-start.49 = (bf16[2,24,3456]{2,1,0:T(8,128)(2,1)S(1)}, bf16[2,24,3456]{2,1,0:T(8,128)(2,1)S(1)}, u32[]{:S(2)}, u32[]{:S(2)}) collective-permute-start(bf16[2,24,3456]{2,1,0:T(8,128)(2,1)S(1)} %get-tuple-element.282), channel_id=1, source_target_pairs={{16,8},{18,10},{20,12},{22,14},{24,16},{26,18},{28,20},{30,22},{17... | collective-permute-start | bytes 995336 | tf_op jit(solution)/shard_map/ppermute | solution.py:483
  304.3 11.3 %collective-permute-start.39 = (bf16[4,24,2304]{2,1,0:T(8,128)(2,1)S(1)}, bf16[4,24,2304]{2,1,0:T(8,128)(2,1)S(1)}, u32[]{:S(2)}, u32[]{:S(2)}) collective-permute-start(bf16[4,24,2304]{2,1,0:T(8,128)(2,1)S(1)} %select_bitcast_fusion.18), channel_id=1, source_target_pairs={{0,2},{2,0},{4,6},{6,4},{8,10},{10,8},{12,14},{14,12},{16,18},{18,... | collective-permute-start | bytes 1327112 | tf_op jit(solution)/shard_map/ppermute | solution.py:372
  305.9 11.0 %collective-permute-start.37 = (bf16[4,24,2304]{2,1,0:T(8,128)(2,1)S(1)}, bf16[4,24,2304]{2,1,0:T(8,128)(2,1)S(1)}, u32[]{:S(2)}, u32[]{:S(2)}) collective-permute-start(bf16[4,24,2304]{2,1,0:T(8,128)(2,1)S(1)} %select_bitcast_fusion.19), channel_id=1, source_target_pairs={{0,4},{2,6},{4,0},{6,2},{8,12},{10,14},{12,8},{14,10},{16,20},{18,... | collective-permute-start | bytes 1327112 | tf_op jit(solution)/shard_map/ppermute | solution.py:372
  307.8 11.4 %collective-permute-start.50 = (bf16[2,24,3456]{2,1,0:T(8,128)(2,1)S(1)}, bf16[2,24,3456]{2,1,0:T(8,128)(2,1)S(1)}, u32[]{:S(2)}, u32[]{:S(2)}) collective-permute-start(bf16[2,24,3456]{2,1,0:T(8,128)(2,1)S(1)} %get-tuple-element.280), channel_id=1, source_target_pairs={{8,0},{10,2},{12,4},{14,6},{16,8},{18,10},{20,12},{22,14},{24,16},... | collective-permute-start | bytes 995336 | tf_op jit(solution)/shard_map/ppermute | solution.py:483
  309.1 11.7 %collective-permute-start.48 = (bf16[2,24,3456]{2,1,0:T(8,128)(2,1)S(1)}, bf16[2,24,3456]{2,1,0:T(8,128)(2,1)S(1)}, u32[]{:S(2)}, u32[]{:S(2)}) collective-permute-start(bf16[2,24,3456]{2,1,0:T(8,128)(2,1)S(1)} %get-tuple-element.279), channel_id=1, source_target_pairs={{0,8},{2,10},{4,12},{6,14},{8,16},{10,18},{12,20},{14,22},{16,24},... | collective-permute-start | bytes 995336 | tf_op jit(solution)/shard_map/ppermute | solution.py:482
  317.1 14.8 %collective-permute-start.43 = (bf16[2,24,2304]{2,1,0:T(8,128)(2,1)S(1)}, bf16[2,24,2304]{2,1,0:T(8,128)(2,1)S(1)}, u32[]{:S(2)}, u32[]{:S(2)}) collective-permute-start(bf16[2,24,2304]{2,1,0:T(8,128)(2,1)S(1)} %get-tuple-element.294), channel_id=1, source_target_pairs={{24,16},{26,18},{28,20},{30,22},{25,17},{27,19},{29,21},{31,23}} | collective-permute-start | bytes 663560 | tf_op jit(solution)/shard_map/ppermute | solution.py:483
  (103 other events, 594.5 us)

commit v3 on v2

--- a/solution.py
+++ b/solution.py
@@ -663,7 +663,7 @@
 
     def rejoin(first, second):
         own = jnp.where(core == 0, first, second)
-        got = swap(jnp.where(core == 0, second, first))
+        got = swap(jnp.where(core == 0, second, first).astype(bf)).astype(f32)
         return jnp.where(core == 0, own, got), jnp.where(core == 0, got, own)
 
     late_cols = jnp.concatenate([d_wout, d_wup], axis=1).reshape(chips, 2, rows, half + ff_half)

time: 358 us -> 358 us (level)
  transfers between devices with their start and end apart: 52 -> 52, of which waited for: 27 -> 28; matrix products, arithmetic and copies ran while one was open for 14% -> 14% of each run, Pallas kernels for 25% -> 25%
where the time goes in v3:
time: 358 us; the launch traced here: 354 us
  Pallas kernels  86.8 us (24%)
  waiting for transfers between devices  84.6 us (24%)
  starting transfers between devices  57.6 us (16%)
  matrix products  46.7 us (13%)
  other arithmetic  38.2 us (11%)
  local copies, waits for them, and re-layouts  35.9 us (10%)
  between operations  3.81 us (1%)
    pallas_call x6, Pallas kernels, attention_backward(): pl.pallas_call(functools.partial(backward_body, head), grid=(1,), in_spec...  55.4 us
    ppermute x18, waiting for transfers between devices, exchange(): return lax.ppermute(value, 'dp', [(i, i ^ mask) for i in range(16)])  44.7 us
    pallas_call x6, Pallas kernels, attention_forward(): pl.pallas_call(functools.partial(forward_body, head), grid=(1,), in_specs...  31.4 us
    ppermute x18, starting transfers between devices, exchange(): return lax.ppermute(value, 'dp', [(i, i ^ mask) for i in range(16)])  19.2 us
    unnamed x170, local copies, waits for them, and re-layouts  19 us
    ppermute x6, starting transfers between devices, line(): up = lax.ppermute(to_above.astype(value.dtype), 'dp', ups)  18.7 us
    dot_general x8, matrix products, product(): return jnp.dot(left, right, preferred_element_type=jnp.float32)  17.3 us
    ppermute x3, waiting for transfers between devices, line(): lax.ppermute(above[-1], 'dp', down)  16.4 us
  transfers between devices with their start and end apart: 52, of which 28 were waited for; matrix products, arithmetic and copies ran while one was open for 14% of the time, Pallas kernels for 25%

profile of v3, /device:TPU:0, one launch (start us, length us, event | category | flops | bytes accessed | tf_op | source)
XLA Modules:
  0.0 353.6 jit_solution(7752639173109645749)
XLA Ops:
  9.1 4.6 %collective-permute-start.1 = (bf16[2,24,2304]{2,1,0:T(8,128)(2,1)S(1)}, bf16[2,24,2304]{2,1,0:T(8,128)(2,1)S(1)}, u32[]{:S(2)}, u32[]{:S(2)}) collective-permute-start(bf16[2,24,2304]{2,1,0:T(8,128)(2,1)S(1)} %pad_maximum_fusion.44), channel_id=1, source_target_pairs={{0,8},{2,10},{4,12},{6,14},{8,16},{10,18},{12,20},{14,22},{16,24},... | collective-permute-start | bytes 663560 | tf_op jit(solution)/shard_map/ppermute | solution.py:392
  25.1 6.6 %collective-permute-done.5 = bf16[2,24,2304]{2,1,0:T(8,128)(2,1)S(1)} collective-permute-done((bf16[2,24,2304]{2,1,0:T(8,128)(2,1)S(1)}, bf16[2,24,2304]{2,1,0:T(8,128)(2,1)S(1)}, u32[]{:S(2)}, u32[]{:S(2)}) %collective-permute-start.5) | collective-permute-done | bytes 221216 | tf_op jit(solution)/shard_map/ppermute | solution.py:392
  33.2 6.3 %collective-permute-done.6 = bf16[2,24,2304]{2,1,0:T(8,128)(2,1)S(1)} collective-permute-done((bf16[2,24,2304]{2,1,0:T(8,128)(2,1)S(1)}, bf16[2,24,2304]{2,1,0:T(8,128)(2,1)S(1)}, u32[]{:S(2)}, u32[]{:S(2)}) %collective-permute-start.6) | collective-permute-done | bytes 221216 | tf_op jit(solution)/shard_map/ppermute | solution.py:392
  44.8 5.4 %collective-permute-done.10 = bf16[2,24,3456]{2,1,0:T(8,128)(2,1)} collective-permute-done((bf16[2,24,3456]{2,1,0:T(8,128)(2,1)S(1)}, bf16[2,24,3456]{2,1,0:T(8,128)(2,1)}, u32[]{:S(2)}, u32[]{:S(2)}) %collective-permute-start.10) | collective-permute-done | bytes 331808 | tf_op jit(solution)/shard_map/ppermute | solution.py:372
  56.2 13.6 %collective-permute-done.14 = bf16[2,4,24,2304]{3,2,1,0:T(8,128)(2,1)S(1)} collective-permute-done((bf16[2,4,24,2304]{3,2,1,0:T(8,128)(2,1)S(1)}, bf16[2,4,24,2304]{3,2,1,0:T(8,128)(2,1)S(1)}, u32[]{:S(2)}, u32[]{:S(2)}) %collective-permute-start.14) | collective-permute-done | bytes 884768 | tf_op jit(solution)/shard_map/ppermute | solution.py:372
  92.6 5.1 %attention_forward.6 = (bf16[1024,128]{1,0:T(8,128)(2,1)S(1)}, bf16[1024,1024]{1,0:T(8,128)(2,1)S(1)}) custom-call(s32[1]{0:T(128)S(6)} %copy.205.prefix_ref, bf16[1024,1152]{1,0:T(8,128)(2,1)S(1)} %add_convert_fusion.q_ref.k_ref.v_ref, bf16[1024,1152]{1,0:T(8,128)(2,1)S(1)} %add_convert_fusion.q_ref.k_ref.v_ref, ...), custom_call_target="tpu_custom_call" | custom-call | flops 300000000 | bytes 3145728 | tf_op jit(solution)/shard_map/attention_forward/pallas_call | solution.py:189
  99.1 5.3 %attention_forward.7 = (bf16[1024,128]{1,0:T(8,128)(2,1)S(1)}, bf16[1024,1024]{1,0:T(8,128)(2,1)S(1)}) custom-call(s32[1]{0:T(128)S(6)} %copy.205.prefix_ref, bf16[1024,1152]{1,0:T(8,128)(2,1)S(1)} %add_convert_fusion.q_ref.k_ref.v_ref, bf16[1024,1152]{1,0:T(8,128)(2,1)S(1)} %add_convert_fusion.q_ref.k_ref.v_ref, ...), custom_call_target="tpu_custom_call" | custom-call | flops 300000000 | bytes 3145728 | tf_op jit(solution)/shard_map/attention_forward/pallas_call | solution.py:189
  112.0 5.1 %attention_forward.8 = (bf16[1024,128]{1,0:T(8,128)(2,1)S(1)}, bf16[1024,1024]{1,0:T(8,128)(2,1)S(1)}) custom-call(s32[1]{0:T(128)S(6)} %copy.205.prefix_ref, bf16[1024,1152]{1,0:T(8,128)(2,1)S(1)} %add_convert_fusion.q_ref.k_ref.v_ref, bf16[1024,1152]{1,0:T(8,128)(2,1)S(1)} %add_convert_fusion.q_ref.k_ref.v_ref, ...), custom_call_target="tpu_custom_call" | custom-call | flops 300000000 | bytes 3145728 | tf_op jit(solution)/shard_map/attention_forward/pallas_call | solution.py:189
  117.2 5.1 %attention_forward.10 = (bf16[1024,128]{1,0:T(8,128)(2,1)S(1)}, bf16[1024,1024]{1,0:T(8,128)(2,1)S(1)}) custom-call(s32[1]{0:T(128)S(6)} %copy.205.prefix_ref, bf16[1024,1152]{1,0:T(8,128)(2,1)S(1)} %add_convert_fusion.q_ref.k_ref.v_ref, bf16[1024,1152]{1,0:T(8,128)(2,1)S(1)} %add_convert_fusion.q_ref.k_ref.v_ref, ...), custom_call_target="tpu_custom_call" | custom-call | flops 300000000 | bytes 3145728 | tf_op jit(solution)/shard_map/attention_forward/pallas_call | solution.py:189
  122.3 5.6 %attention_forward.9 = (bf16[1024,128]{1,0:T(8,128)(2,1)S(1)}, bf16[1024,1024]{1,0:T(8,128)(2,1)S(1)}) custom-call(s32[1]{0:T(128)S(6)} %copy.205.prefix_ref, bf16[1024,1152]{1,0:T(8,128)(2,1)S(1)} %add_convert_fusion.q_ref.k_ref.v_ref, bf16[1024,1152]{1,0:T(8,128)(2,1)S(1)} %add_convert_fusion.q_ref.k_ref.v_ref, ...), custom_call_target="tpu_custom_call" | custom-call | flops 300000000 | bytes 3145728 | tf_op jit(solution)/shard_map/attention_forward/pallas_call | solution.py:189
  127.9 5.1 %attention_forward.11 = (bf16[1024,128]{1,0:T(8,128)(2,1)S(1)}, bf16[1024,1024]{1,0:T(8,128)(2,1)S(1)}) custom-call(s32[1]{0:T(128)S(6)} %copy.205.prefix_ref, bf16[1024,1152]{1,0:T(8,128)(2,1)S(1)} %add_convert_fusion.q_ref.k_ref.v_ref, bf16[1024,1152]{1,0:T(8,128)(2,1)S(1)} %add_convert_fusion.q_ref.k_ref.v_ref, ...), custom_call_target="tpu_custom_call" | custom-call | flops 300000000 | bytes 3145728 | tf_op jit(solution)/shard_map/attention_forward/pallas_call | solution.py:189
  152.1 6.5 %fusion.4 = (bf16[1024,1536]{1,0:T(8,128)(2,1)}, bf16[1024,1536]{1,0:T(8,128)(2,1)S(1)}) fusion(f32[1536]{0:T(1024)S(1)} %fusion.54, bf16[768,1536]{1,0:T(8,128)(2,1)S(1)} %bitcast.382, bf16[512,768]{1,0:T(8,128)(2,1)S(1)} %get-tuple-element.276, bf16[512,768]{1,0:T(8,128)(2,1)S(1)} %get-tuple-element.275), kind=kOutput, calls=%fused_computation.5 | convolution fusion | flops 2437939200 | bytes 10229760 | tf_op jit(solution)/shard_map/dot_general | solution.py:36
  170.0 4.4 %fusion.260 = (bf16[1536]{0:T(1024)(128)(2,1)S(1)}, bf16[1024,1536]{1,0:T(8,128)(2,1)S(1)}) fusion(bf16[1024,1536]{1,0:T(8,128)(2,1)} %get-tuple-element.151, bf16[1536,768]{1,0:T(8,128)(2,1)S(1)} %bitcast.387, bf16[512,768]{1,0:T(8,128)(2,1)S(1)} %get-tuple-element.274, bf16[512,768]{1,0:T(8,128)(2,1)S(1)} %get-tuple-element.273), kind=kOutput, calls=%fused_computation.550 | convolution fusion | flops 2425354752 | bytes 10226688 | tf_op jit(solution)/shard_map/dot_general | solution.py:46
  197.2 9.1 %attention_backward.9 = (bf16[1024,128]{1,0:T(8,128)(2,1)S(1)}, bf16[1024,128]{1,0:T(8,128)(2,1)S(1)}, bf16[1024,128]{1,0:T(8,128)(2,1)S(1)}, f32[64,768]{1,0:T(8,128)S(1)}, f32[64,768]{1,0:T(8,128)S(1)}) custom-call(bf16[1024,1152]{1,0:T(8,128)(2,1)S(1)} %add_convert_fusion.q_ref.k_ref.v_ref, bf16[1024,1152]{1,0:T(8,128)(2,1)S(1)} %add_convert_fusion.q_ref.k_ref.v_ref, ...), custom_call_target="tpu_custom_call" | custom-call | flops 1000000000 | bytes 4194304 | tf_op jit(solution)/shard_map/attention_backward/pallas_call | solution.py:331
  206.3 9.3 %attention_backward.10 = (bf16[1024,128]{1,0:T(8,128)(2,1)S(1)}, bf16[1024,128]{1,0:T(8,128)(2,1)S(1)}, bf16[1024,128]{1,0:T(8,128)(2,1)S(1)}, f32[64,768]{1,0:T(8,128)S(1)}, f32[64,768]{1,0:T(8,128)S(1)}) custom-call(bf16[1024,1152]{1,0:T(8,128)(2,1)S(1)} %add_convert_fusion.q_ref.k_ref.v_ref, bf16[1024,1152]{1,0:T(8,128)(2,1)S(1)} %add_convert_fusion.q_ref.k_ref.v_ref, ...), custom_call_target="tpu_custom_call" | custom-call | flops 1000000000 | bytes 4194304 | tf_op jit(solution)/shard_map/attention_backward/pallas_call | solution.py:331
  216.4 9.5 %attention_backward.6 = (bf16[1024,128]{1,0:T(8,128)(2,1)S(1)}, bf16[1024,128]{1,0:T(8,128)(2,1)S(1)}, bf16[1024,128]{1,0:T(8,128)(2,1)S(1)}, f32[64,768]{1,0:T(8,128)S(1)}, f32[64,768]{1,0:T(8,128)S(1)}) custom-call(bf16[1024,1152]{1,0:T(8,128)(2,1)S(1)} %add_convert_fusion.q_ref.k_ref.v_ref, bf16[1024,1152]{1,0:T(8,128)(2,1)S(1)} %add_convert_fusion.q_ref.k_ref.v_ref, ...), custom_call_target="tpu_custom_call" | custom-call | flops 1000000000 | bytes 4194304 | tf_op jit(solution)/shard_map/attention_backward/pallas_call | solution.py:331
  229.7 9.1 %attention_backward.7 = (bf16[1024,128]{1,0:T(8,128)(2,1)S(1)}, bf16[1024,128]{1,0:T(8,128)(2,1)S(1)}, bf16[1024,128]{1,0:T(8,128)(2,1)S(1)}, f32[64,768]{1,0:T(8,128)S(1)}, f32[64,768]{1,0:T(8,128)S(1)}) custom-call(bf16[1024,1152]{1,0:T(8,128)(2,1)S(1)} %add_convert_fusion.q_ref.k_ref.v_ref, bf16[1024,1152]{1,0:T(8,128)(2,1)S(1)} %add_convert_fusion.q_ref.k_ref.v_ref, ...), custom_call_target="tpu_custom_call" | custom-call | flops 1000000000 | bytes 4194304 | tf_op jit(solution)/shard_map/attention_backward/pallas_call | solution.py:331
  238.8 9.3 %attention_backward.11 = (bf16[1024,128]{1,0:T(8,128)(2,1)S(1)}, bf16[1024,128]{1,0:T(8,128)(2,1)S(1)}, bf16[1024,128]{1,0:T(8,128)(2,1)S(1)}, f32[64,768]{1,0:T(8,128)S(1)}, f32[64,768]{1,0:T(8,128)S(1)}) custom-call(bf16[1024,1152]{1,0:T(8,128)(2,1)S(1)} %add_convert_fusion.q_ref.k_ref.v_ref, bf16[1024,1152]{1,0:T(8,128)(2,1)S(1)} %add_convert_fusion.q_ref.k_ref.v_ref, ...), custom_call_target="tpu_custom_call" | custom-call | flops 1000000000 | bytes 4194304 | tf_op jit(solution)/shard_map/attention_backward/pallas_call | solution.py:331
  252.6 9.1 %attention_backward.8 = (bf16[1024,128]{1,0:T(8,128)(2,1)S(1)}, bf16[1024,128]{1,0:T(8,128)(2,1)S(1)}, bf16[1024,128]{1,0:T(8,128)(2,1)S(1)}, f32[64,768]{1,0:T(8,128)S(1)}, f32[64,768]{1,0:T(8,128)S(1)}) custom-call(bf16[1024,1152]{1,0:T(8,128)(2,1)S(1)} %add_convert_fusion.q_ref.k_ref.v_ref, bf16[1024,1152]{1,0:T(8,128)(2,1)S(1)} %add_convert_fusion.q_ref.k_ref.v_ref, ...), custom_call_target="tpu_custom_call" | custom-call | flops 1000000000 | bytes 4194304 | tf_op jit(solution)/shard_map/attention_backward/pallas_call | solution.py:331
  290.0 14.0 %collective-permute-done.38 = bf16[4,2,24,2304]{3,2,0,1:T(8,128)(2,1)S(1)} collective-permute-done((bf16[4,2,24,2304]{3,2,0,1:T(8,128)(2,1)S(1)}, bf16[4,2,24,2304]{3,2,0,1:T(8,128)(2,1)S(1)}, u32[]{:S(2)}, u32[]{:S(2)}) %collective-permute-start.38) | collective-permute-done | bytes 884768 | tf_op jit(solution)/shard_map/ppermute | solution.py:372
  309.1 4.6 %collective-permute-start.48 = (bf16[2,24,3456]{2,1,0:T(8,128)(2,1)S(1)}, bf16[2,24,3456]{2,1,0:T(8,128)(2,1)S(1)}, u32[]{:S(2)}, u32[]{:S(2)}) collective-permute-start(bf16[2,24,3456]{2,1,0:T(8,128)(2,1)S(1)} %get-tuple-element.279), channel_id=1, source_target_pairs={{0,8},{2,10},{4,12},{6,14},{8,16},{10,18},{12,20},{14,22},{16,24},... | collective-permute-start | bytes 995336 | tf_op jit(solution)/shard_map/ppermute | solution.py:482
  324.0 4.4 %collective-permute-start.41 = (bf16[2,24,2304]{2,1,0:T(8,128)(2,1)S(1)}, bf16[2,24,2304]{2,1,0:T(8,128)(2,1)S(1)}, u32[]{:S(2)}, u32[]{:S(2)}) collective-permute-start(bf16[2,24,2304]{2,1,0:T(8,128)(2,1)S(1)} %get-tuple-element.240), channel_id=1, source_target_pairs={{0,8},{2,10},{4,12},{6,14},{8,16},{10,18},{12,20},{14,22},{1,9},{3... | collective-permute-start | bytes 663560 | tf_op jit(solution)/shard_map/ppermute | solution.py:482
  333.0 5.0 %collective-permute-start.42 = (bf16[2,24,2304]{2,1,0:T(8,128)(2,1)S(1)}, bf16[2,24,2304]{2,1,0:T(8,128)(2,1)S(1)}, u32[]{:S(2)}, u32[]{:S(2)}) collective-permute-start(bf16[2,24,2304]{2,1,0:T(8,128)(2,1)S(1)} %get-tuple-element.238), channel_id=1, source_target_pairs={{0,8},{2,10},{4,12},{6,14},{8,16},{10,18},{12,20},{14,22},{16,24},... | collective-permute-start | bytes 663560 | tf_op jit(solution)/shard_map/ppermute | solution.py:482
  341.5 7.1 %collective-permute-done.45 = bf16[2,24,2304]{2,1,0:T(8,128)(2,1)S(1)} collective-permute-done((bf16[2,24,2304]{2,1,0:T(8,128)(2,1)S(1)}, bf16[2,24,2304]{2,1,0:T(8,128)(2,1)S(1)}, u32[]{:S(2)}, u32[]{:S(2)}) %collective-permute-start.45) | collective-permute-done | bytes 221216 | tf_op jit(solution)/shard_map/ppermute | solution.py:483
  (495 shorter events, 180.7 us)
Async XLA Ops:
  8.4 15.9 %collective-permute-start.7 = (bf16[24,1920]{1,0:T(8,128)(2,1)S(1)}, bf16[24,1920]{1,0:T(8,128)(2,1)S(1)}, u32[]{:S(2)}, u32[]{:S(2)}) collective-permute-start(bf16[24,1920]{1,0:T(8,128)(2,1)S(1)} %broadcast_select_fusion.17), channel_id=1, source_target_pairs={{0,1},{1,0},{2,3},{3,2},{4,5},{5,4},{6,7},{7,6},{8,9},{9,8},{10,11... | collective-permute-start | bytes 276488 | tf_op jit(solution)/shard_map/ppermute | solution.py:352
  8.5 35.0 %collective-permute-start.12 = (bf16[512,768]{1,0:T(8,128)(2,1)S(1)}, bf16[512,768]{1,0:T(8,128)(2,1)S(1)}, u32[]{:S(2)}, u32[]{:S(2)}) collective-permute-start(bf16[512,768]{1,0:T(8,128)(2,1)S(1)} %copy-done.28), channel_id=1, source_target_pairs={{0,1},{1,0},{2,3},{3,2},{4,5},{5,4},{6,7},{7,6},{8,9},{9,8},{10,11... | collective-permute-start | bytes 2359304 | tf_op jit(solution)/shard_map/ppermute | solution.py:352
  51.9 17.9 %collective-permute-start.14 = (bf16[2,4,24,2304]{3,2,1,0:T(8,128)(2,1)S(1)}, bf16[2,4,24,2304]{3,2,1,0:T(8,128)(2,1)S(1)}, u32[]{:S(2)}, u32[]{:S(2)}) collective-permute-start(bf16[2,4,24,2304]{3,2,1,0:T(8,128)(2,1)S(1)} %pad_maximum_fusion.24), channel_id=1, source_target_pairs={{0,2},{2,0},{4,6},{6,4},{8,10},{10,8},{12,14},{14,12},{16,18},{18,... | collective-permute-start | bytes 2654216 | tf_op jit(solution)/shard_map/ppermute | solution.py:372
  52.7 18.2 %collective-permute-start.13 = (bf16[2,4,24,2304]{3,2,1,0:T(8,128)(2,1)S(1)}, bf16[2,4,24,2304]{3,2,1,0:T(8,128)(2,1)S(1)}, u32[]{:S(2)}, u32[]{:S(2)}) collective-permute-start(bf16[2,4,24,2304]{3,2,1,0:T(8,128)(2,1)S(1)} %pad_maximum_fusion.23), channel_id=1, source_target_pairs={{0,4},{2,6},{4,0},{6,2},{8,12},{10,14},{12,8},{14,10},{16,20},{18,... | collective-permute-start | bytes 2654216 | tf_op jit(solution)/shard_map/ppermute | solution.py:372
  56.2 31.7 %collective-permute-start.11 = (bf16[2,2,24,3456]{3,2,1,0:T(8,128)(2,1)}, bf16[2,2,24,3456]{3,2,1,0:T(8,128)(2,1)}, u32[]{:S(2)}, u32[]{:S(2)}) collective-permute-start(bf16[2,2,24,3456]{3,2,1,0:T(8,128)(2,1)} %pad_maximum_fusion.27), channel_id=1, source_target_pairs={{0,16},{2,18},{4,20},{6,22},{8,24},{10,26},{12,28},{14,30},{16,0},... | collective-permute-start | bytes 1990664 | tf_op jit(solution)/shard_map/ppermute | solution.py:372
  89.5 15.7 %collective-permute-start.16 = (bf16[4,24,3456]{2,1,0:T(8,128)(2,1)S(1)}, bf16[4,24,3456]{2,1,0:T(8,128)(2,1)S(1)}, u32[]{:S(2)}, u32[]{:S(2)}) collective-permute-start(bf16[4,24,3456]{2,1,0:T(8,128)(2,1)S(1)} %bitcast.380), channel_id=1, source_target_pairs={{0,2},{2,0},{4,6},{6,4},{8,10},{10,8},{12,14},{14,12},{16,18},{18,... | collective-permute-start | bytes 1990664 | tf_op jit(solution)/shard_map/ppermute | solution.py:372
  90.5 15.4 %collective-permute-start.17 = (bf16[4,24,3456]{2,1,0:T(8,128)(2,1)S(1)}, bf16[4,24,3456]{2,1,0:T(8,128)(2,1)S(1)}, u32[]{:S(2)}, u32[]{:S(2)}) collective-permute-start(bf16[4,24,3456]{2,1,0:T(8,128)(2,1)S(1)} %bitcast.378), channel_id=1, source_target_pairs={{0,4},{2,6},{4,0},{6,2},{8,12},{10,14},{12,8},{14,10},{16,20},{18,... | collective-permute-start | bytes 1990664 | tf_op jit(solution)/shard_map/ppermute | solution.py:372
  107.2 29.0 %collective-permute-start.18 = (bf16[2,4,24,3456]{3,2,0,1:T(8,128)(2,1)}, bf16[2,4,24,3456]{3,2,0,1:T(8,128)(2,1)}, u32[]{:S(2)}, u32[]{:S(2)}) collective-permute-start(bf16[2,4,24,3456]{3,2,0,1:T(8,128)(2,1)} %pad_maximum_fusion.9), channel_id=1, source_target_pairs={{0,4},{2,6},{4,0},{6,2},{8,12},{10,14},{12,8},{14,10},{16,20},{18,... | collective-permute-start | bytes 3981320 | tf_op jit(solution)/shard_map/ppermute | solution.py:372
  110.0 28.8 %collective-permute-start.19 = (bf16[2,4,24,3456]{3,2,0,1:T(8,128)(2,1)}, bf16[2,4,24,3456]{3,2,0,1:T(8,128)(2,1)}, u32[]{:S(2)}, u32[]{:S(2)}) collective-permute-start(bf16[2,4,24,3456]{3,2,0,1:T(8,128)(2,1)} %pad_maximum_fusion.10), channel_id=1, source_target_pairs={{0,2},{2,0},{4,6},{6,4},{8,10},{10,8},{12,14},{14,12},{16,18},{18,... | collective-permute-start | bytes 3981320 | tf_op jit(solution)/shard_map/ppermute | solution.py:372
  195.3 31.2 %collective-permute-start.28 = (bf16[4,2,24,3456]{3,2,0,1:T(8,128)(2,1)S(1)}, bf16[4,2,24,3456]{3,2,0,1:T(8,128)(2,1)S(1)}, u32[]{:S(2)}, u32[]{:S(2)}) collective-permute-start(bf16[4,2,24,3456]{3,2,0,1:T(8,128)(2,1)S(1)} %fusion.44), channel_id=1, source_target_pairs={{0,2},{2,0},{4,6},{6,4},{8,10},{10,8},{12,14},{14,12},{16,18},{18,... | collective-permute-start | bytes 3981320 | tf_op jit(solution)/shard_map/ppermute | solution.py:372
  196.6 31.0 %collective-permute-start.29 = (bf16[4,2,24,3456]{3,2,0,1:T(8,128)(2,1)S(1)}, bf16[4,2,24,3456]{3,2,0,1:T(8,128)(2,1)S(1)}, u32[]{:S(2)}, u32[]{:S(2)}) collective-permute-start(bf16[4,2,24,3456]{3,2,0,1:T(8,128)(2,1)S(1)} %select_bitcast_fusion), channel_id=1, source_target_pairs={{0,4},{2,6},{4,0},{6,2},{8,12},{10,14},{12,8},{14,10},{16,20},{18,... | collective-permute-start | bytes 3981320 | tf_op jit(solution)/shard_map/ppermute | solution.py:372
  228.1 20.1 %collective-permute-start.31 = (bf16[4,24,3456]{2,1,0:T(8,128)(2,1)S(1)}, bf16[4,24,3456]{2,1,0:T(8,128)(2,1)S(1)}, u32[]{:S(2)}, u32[]{:S(2)}) collective-permute-start(bf16[4,24,3456]{2,1,0:T(8,128)(2,1)S(1)} %select_bitcast_fusion.10), channel_id=1, source_target_pairs={{0,2},{2,0},{4,6},{6,4},{8,10},{10,8},{12,14},{14,12},{16,18},{18,... | collective-permute-start | bytes 1990664 | tf_op jit(solution)/shard_map/ppermute | solution.py:372
  229.2 19.3 %collective-permute-start.30 = (bf16[4,24,3456]{2,1,0:T(8,128)(2,1)S(1)}, bf16[4,24,3456]{2,1,0:T(8,128)(2,1)S(1)}, u32[]{:S(2)}, u32[]{:S(2)}) collective-permute-start(bf16[4,24,3456]{2,1,0:T(8,128)(2,1)S(1)} %select_bitcast_fusion.11), channel_id=1, source_target_pairs={{0,4},{2,6},{4,0},{6,2},{8,12},{10,14},{12,8},{14,10},{16,20},{18,... | collective-permute-start | bytes 1990664 | tf_op jit(solution)/shard_map/ppermute | solution.py:372
  249.1 12.7 %collective-permute-start.32 = (bf16[2,24,3456]{2,1,0:T(8,128)(2,1)S(1)}, bf16[2,24,3456]{2,1,0:T(8,128)(2,1)S(1)}, u32[]{:S(2)}, u32[]{:S(2)}) collective-permute-start(bf16[2,24,3456]{2,1,0:T(8,128)(2,1)S(1)} %get-tuple-element.284), channel_id=1, source_target_pairs={{0,8},{2,10},{4,12},{6,14},{1,9},{3,11},{5,13},{7,15}} | collective-permute-start | bytes 995336 | tf_op jit(solution)/shard_map/ppermute | solution.py:482
  251.1 10.6 %collective-permute-start.33 = (bf16[2,24,3456]{2,1,0:T(8,128)(2,1)S(1)}, bf16[2,24,3456]{2,1,0:T(8,128)(2,1)S(1)}, u32[]{:S(2)}, u32[]{:S(2)}) collective-permute-start(bf16[2,24,3456]{2,1,0:T(8,128)(2,1)S(1)} %get-tuple-element.283), channel_id=1, source_target_pairs={{24,16},{26,18},{28,20},{30,22},{25,17},{27,19},{29,21},{31,23}} | collective-permute-start | bytes 995336 | tf_op jit(solution)/shard_map/ppermute | solution.py:483
  282.3 21.7 %collective-permute-start.38 = (bf16[4,2,24,2304]{3,2,0,1:T(8,128)(2,1)S(1)}, bf16[4,2,24,2304]{3,2,0,1:T(8,128)(2,1)S(1)}, u32[]{:S(2)}, u32[]{:S(2)}) collective-permute-start(bf16[4,2,24,2304]{3,2,0,1:T(8,128)(2,1)S(1)} %select_bitcast_fusion.5), channel_id=1, source_target_pairs={{0,4},{2,6},{4,0},{6,2},{8,12},{10,14},{12,8},{14,10},{16,20},{18,... | collective-permute-start | bytes 2654216 | tf_op jit(solution)/shard_map/ppermute | solution.py:372
  284.1 21.4 %collective-permute-start.36 = (bf16[4,2,24,2304]{3,2,0,1:T(8,128)(2,1)S(1)}, bf16[4,2,24,2304]{3,2,0,1:T(8,128)(2,1)S(1)}, u32[]{:S(2)}, u32[]{:S(2)}) collective-permute-start(bf16[4,2,24,2304]{3,2,0,1:T(8,128)(2,1)S(1)} %fusion.84), channel_id=1, source_target_pairs={{0,2},{2,0},{4,6},{6,4},{8,10},{10,8},{12,14},{14,12},{16,18},{18,... | collective-permute-start | bytes 2654216 | tf_op jit(solution)/shard_map/ppermute | solution.py:372
  287.9 19.5 %collective-permute-start.47 = (bf16[2,24,3456]{2,1,0:T(8,128)(2,1)S(1)}, bf16[2,24,3456]{2,1,0:T(8,128)(2,1)S(1)}, u32[]{:S(2)}, u32[]{:S(2)}) collective-permute-start(bf16[2,24,3456]{2,1,0:T(8,128)(2,1)S(1)} %get-tuple-element.281), channel_id=1, source_target_pairs={{0,8},{2,10},{4,12},{6,14},{8,16},{10,18},{12,20},{14,22},{1,9},{3... | collective-permute-start | bytes 995336 | tf_op jit(solution)/shard_map/ppermute | solution.py:482
  289.3 18.2 %collective-permute-start.49 = (bf16[2,24,3456]{2,1,0:T(8,128)(2,1)S(1)}, bf16[2,24,3456]{2,1,0:T(8,128)(2,1)S(1)}, u32[]{:S(2)}, u32[]{:S(2)}) collective-permute-start(bf16[2,24,3456]{2,1,0:T(8,128)(2,1)S(1)} %get-tuple-element.282), channel_id=1, source_target_pairs={{16,8},{18,10},{20,12},{22,14},{24,16},{26,18},{28,20},{30,22},{17... | collective-permute-start | bytes 995336 | tf_op jit(solution)/shard_map/ppermute | solution.py:483
  304.3 11.3 %collective-permute-start.39 = (bf16[4,24,2304]{2,1,0:T(8,128)(2,1)S(1)}, bf16[4,24,2304]{2,1,0:T(8,128)(2,1)S(1)}, u32[]{:S(2)}, u32[]{:S(2)}) collective-permute-start(bf16[4,24,2304]{2,1,0:T(8,128)(2,1)S(1)} %select_bitcast_fusion.18), channel_id=1, source_target_pairs={{0,2},{2,0},{4,6},{6,4},{8,10},{10,8},{12,14},{14,12},{16,18},{18,... | collective-permute-start | bytes 1327112 | tf_op jit(solution)/shard_map/ppermute | solution.py:372
  305.9 11.0 %collective-permute-start.37 = (bf16[4,24,2304]{2,1,0:T(8,128)(2,1)S(1)}, bf16[4,24,2304]{2,1,0:T(8,128)(2,1)S(1)}, u32[]{:S(2)}, u32[]{:S(2)}) collective-permute-start(bf16[4,24,2304]{2,1,0:T(8,128)(2,1)S(1)} %select_bitcast_fusion.19), channel_id=1, source_target_pairs={{0,4},{2,6},{4,0},{6,2},{8,12},{10,14},{12,8},{14,10},{16,20},{18,... | collective-permute-start | bytes 1327112 | tf_op jit(solution)/shard_map/ppermute | solution.py:372
  307.8 11.3 %collective-permute-start.50 = (bf16[2,24,3456]{2,1,0:T(8,128)(2,1)S(1)}, bf16[2,24,3456]{2,1,0:T(8,128)(2,1)S(1)}, u32[]{:S(2)}, u32[]{:S(2)}) collective-permute-start(bf16[2,24,3456]{2,1,0:T(8,128)(2,1)S(1)} %get-tuple-element.280), channel_id=1, source_target_pairs={{8,0},{10,2},{12,4},{14,6},{16,8},{18,10},{20,12},{22,14},{24,16},... | collective-permute-start | bytes 995336 | tf_op jit(solution)/shard_map/ppermute | solution.py:483
  309.1 11.7 %collective-permute-start.48 = (bf16[2,24,3456]{2,1,0:T(8,128)(2,1)S(1)}, bf16[2,24,3456]{2,1,0:T(8,128)(2,1)S(1)}, u32[]{:S(2)}, u32[]{:S(2)}) collective-permute-start(bf16[2,24,3456]{2,1,0:T(8,128)(2,1)S(1)} %get-tuple-element.279), channel_id=1, source_target_pairs={{0,8},{2,10},{4,12},{6,14},{8,16},{10,18},{12,20},{14,22},{16,24},... | collective-permute-start | bytes 995336 | tf_op jit(solution)/shard_map/ppermute | solution.py:482
  317.1 15.1 %collective-permute-start.43 = (bf16[2,24,2304]{2,1,0:T(8,128)(2,1)S(1)}, bf16[2,24,2304]{2,1,0:T(8,128)(2,1)S(1)}, u32[]{:S(2)}, u32[]{:S(2)}) collective-permute-start(bf16[2,24,2304]{2,1,0:T(8,128)(2,1)S(1)} %get-tuple-element.294), channel_id=1, source_target_pairs={{24,16},{26,18},{28,20},{30,22},{25,17},{27,19},{29,21},{31,23}} | collective-permute-start | bytes 663560 | tf_op jit(solution)/shard_map/ppermute | solution.py:483
  (103 other events, 608.5 us)
